TPU v7x, 512 devices: a whole 4x8x8 slice. The times are simulated.
512 devices in a mesh: ctx: 64 (over x, y, core), head: 8 (over z).
Axes of the slice: x: 4, y: 8, z: 8, core: 2. Of those that a mesh axis runs over, the one named last changes fastest.
Arguments:
- hidden_in: bfloat16 [16384, 4096], P('ctx', 'head'), may hold values from -6 to 6
- proj_weights: bfloat16 [3, 4096, 16, 128], P(None, None, 'head', 'ctx'), may hold values from -0.09375 to 0.09375
- directions: bfloat16 [3, 4096, 16, 128], P(None, None, 'head', 'ctx'), may hold values from -6 to 6
Outputs:
- attn_out: bfloat16 [2, 16384, 16, 128], P(None, 'ctx', 'head')
All inputs are finite; a program needn't handle non-finite values.
Results may differ from a plain program's by a relative error of at most 0.011.
Values may be sent and summed in bfloat16 or wider, within the bound.
No kernel may reach another device: no remote copies, remote signals or barrier semaphores. Data moves between devices by JAX's collectives and lax.ppermute only.
A program may use at most 64 MiB of HBM per device.

v0:
```python
import jax
import jax.numpy as jnp
from jax import lax
from jax.sharding import PartitionSpec as P


def prefix(shard, axis, join, neutral):
    place = lax.axis_index(axis)
    gathered = lax.all_gather(shard.astype(jnp.bfloat16), axis)
    state = jnp.zeros_like(shard) + jnp.asarray(neutral, shard.dtype)

    def one(hop, state):
        return join(state, lax.dynamic_index_in_dim(gathered, hop, 0, False).astype(shard.dtype))

    return lax.fori_loop(0, place, one, state)


def add_states(earlier, later):
    return earlier + later


def on_device(hidden_in, proj_weights, directions):
    tokens = lax.all_gather(hidden_in, "head", axis=1, tiled=True)

    def project(block_piece):
        return jnp.einsum("td,mdhc->mthc", tokens, block_piece, preferred_element_type=jnp.float32)

    base_out = project(lax.all_gather(proj_weights, "ctx", axis=3, tiled=True))
    direct_out = project(lax.all_gather(directions, "ctx", axis=3, tiled=True))
    step_size = 0.1 * tokens.shape[1] ** (-0.5)
    sign_pair = jnp.array([1.0, -1.0], jnp.float32) * jnp.float32(step_size)
    signed = (base_out[None] + sign_pair[:, None, None, None, None] * direct_out[None]).astype(
        jnp.bfloat16
    )
    query_rows = signed[:, 0]
    key_rows = signed[:, 1]
    value_rows = signed[:, 2]
    length = query_rows.shape[1]
    scores = jnp.einsum("sthe,suhe->shtu", query_rows, key_rows, preferred_element_type=jnp.float32)
    row_index = lax.broadcasted_iota(jnp.int32, (length, length), 0)
    col_index = lax.broadcasted_iota(jnp.int32, (length, length), 1)
    attn_weights = jnp.where(col_index <= row_index, scores, jnp.float32(0.0)).astype(jnp.bfloat16)
    inner_part = jnp.einsum(
        "shtu,suhe->sthe", attn_weights, value_rows, preferred_element_type=jnp.float32
    )
    block_state = jnp.einsum(
        "sthe,sthf->shef", key_rows, value_rows, preferred_element_type=jnp.float32
    )
    prior_plus = prefix(block_state[0], "ctx", add_states, jnp.zeros_like(block_state[0]))
    prior_minus = prefix(block_state[1], "ctx", add_states, jnp.zeros_like(block_state[1]))
    prior_state = jnp.stack([prior_plus, prior_minus], axis=0)
    carried = prior_state.astype(jnp.bfloat16)
    cross_part = jnp.einsum(
        "sthe,shef->sthf", query_rows, carried, preferred_element_type=jnp.float32
    )
    combined = inner_part + cross_part
    normed = combined * lax.rsqrt(jnp.mean(combined * combined, axis=-1, keepdims=True) + 1e-05)
    return normed.astype(jnp.bfloat16)


def solution(mesh):
    placed = (P("ctx", "head"), P(None, None, "head", "ctx"), P(None, None, "head", "ctx"))
    return jax.shard_map(
        on_device,
        mesh=mesh,
        in_specs=placed,
        out_specs=P(None, "ctx", "head", None),
        check_vma=False,
    )
```

profile of v0, /device:TPU:63, one launch (start us, length us, event | category | flops | bytes accessed | tf_op | source)
XLA Modules:
  0.0 473.0 jit_solution(1537425431540366236)
XLA Ops:
  7.3 1.6 copy.12
  9.0 1.6 copy.10
  10.7 43.3 %all-gather.8.cloned.1.call-done = bf16[256,4096]{1,0:T(8,128)(2,1)} async-done(((bf16[256,512]{1,0:T(8,128)(2,1)}), bf16[256,4096]{1,0:T(8,128)(2,1)}) %all-gather.8.cloned.1.call-update) | async-done | bytes 2097168 | tf_op jit(solution)/shard_map/all_gather | solution.py:23
  54.0 89.6 %all-gather.10.cloned.1.call-done = bf16[3,4096,2,128]{1,2,0,3:T(2,128)(2,1)} async-done(((bf16[3,4096,2,2]{1,2,0,3:T(2,128)(2,1)}), bf16[3,4096,2,128]{1,2,0,3:T(2,128)(2,1)}) %all-gather.10.cloned.1.call-update) | async-done | bytes 6291472 | tf_op jit(solution)/shard_map/all_gather | solution.py:29
  143.7 10.3 %fusion.11 = f32[3,256,2,128]{1,3,2,0:T(8,128)S(1)} fusion(bf16[256,4096]{1,0:T(8,128)(2,1)} %all-gather.8.cloned.1.call-done, bf16[3,4096,2,128]{1,2,0,3:T(2,128)(2,1)} %all-gather.10.cloned.1.call-done), kind=kOutput, calls=%fused_computation.11 | convolution fusion | flops 1610612736 | bytes 9175040 | tf_op jit(solution)/shard_map/td,mdhc->mthc/dot_general | solution.py:26
  154.0 76.3 %all-gather.6.cloned.1.call-done = bf16[3,4096,2,128]{1,2,0,3:T(2,128)(2,1)} async-done(((bf16[3,4096,2,2]{1,2,0,3:T(2,128)(2,1)}), bf16[3,4096,2,128]{1,2,0,3:T(2,128)(2,1)}) %all-gather.6.cloned.1.call-update) | async-done | bytes 6291472 | tf_op jit(solution)/shard_map/all_gather | solution.py:28
  230.3 10.5 %fusion.6 = f32[3,256,2,128]{1,3,2,0:T(8,128)S(1)} fusion(bf16[256,4096]{1,0:T(8,128)(2,1)} %all-gather.8.cloned.1.call-done, bf16[3,4096,2,128]{1,2,0,3:T(2,128)(2,1)} %all-gather.6.cloned.1.call-done), kind=kOutput, calls=%fused_computation.10 | convolution fusion | flops 1610612736 | bytes 9175040 | tf_op jit(solution)/shard_map/td,mdhc->mthc/dot_general | solution.py:26
  242.5 80.8 %all-gather.14.cloned.1.call-done = bf16[64,2,128,128]{3,2,1,0:T(8,128)(2,1)} async-done(((bf16[1,2,128,128]{3,2,1,0:T(8,128)(2,1)}), bf16[64,2,128,128]{3,2,1,0:T(8,128)(2,1)}) %all-gather.14.cloned.1.call-update) | async-done | bytes 4194320 | tf_op jit(solution)/shard_map/all_gather | solution.py:9
  323.4 56.1 %while.21 = (s32[]{:T(128)}, f32[2,128,128]{2,1,0:T(8,128)S(1)}, s32[]{:T(128)}, bf16[64,2,128,128]{3,2,1,0:T(8,128)(2,1)}, s32[]{:T(128)}, /*index=5*/s32[]{:T(128)}, s32[]{:T(128)}) while((s32[]{:T(128)}, f32[2,128,128]{2,1,0:T(8,128)S(1)}, s32[]{:T(128)}, bf16[64,2,128,128]{3,2,1,0:T(8,128)(2,1)}, s32[]{:T(128)}, /*index=5*/s32[]{:T(128)}, ...), condition=%wide.region_3.4_spmd, body=%wide.region_2.3_spmd.sunk | while | flops 65541 | bytes 327795 | solution.py:15
  328.7 0.9 convert_add_fusion.5
  331.4 0.9 convert_add_fusion.5
  334.1 0.9 convert_add_fusion.5
  336.7 0.9 convert_add_fusion.5
  340.3 0.9 convert_add_fusion.5
  341.2 0.9 convert_add_fusion.5
  342.1 0.9 convert_add_fusion.5
  344.8 0.9 convert_add_fusion.5
  347.4 0.9 convert_add_fusion.5
  352.8 0.9 convert_add_fusion.5
  354.6 0.9 convert_add_fusion.5
  356.3 0.9 convert_add_fusion.5
  358.1 0.9 convert_add_fusion.5
  359.0 0.9 convert_add_fusion.5
  359.9 0.9 convert_add_fusion.5
  368.8 0.9 convert_add_fusion.5
  371.5 0.9 convert_add_fusion.5
  374.1 0.9 convert_add_fusion.5
  376.8 0.9 convert_add_fusion.5
  379.6 28.9 %all-gather.12.cloned.1.call-done = bf16[64,2,128,128]{3,2,1,0:T(8,128)(2,1)} async-done(((bf16[1,2,128,128]{3,2,1,0:T(8,128)(2,1)}), bf16[64,2,128,128]{3,2,1,0:T(8,128)(2,1)}) %all-gather.12.cloned.1.call-update) | async-done | bytes 4194320 | tf_op jit(solution)/shard_map/all_gather | solution.py:9
  408.5 56.1 %while.20 = (s32[]{:T(128)}, f32[2,128,128]{2,1,0:T(8,128)S(1)}, s32[]{:T(128)}, bf16[64,2,128,128]{3,2,1,0:T(8,128)(2,1)}, s32[]{:T(128)}, /*index=5*/s32[]{:T(128)}, s32[]{:T(128)}) while((s32[]{:T(128)}, f32[2,128,128]{2,1,0:T(8,128)S(1)}, s32[]{:T(128)}, bf16[64,2,128,128]{3,2,1,0:T(8,128)(2,1)}, s32[]{:T(128)}, /*index=5*/s32[]{:T(128)}, ...), condition=%wide.region_1.2_spmd, body=%wide.region_0.1_spmd.sunk | while | flops 65541 | bytes 327795 | solution.py:15
  410.3 0.9 convert_add_fusion.4
  465.6 0.9 copy.18
  (130 shorter events, 95.2 us)
Async XLA Ops:
  6.5 47.5 %all-gather.8.cloned.1.call-start = ((), (), s32[]{:S(2)}) async-start(), calls=%async_computation.1 | async-start | bytes 2359296 | tf_op jit(solution)/shard_map/all_gather | solution.py:23
  7.3 136.4 %all-gather.10.cloned.1.call-start = ((), (), s32[]{:S(2)}) async-start(), calls=%async_computation.2 | async-start | bytes 6389760 | tf_op jit(solution)/shard_map/all_gather | solution.py:29
  9.0 221.3 %all-gather.6.cloned.1.call-start = ((), (), s32[]{:S(2)}) async-start(), calls=%async_computation | async-start | bytes 6389760 | tf_op jit(solution)/shard_map/all_gather | solution.py:28
  10.7 312.7 %all-gather.14.cloned.1.call-start = ((), (), s32[]{:S(2)}) async-start(), calls=%async_computation.4 | async-start | bytes 4259840 | tf_op jit(solution)/shard_map/all_gather | solution.py:9
  154.0 86.8 %copy-start = (f32[2]{0:T(128)S(1)}, f32[2]{0:T(128)}, u32[]{:S(2)}) copy-start(f32[2]{0:T(128)} %constant.37) | copy-start | bytes 28
  241.9 166.6 %all-gather.12.cloned.1.call-start = ((), (), s32[]{:S(2)}) async-start(), calls=%async_computation.3 | async-start | bytes 4259840 | tf_op jit(solution)/shard_map/all_gather | solution.py:9
Sparse Core Ops, SparseCore 0:
  9.4 44.5 all-gather.7
  57.4 86.2 all-gather.9
  147.0 83.2 all-gather.5
  242.0 81.2 all-gather.13
  326.6 81.9 all-gather.11
where the time goes:
time: 479 us; the launch traced here: 473 us
  waiting for transfers between devices  320 us (67%)
  other arithmetic  109 us (23%)
  matrix products  21.8 us (5%)
  between operations  13.3 us (3%)
  local copies, waits for them, and re-layouts  5.03 us (1%)
    all_gather x2, waiting for transfers between devices, prefix(): gathered = lax.all_gather(shard.astype(jnp.bfloat16), axis)  110 us
    add x126, other arithmetic, add_states(): return earlier + later  109 us
    all_gather x1, waiting for transfers between devices, on_device(): direct_out = project(lax.all_gather(directions, 'ctx', axis=3, tiled=True))  89.6 us
    all_gather x1, waiting for transfers between devices, on_device(): base_out = project(lax.all_gather(proj_weights, 'ctx', axis=3, tiled=True))  76.3 us
    all_gather x1, waiting for transfers between devices, on_device(): tokens = lax.all_gather(hidden_in, 'head', axis=1, tiled=True)  43.3 us
    dot_general x2, matrix products, project(): jnp.einsum('td,mdhc->mthc', tokens, block_piece, preferred_element_type=j...  20.8 us
  transfers between devices with their start and end apart: 5, of which 5 were waited for; matrix products, arithmetic and copies ran while one was open for 14% of the time, Pallas kernels for 0%

commit v1 on v0

v1 whole, which is shorter than its diff:
```python
import functools

import jax
import jax.numpy as jnp
from jax import lax
from jax.experimental import pallas as pl
from jax.experimental.pallas import tpu as pltpu
from jax.sharding import Mesh
from jax.sharding import PartitionSpec as P

NX, NY, NC, NZ = 4, 8, 2, 8
TOK, HD, PIECE = 256, 128, 512
D = NZ * PIECE
STEP = 0.1 * D ** (-0.5)
F32, BF16 = jnp.float32, jnp.bfloat16


def replicate(x, n):
    return jnp.broadcast_to(x[None], (n,) + x.shape)


def exchange(x, axes):
    return lax.all_to_all(x, axes, 0, 0, tiled=True)


def signs_and_order(acc, kinds, x_major):
    cols = acc.shape[1]
    lane = lax.broadcasted_iota(jnp.int32, acc.shape, 1)
    left = pltpu.roll(acc, cols - 2, 1)
    right = pltpu.roll(acc, 2, 1)
    step = jnp.float32(STEP)
    signed = jnp.where((lane & 3) < 2, acc + step * left, right + (-step) * acc).astype(BF16)
    row = lax.broadcasted_iota(jnp.int32, (cols, cols), 0)
    col = lax.broadcasted_iota(jnp.int32, (cols, cols), 1)
    j = row & 1
    sign = (row >> 1) & 1
    kind = (row >> 2) & (kinds - 1)
    rest = row >> (2 + (kinds - 1))
    core = rest & 1
    chip = rest >> 1
    if not x_major:
        chip = (chip & (NX - 1)) * NY + (chip >> 2)
    target = (kind * 2 + sign) * HD + (chip * 2 + core) * 2 + j
    pick = jnp.where(col == target, jnp.float32(1.0), jnp.float32(0.0)).astype(BF16)
    return jnp.dot(signed, pick, preferred_element_type=F32).astype(BF16)


NT = (((1,), (1,)), ((), ()))
TN = (((0,), (0,)), ((), ()))


def accumulate(own_ref, other_ref, weight_ref, acc):
    @pl.when(pl.program_id(0) == 0)
    def _():
        acc[...] = jnp.zeros_like(acc)

    weight = weight_ref[...]
    for block, ref in enumerate((own_ref, other_ref)):
        acc[block] += lax.dot_general(ref[0], weight, NT, preferred_element_type=F32)


def query_kernel(own_ref, other_ref, weight_ref, out_ref, acc):
    accumulate(own_ref, other_ref, weight_ref, acc)

    @pl.when(pl.program_id(0) == NZ - 1)
    def _():
        for block in range(2):
            rows = signs_and_order(acc[block], 1, True)
            for s in range(2):
                out_ref[block, s] = rows[:, s * HD : (s + 1) * HD]


def key_value_kernel(own_ref, other_ref, weight_ref, out_ref, state_ref, total_ref, acc):
    accumulate(own_ref, other_ref, weight_ref, acc)

    @pl.when(pl.program_id(0) == NZ - 1)
    def _():
        for block in range(2):
            rows = signs_and_order(acc[block], 2, False)
            for s in range(2):
                key = rows[:, s * HD : (s + 1) * HD]
                value = rows[:, (2 + s) * HD : (3 + s) * HD]
                out_ref[0, block, s] = key
                out_ref[1, block, s] = value
                state_ref[block, s] = lax.dot_general(key, value, TN, preferred_element_type=F32)
        total_ref[...] = (state_ref[0] + state_ref[1]).astype(BF16)


def project(kernel, own, other, weight, out_shape):
    rows = weight.shape[0]
    piece = pl.BlockSpec((1, TOK, PIECE), lambda k: (k, 0, 0))
    whole = jax.tree.map(lambda s: pl.BlockSpec(s.shape, lambda k, n=len(s.shape): (0,) * n), out_shape)
    return pl.pallas_call(
        kernel,
        grid=(NZ,),
        in_specs=[piece, piece, pl.BlockSpec((rows, PIECE), lambda k: (0, k))],
        out_specs=whole,
        out_shape=out_shape,
        scratch_shapes=[pltpu.VMEM((2, TOK, rows), F32)],
        compiler_params=pltpu.CompilerParams(
            dimension_semantics=("arbitrary",), vmem_limit_bytes=32 << 20
        ),
    )(own, other, weight)


def inner_kernel(query_ref, kv_ref, out_ref):
    row = lax.broadcasted_iota(jnp.int32, (TOK, TOK), 0)
    col = lax.broadcasted_iota(jnp.int32, (TOK, TOK), 1)
    for block in range(2):
        for s in range(2):
            scores = lax.dot_general(
                query_ref[block, s], kv_ref[0, block, s], NT, preferred_element_type=F32
            )
            weights = jnp.where(col <= row, scores, 0.0).astype(BF16)
            out_ref[block, s] = jnp.dot(weights, kv_ref[1, block, s], preferred_element_type=F32)


def cross_kernel(query_ref, inner_ref, state_ref, partial_ref, out_ref):
    core = lax.axis_index("c")
    prior = jnp.sum(partial_ref[...].astype(F32), axis=0)
    for block in range(2):
        later = jnp.where(core == (1 - block), jnp.float32(1.0), jnp.float32(0.0))
        for s in range(2):
            carried = (prior[s] + later * state_ref[1 - block, s]).astype(BF16)
            combined = inner_ref[block, s] + jnp.dot(
                query_ref[block, s], carried, preferred_element_type=F32
            )
            scale = lax.rsqrt(jnp.mean(combined * combined, axis=-1, keepdims=True) + 1e-05)
            out_ref[block, s] = (combined * scale).astype(BF16)


def call(kernel, out_shape, *args):
    return pl.pallas_call(
        kernel,
        out_shape=out_shape,
        in_specs=[pl.BlockSpec(memory_space=pltpu.VMEM)] * len(args),
        out_specs=pl.BlockSpec(memory_space=pltpu.VMEM),
        compiler_params=pltpu.CompilerParams(vmem_limit_bytes=32 << 20),
    )(*args)


def shape(*dims, dtype=BF16):
    return jax.ShapeDtypeStruct(dims, dtype)


def on_device(hidden_in, proj_weights, directions):
    x, y, c = (lax.axis_index(name) for name in "xyc")
    swap = [(0, 1), (1, 0)]

    both = jnp.stack(
        [jnp.transpose(proj_weights, (0, 2, 3, 1)), jnp.transpose(directions, (0, 2, 3, 1))], axis=2
    )
    kv_rows = jnp.transpose(both[1:], (1, 0, 2, 3, 4)).reshape(NC, 8, D)
    q_rows = both[0].reshape(NC, 4, D)

    own = exchange(replicate(hidden_in, NZ), "z")
    kv_part = exchange(replicate(kv_rows, NX).reshape(NX * NC, 8, D), ("x", "c"))
    q_part = exchange(replicate(q_rows, NY).reshape(NY * NC, 4, D), ("y", "c"))
    kv_weight = lax.all_gather(kv_part.reshape(64, D), "y", axis=0, tiled=True)
    q_weight = exchange(replicate(q_part.reshape(64, D), NX), "x").reshape(256, D)
    other = lax.ppermute(own, "c", swap)

    query = project(query_kernel, own, other, q_weight, shape(2, 2, TOK, HD))
    kv, state, total = project(
        key_value_kernel,
        own,
        other,
        kv_weight,
        (shape(2, 2, 2, TOK, HD), shape(2, 2, HD, HD, dtype=F32), shape(2, HD, HD)),
    )

    over_x = exchange(replicate(total, NX), "x")
    before = (jnp.arange(NX) < x).astype(F32)
    earlier = jnp.sum(over_x.astype(F32) * before[:, None, None, None], axis=0)
    later = (jnp.arange(NY) > y).astype(F32)
    sent = earlier[None] + later[:, None, None, None] * (state[0] + state[1])[None]
    partial = exchange(sent.astype(BF16), "y")

    inner = call(inner_kernel, shape(2, 2, TOK, HD, dtype=F32), query, kv)
    out = call(cross_kernel, shape(2, 2, TOK, HD), query, inner, state, partial)
    mine, theirs = out[0], lax.ppermute(out[1], "c", swap)
    first = jnp.where(c == 0, mine, theirs)
    second = jnp.where(c == 0, theirs, mine)
    return jnp.stack([first, second], axis=2)


def solution(mesh):
    mesh4 = Mesh(mesh.devices.reshape(NX, NY, NC, NZ), ("x", "y", "c", "z"))
    ctx = ("x", "y", "c")
    return jax.shard_map(
        on_device,
        mesh=mesh4,
        in_specs=(P(ctx, "z"), P(None, None, "z", ctx), P(None, None, "z", ctx)),
        out_specs=P(None, ctx, "z", None),
        check_vma=False,
    )
```

time: 479 us -> 191 us (0.40)
  the two profiles are of different devices: /device:TPU:63 before, /device:TPU:1 now
where the time goes in v1:
time: 191 us; the launch traced here: 190 us
  blocking collectives  74.3 us (39%)
  waiting for transfers between devices  48.8 us (26%)
  starting transfers between devices  26.4 us (14%)
  Pallas kernels  15.3 us (8%)
  between operations  13.7 us (7%)
  local copies, waits for them, and re-layouts  7.94 us (4%)
  other arithmetic  3.35 us (2%)
    all_to_all x2, blocking collectives, exchange(): return lax.all_to_all(x, axes, 0, 0, tiled=True)  74.3 us
    all_to_all x4, waiting for transfers between devices, exchange(): return lax.all_to_all(x, axes, 0, 0, tiled=True)  47.8 us
    all_to_all x4, starting transfers between devices, exchange(): return lax.all_to_all(x, axes, 0, 0, tiled=True)  19.2 us
    pallas_call x2, Pallas kernels, project(): pl.pallas_call(kernel, grid=(NZ,), in_specs=[piece, piece, pl.BlockSpec((...  14.2 us
    ppermute x1, starting transfers between devices, on_device(): other = lax.ppermute(own, 'c', swap)  4.79 us
  transfers between devices with their start and end apart: 7, of which 5 were waited for; matrix products, arithmetic and copies ran while one was open for 2% of the time, Pallas kernels for 8%

profile of v1, /device:TPU:1, one launch (start us, length us, event | category | flops | bytes accessed | tf_op | source)
XLA Modules:
  0.0 189.8 jit_solution(6668088964826162354)
XLA Ops:
  6.5 1.1 fusion
  7.6 0.1 copy.12
  7.8 0.1 copy.13
  7.9 19.3 %all_to_all.30 = bf16[8,8,4096]{2,1,0:T(8,128)(2,1)} all-to-all(bf16[8,8,4096]{2,1,0:T(8,128)(2,1)S(1)} %bitcast.28), channel_id=1, replica_groups=mesh['x'=4,'y'=8,'c'=2,'z'=8] {'x','c'}, dimensions={0} | all-to-all | bytes 1048576 | tf_op jit(solution)/shard_map/all_to_all | solution.py:23
  27.3 0.2 broadcast_in_dim.16
  27.5 55.0 %all_to_all.31.own_ref = bf16[8,256,512]{2,1,0:T(8,128)(2,1)S(1)} all-to-all(bf16[8,256,512]{2,1,0:T(8,128)(2,1)S(1)} %broadcast_in_dim.16), channel_id=1, replica_groups=mesh['x'=4,'y'=8,'c'=2,'z'=8] {'z'}, dimensions={0} | all-to-all | bytes 4194304 | tf_op jit(solution)/shard_map/all_to_all | solution.py:23
  82.5 4.8 %collective-permute-start = (bf16[8,256,512]{2,1,0:T(8,128)(2,1)S(1)}, bf16[8,256,512]{2,1,0:T(8,128)(2,1)}, u32[]{:S(2)}, u32[]{:S(2)}) collective-permute-start(bf16[8,256,512]{2,1,0:T(8,128)(2,1)S(1)} %all_to_all.31.own_ref), channel_id=1, source_target_pairs={{0,8},{8,0},{1,9},{9,1},{2,10},{10,2},{3,11},{11,3},{4,12},{12,4},... | collective-permute-start | bytes 6291464 | tf_op jit(solution)/shard_map/ppermute | solution.py:161
  87.3 0.1 pad_maximum_fusion.2
  87.4 0.1 copy.10
  87.5 1.0 broadcast_in_dim.18
  88.5 7.2 %all-to-all-start.1 = ((bf16[16,4,4096]{2,1,0:T(4,128)(2,1)}), bf16[16,4,4096]{2,1,0:T(4,128)(2,1)S(1)}, u32[]{:S(2)}, u32[]{:S(2)}) async-start(bf16[16,4,4096]{2,1,0:T(4,128)(2,1)} %bitcast.5), calls=%async_computation.1 | async-start | bytes 1048576 | tf_op jit(solution)/shard_map/all_to_all | solution.py:23
  95.8 2.2 %copy-done = bf16[512,4096]{1,0:T(8,128)(2,1)S(1)} copy-done((bf16[512,4096]{1,0:T(8,128)(2,1)S(1)}, bf16[512,4096]{1,0:T(8,128)(2,1)}, u32[]{:S(2)}) %copy-start) | copy-done | bytes 4194328
  98.0 7.7 %shard_map.38 = (bf16[2,2,2,256,128]{4,3,2,1,0:T(8,128)(2,1)S(1)}, f32[2,2,128,128]{3,2,1,0:T(8,128)S(1)}, bf16[2,128,128]{2,1,0:T(8,128)(2,1)S(1)}) custom-call(bf16[8,256,512]{2,1,0:T(8,128)(2,1)S(1)} %all_to_all.31.own_ref, bf16[8,256,512]{2,1,0:T(8,128)(2,1)} %collective-permute-done.other_ref, bf16[512,4096]{1,0:T(8,128)(2,1)S(1)} %copy-done), custom_call_target="tpu_custom_call" | custom-call | tf_op jit(solution)/shard_map/pallas_call | solution.py:93
  105.7 0.8 copy-done.1
  106.5 6.6 %all-to-all-done.1 = bf16[16,4,4096]{2,1,0:T(4,128)(2,1)S(1)} async-done(((bf16[16,4,4096]{2,1,0:T(4,128)(2,1)}), bf16[16,4,4096]{2,1,0:T(4,128)(2,1)S(1)}, u32[]{:S(2)}, u32[]{:S(2)}) %all-to-all-start.1) | async-done | bytes 524320 | tf_op jit(solution)/shard_map/all_to_all | solution.py:23
  113.1 0.7 broadcast_in_dim.44
  113.8 4.0 %all-to-all-start.4 = ((bf16[4,2,128,128]{3,2,1,0:T(8,128)(2,1)}), bf16[4,2,128,128]{3,2,1,0:T(8,128)(2,1)}, u32[]{:S(2)}, u32[]{:S(2)}) async-start(bf16[4,2,128,128]{3,2,1,0:T(8,128)(2,1)} %broadcast_in_dim.44), calls=%async_computation.4 | async-start | bytes 524288 | tf_op jit(solution)/shard_map/all_to_all | solution.py:23
  117.9 0.1 broadcast_in_dim.19
  118.0 6.1 %all-to-all-done.4 = bf16[4,2,128,128]{3,2,1,0:T(8,128)(2,1)} async-done(((bf16[4,2,128,128]{3,2,1,0:T(8,128)(2,1)}), bf16[4,2,128,128]{3,2,1,0:T(8,128)(2,1)}, u32[]{:S(2)}, u32[]{:S(2)}) %all-to-all-start.4) | async-done | bytes 262176 | tf_op jit(solution)/shard_map/all_to_all | solution.py:23
  124.1 1.6 broadcast_in_dim.20
  125.7 4.5 %all-to-all-start.2 = ((bf16[4,64,4096]{2,1,0:T(8,128)(2,1)}), bf16[4,64,4096]{2,1,0:T(8,128)(2,1)}, u32[]{:S(2)}, u32[]{:S(2)}) async-start(bf16[4,64,4096]{2,1,0:T(8,128)(2,1)} %broadcast_in_dim.20), calls=%async_computation.2 | async-start | bytes 4194304 | tf_op jit(solution)/shard_map/all_to_all | solution.py:23
  130.2 1.1 multiply_reduce_fusion
  131.3 1.0 add_convert_fusion
  132.3 24.4 %all-to-all-done.2 = bf16[4,64,4096]{2,1,0:T(8,128)(2,1)} async-done(((bf16[4,64,4096]{2,1,0:T(8,128)(2,1)}), bf16[4,64,4096]{2,1,0:T(8,128)(2,1)}, u32[]{:S(2)}, u32[]{:S(2)}) %all-to-all-start.2) | async-done | bytes 2097184 | tf_op jit(solution)/shard_map/all_to_all | solution.py:23
  156.7 3.5 %all-to-all-start.5 = ((bf16[8,2,128,128]{3,2,1,0:T(8,128)(2,1)}), bf16[8,2,128,128]{3,2,1,0:T(8,128)(2,1)S(1)}, u32[]{:S(2)}, u32[]{:S(2)}) async-start(bf16[8,2,128,128]{3,2,1,0:T(8,128)(2,1)} %add_convert_fusion), calls=%async_computation.5 | async-start | bytes 1048576 | tf_op jit(solution)/shard_map/all_to_all | solution.py:23
  160.2 6.5 %shard_map.37.query_ref = bf16[2,2,256,128]{3,2,1,0:T(8,128)(2,1)S(1)} custom-call(bf16[8,256,512]{2,1,0:T(8,128)(2,1)S(1)} %all_to_all.31.own_ref, bf16[8,256,512]{2,1,0:T(8,128)(2,1)} %collective-permute-done.other_ref, bf16[256,4096]{1,0:T(8,128)(2,1)} %bitcast.6.weight_ref), custom_call_target="tpu_custom_call" | custom-call | tf_op jit(solution)/shard_map/pallas_call | solution.py:93
  166.7 0.7 shard_map.39.inner_ref
  167.4 10.7 %all-to-all-done.5.partial_ref = bf16[8,2,128,128]{3,2,1,0:T(8,128)(2,1)S(1)} async-done(((bf16[8,2,128,128]{3,2,1,0:T(8,128)(2,1)}), bf16[8,2,128,128]{3,2,1,0:T(8,128)(2,1)S(1)}, u32[]{:S(2)}, u32[]{:S(2)}) %all-to-all-start.5) | async-done | bytes 524320 | tf_op jit(solution)/shard_map/all_to_all | solution.py:23
  178.1 0.4 shard_map.40
  178.5 2.4 %collective-permute-start.1 = (bf16[2,256,128]{2,1,0:T(8,128)(2,1)S(1)}, bf16[2,256,128]{2,1,0:T(8,128)(2,1)S(1)}, u32[]{:S(2)}, u32[]{:S(2)}) collective-permute-start(bf16[2,256,128]{2,1,0:T(8,128)(2,1)S(1)} %slice_bitcast_fusion), channel_id=1, source_target_pairs={{0,8},{8,0},{1,9},{9,1},{2,10},{10,2},{3,11},{11,3},{4,12},{12,4},... | collective-permute-start | bytes 393224 | tf_op jit(solution)/shard_map/ppermute | solution.py:181
  180.9 1.0 collective-permute-done.1
  182.0 1.0 copy.14
  (22 shorter events, 0.2 us)
Async XLA Ops:
  6.5 20.7 %copy-start.5 = (bf16[256,512]{1,0:T(8,128)(2,1)S(1)}, bf16[256,512]{1,0:T(8,128)(2,1)}, u32[]{:S(2)}) copy-start(bf16[256,512]{1,0:T(8,128)(2,1)} %param.3) | copy-start | bytes 786436
  6.5 89.2 %all-gather.2.cloned.1.call-start = ((), (), s32[]{:S(2)}) async-start(), calls=%async_computation.6 | async-start | bytes 4718592 | tf_op jit(solution)/shard_map/all_gather | solution.py:159
  27.5 59.8 %copy-start.3 = (bf16[3,4096,2,2]{1,3,2,0:T(2,128)(2,1)S(1)}, bf16[3,4096,2,2]{1,3,2,0:T(2,128)(2,1)}, u32[]{:S(2)}) copy-start(bf16[3,4096,2,2]{1,3,2,0:T(2,128)(2,1)} %param.5) | copy-start | bytes 294916
  27.5 59.8 %copy-start.4 = (bf16[3,4096,2,2]{1,3,2,0:T(2,128)(2,1)S(1)}, bf16[3,4096,2,2]{1,3,2,0:T(2,128)(2,1)}, u32[]{:S(2)}) copy-start(bf16[3,4096,2,2]{1,3,2,0:T(2,128)(2,1)} %param.4) | copy-start | bytes 294916
  82.5 13.3 %collective-permute-start = (bf16[8,256,512]{2,1,0:T(8,128)(2,1)S(1)}, bf16[8,256,512]{2,1,0:T(8,128)(2,1)}, u32[]{:S(2)}, u32[]{:S(2)}) collective-permute-start(bf16[8,256,512]{2,1,0:T(8,128)(2,1)S(1)} %all_to_all.31.own_ref), channel_id=1, source_target_pairs={{0,8},{8,0},{1,9},{9,1},{2,10},{10,2},{3,11},{11,3},{4,12},{12,4},... | collective-permute-start | bytes 6291464 | tf_op jit(solution)/shard_map/ppermute | solution.py:161
  88.5 24.5 %all-to-all-start.1 = ((bf16[16,4,4096]{2,1,0:T(4,128)(2,1)}), bf16[16,4,4096]{2,1,0:T(4,128)(2,1)S(1)}, u32[]{:S(2)}, u32[]{:S(2)}) async-start(bf16[16,4,4096]{2,1,0:T(4,128)(2,1)} %bitcast.5), calls=%async_computation.1 | async-start | bytes 1048576 | tf_op jit(solution)/shard_map/all_to_all | solution.py:23
  95.8 2.2 %copy-start = (bf16[512,4096]{1,0:T(8,128)(2,1)S(1)}, bf16[512,4096]{1,0:T(8,128)(2,1)}, u32[]{:S(2)}) copy-start(bf16[512,4096]{1,0:T(8,128)(2,1)} %all-gather.2.cloned.1.call-done.weight_ref) | copy-start | bytes 12582916
  105.7 0.8 copy-start.1
  113.8 10.3 %all-to-all-start.4 = ((bf16[4,2,128,128]{3,2,1,0:T(8,128)(2,1)}), bf16[4,2,128,128]{3,2,1,0:T(8,128)(2,1)}, u32[]{:S(2)}, u32[]{:S(2)}) async-start(bf16[4,2,128,128]{3,2,1,0:T(8,128)(2,1)} %broadcast_in_dim.44), calls=%async_computation.4 | async-start | bytes 524288 | tf_op jit(solution)/shard_map/all_to_all | solution.py:23
  125.7 31.0 %all-to-all-start.2 = ((bf16[4,64,4096]{2,1,0:T(8,128)(2,1)}), bf16[4,64,4096]{2,1,0:T(8,128)(2,1)}, u32[]{:S(2)}, u32[]{:S(2)}) async-start(bf16[4,64,4096]{2,1,0:T(8,128)(2,1)} %broadcast_in_dim.20), calls=%async_computation.2 | async-start | bytes 4194304 | tf_op jit(solution)/shard_map/all_to_all | solution.py:23
  156.7 21.4 %all-to-all-start.5 = ((bf16[8,2,128,128]{3,2,1,0:T(8,128)(2,1)}), bf16[8,2,128,128]{3,2,1,0:T(8,128)(2,1)S(1)}, u32[]{:S(2)}, u32[]{:S(2)}) async-start(bf16[8,2,128,128]{3,2,1,0:T(8,128)(2,1)} %add_convert_fusion), calls=%async_computation.5 | async-start | bytes 1048576 | tf_op jit(solution)/shard_map/all_to_all | solution.py:23
  160.2 6.5 %copy-start.2 = (bf16[2,2,2,256,128]{4,3,2,1,0:T(8,128)(2,1)S(1)}, bf16[2,2,2,256,128]{4,3,2,1,0:T(8,128)(2,1)}, u32[]{:S(2)}) copy-start(bf16[2,2,2,256,128]{4,3,2,1,0:T(8,128)(2,1)} %copy-done.1) | copy-start | bytes 1572868
  178.5 3.4 %collective-permute-start.1 = (bf16[2,256,128]{2,1,0:T(8,128)(2,1)S(1)}, bf16[2,256,128]{2,1,0:T(8,128)(2,1)S(1)}, u32[]{:S(2)}, u32[]{:S(2)}) collective-permute-start(bf16[2,256,128]{2,1,0:T(8,128)(2,1)S(1)} %slice_bitcast_fusion), channel_id=1, source_target_pairs={{0,8},{8,0},{1,9},{9,1},{2,10},{10,2},{3,11},{11,3},{4,12},{12,4},... | collective-permute-start | bytes 393224 | tf_op jit(solution)/shard_map/ppermute | solution.py:181
Sparse Core Ops, SparseCore 0:
  27.4 56.0 all-gather.1

commit v2 on v1

--- a/solution.py
+++ b/solution.py
@@ -23,13 +23,8 @@
     return lax.all_to_all(x, axes, 0, 0, tiled=True)
 
 
-def signs_and_order(acc, kinds, x_major):
-    cols = acc.shape[1]
-    lane = lax.broadcasted_iota(jnp.int32, acc.shape, 1)
-    left = pltpu.roll(acc, cols - 2, 1)
-    right = pltpu.roll(acc, 2, 1)
-    step = jnp.float32(STEP)
-    signed = jnp.where((lane & 3) < 2, acc + step * left, right + (-step) * acc).astype(BF16)
+def column_order(kinds, x_major):
+    cols = kinds * 2 * HD
     row = lax.broadcasted_iota(jnp.int32, (cols, cols), 0)
     col = lax.broadcasted_iota(jnp.int32, (cols, cols), 1)
     j = row & 1
@@ -41,8 +36,17 @@
     if not x_major:
         chip = (chip & (NX - 1)) * NY + (chip >> 2)
     target = (kind * 2 + sign) * HD + (chip * 2 + core) * 2 + j
-    pick = jnp.where(col == target, jnp.float32(1.0), jnp.float32(0.0)).astype(BF16)
-    return jnp.dot(signed, pick, preferred_element_type=F32).astype(BF16)
+    return (col == target).astype(BF16)
+
+
+def signs_and_order(acc, order):
+    cols = acc.shape[1]
+    lane = lax.broadcasted_iota(jnp.int32, acc.shape, 1)
+    left = pltpu.roll(acc, cols - 2, 1)
+    right = pltpu.roll(acc, 2, 1)
+    step = jnp.float32(STEP)
+    signed = jnp.where((lane & 3) < 2, acc + step * left, right + (-step) * acc).astype(BF16)
+    return jnp.dot(signed, order, preferred_element_type=F32).astype(BF16)
 
 
 NT = (((1,), (1,)), ((), ()))
@@ -59,24 +63,26 @@
         acc[block] += lax.dot_general(ref[0], weight, NT, preferred_element_type=F32)
 
 
-def query_kernel(own_ref, other_ref, weight_ref, out_ref, acc):
+def query_kernel(z_ref, own_ref, other_ref, weight_ref, order_ref, out_ref, acc):
     accumulate(own_ref, other_ref, weight_ref, acc)
 
     @pl.when(pl.program_id(0) == NZ - 1)
     def _():
         for block in range(2):
-            rows = signs_and_order(acc[block], 1, True)
+            rows = signs_and_order(acc[block], order_ref[...])
             for s in range(2):
                 out_ref[block, s] = rows[:, s * HD : (s + 1) * HD]
 
 
-def key_value_kernel(own_ref, other_ref, weight_ref, out_ref, state_ref, total_ref, acc):
+def key_value_kernel(
+    z_ref, own_ref, other_ref, weight_ref, order_ref, out_ref, state_ref, total_ref, acc
+):
     accumulate(own_ref, other_ref, weight_ref, acc)
 
     @pl.when(pl.program_id(0) == NZ - 1)
     def _():
         for block in range(2):
-            rows = signs_and_order(acc[block], 2, False)
+            rows = signs_and_order(acc[block], order_ref[...])
             for s in range(2):
                 key = rows[:, s * HD : (s + 1) * HD]
                 value = rows[:, (2 + s) * HD : (3 + s) * HD]
@@ -86,21 +92,31 @@
         total_ref[...] = (state_ref[0] + state_ref[1]).astype(BF16)
 
 
-def project(kernel, own, other, weight, out_shape):
+def project(kernel, z, own, other, weight, order, out_shape):
     rows = weight.shape[0]
-    piece = pl.BlockSpec((1, TOK, PIECE), lambda k: (k, 0, 0))
-    whole = jax.tree.map(lambda s: pl.BlockSpec(s.shape, lambda k, n=len(s.shape): (0,) * n), out_shape)
+    piece = pl.BlockSpec((1, TOK, PIECE), lambda k, z: (k, 0, 0))
+    whole = jax.tree.map(
+        lambda s: pl.BlockSpec(s.shape, lambda k, z, n=len(s.shape): (0,) * n), out_shape
+    )
     return pl.pallas_call(
         kernel,
-        grid=(NZ,),
-        in_specs=[piece, piece, pl.BlockSpec((rows, PIECE), lambda k: (0, k))],
-        out_specs=whole,
+        grid_spec=pltpu.PrefetchScalarGridSpec(
+            num_scalar_prefetch=1,
+            grid=(NZ,),
+            in_specs=[
+                piece,
+                piece,
+                pl.BlockSpec((rows, PIECE), lambda k, z: (0, (z[0] + k) & (NZ - 1))),
+                pl.BlockSpec((rows, rows), lambda k, z: (0, 0)),
+            ],
+            out_specs=whole,
+            scratch_shapes=[pltpu.VMEM((2, TOK, rows), F32)],
+        ),
         out_shape=out_shape,
-        scratch_shapes=[pltpu.VMEM((2, TOK, rows), F32)],
         compiler_params=pltpu.CompilerParams(
-            dimension_semantics=("arbitrary",), vmem_limit_bytes=32 << 20
+            dimension_semantics=("arbitrary",), vmem_limit_bytes=16 << 20
         ),
-    )(own, other, weight)
+    )(z, own, other, pltpu.with_memory_space_constraint(weight, pltpu.HBM), order)
 
 
 def inner_kernel(query_ref, kv_ref, out_ref):
@@ -135,7 +151,7 @@
         out_shape=out_shape,
         in_specs=[pl.BlockSpec(memory_space=pltpu.VMEM)] * len(args),
         out_specs=pl.BlockSpec(memory_space=pltpu.VMEM),
-        compiler_params=pltpu.CompilerParams(vmem_limit_bytes=32 << 20),
+        compiler_params=pltpu.CompilerParams(vmem_limit_bytes=12 << 20),
     )(*args)
 
 
@@ -143,8 +159,19 @@
     return jax.ShapeDtypeStruct(dims, dtype)
 
 
+def token_ring(piece):
+    up = [(i, (i + 1) % NZ) for i in range(NZ)]
+    down = [(i, (i - 1) % NZ) for i in range(NZ)]
+    below, above = [piece], [piece]
+    for hop in range(NZ // 2):
+        below.append(lax.ppermute(below[-1], "z", up))
+        if hop < NZ // 2 - 1:
+            above.append(lax.ppermute(above[-1], "z", down))
+    return jnp.stack(above + below[:0:-1])
+
+
 def on_device(hidden_in, proj_weights, directions):
-    x, y, c = (lax.axis_index(name) for name in "xyc")
+    x, y, c, z = (lax.axis_index(name) for name in "xycz")
     swap = [(0, 1), (1, 0)]
 
     both = jnp.stack(
@@ -153,19 +180,25 @@
     kv_rows = jnp.transpose(both[1:], (1, 0, 2, 3, 4)).reshape(NC, 8, D)
     q_rows = both[0].reshape(NC, 4, D)
 
-    own = exchange(replicate(hidden_in, NZ), "z")
     kv_part = exchange(replicate(kv_rows, NX).reshape(NX * NC, 8, D), ("x", "c"))
+    kv_weight = lax.all_gather(kv_part.reshape(64, D), "y", axis=0, tiled=True)
+    own = token_ring(hidden_in)
+    other = lax.ppermute(own, "c", swap)
     q_part = exchange(replicate(q_rows, NY).reshape(NY * NC, 4, D), ("y", "c"))
-    kv_weight = lax.all_gather(kv_part.reshape(64, D), "y", axis=0, tiled=True)
     q_weight = exchange(replicate(q_part.reshape(64, D), NX), "x").reshape(256, D)
-    other = lax.ppermute(own, "c", swap)
-
-    query = project(query_kernel, own, other, q_weight, shape(2, 2, TOK, HD))
+
+    where = z.astype(jnp.int32).reshape(1)
+    query = project(
+        query_kernel, where, own, other, q_weight, column_order(1, True), shape(2, 2, TOK, HD)
+    )
+    kv_weight, query = lax.optimization_barrier((kv_weight, query))
     kv, state, total = project(
         key_value_kernel,
+        where,
         own,
         other,
         kv_weight,
+        column_order(2, False),
         (shape(2, 2, 2, TOK, HD), shape(2, 2, HD, HD, dtype=F32), shape(2, HD, HD)),
     )
 

time: 191 us -> 178 us (0.932)
  blocking collectives: 74.3 us -> 19.3 us
  starting transfers between devices: 26.4 us -> 56.2 us
  waiting for transfers between devices: 48.8 us -> 61.4 us
    all_to_all x2 -> x1, blocking collectives: 74.3 us -> 19.3 us  [exchange(): return lax.all_to_all(x, axes, 0, 0, tiled=True)]
    ppermute x0 -> x7, starting transfers between devices: none -> 24.4 us  [the longest x3 16.7 us: token_ring(): above.append(lax.ppermute(above[-1], 'z', down))]
    ppermute x0 -> x7, waiting for transfers between devices: none -> 13.9 us  [the longest x4 11.3 us: token_ring(): below.append(lax.ppermute(below[-1], 'z', up))]
    all_to_all x4, starting transfers between devices: 19.2 us -> 23.6 us  [exchange(): return lax.all_to_all(x, axes, 0, 0, tiled=True)]
    ppermute x1, starting transfers between devices: 2.4 us -> 5.05 us  [on_device(): mine, theirs = (out[0], lax.ppermute(out[1], 'c', swap))]
  transfers between devices with their start and end apart: 7 -> 14, of which waited for: 5 -> 7; matrix products, arithmetic and copies ran while one was open for 2% -> 3% of each run, Pallas kernels for 8% -> 4%
where the time goes in v2:
time: 178 us; the launch traced here: 177 us
  waiting for transfers between devices  61.4 us (34%)
  starting transfers between devices  56.2 us (32%)
  blocking collectives  19.3 us (11%)
  Pallas kernels  15.9 us (9%)
  between operations  13.8 us (8%)
  local copies, waits for them, and re-layouts  7.73 us (4%)
  other arithmetic  2.7 us (2%)
    all_to_all x4, waiting for transfers between devices, exchange(): return lax.all_to_all(x, axes, 0, 0, tiled=True)  46.5 us
    all_to_all x4, starting transfers between devices, exchange(): return lax.all_to_all(x, axes, 0, 0, tiled=True)  23.6 us
    all_to_all x1, blocking collectives, exchange(): return lax.all_to_all(x, axes, 0, 0, tiled=True)  19.3 us
    ppermute x3, starting transfers between devices, token_ring(): above.append(lax.ppermute(above[-1], 'z', down))  16.7 us
    pallas_call x2, Pallas kernels, project(): pl.pallas_call(kernel, grid_spec=pltpu.PrefetchScalarGridSpec(num_scalar_...  14.8 us
    ppermute x4, waiting for transfers between devices, token_ring(): below.append(lax.ppermute(below[-1], 'z', up))  11.3 us
    ppermute x4, starting transfers between devices, token_ring(): below.append(lax.ppermute(below[-1], 'z', up))  7.67 us
    ppermute x1, starting transfers between devices, on_device(): mine, theirs = (out[0], lax.ppermute(out[1], 'c', swap))  5.05 us
  transfers between devices with their start and end apart: 14, of which 7 were waited for; matrix products, arithmetic and copies ran while one was open for 3% of the time, Pallas kernels for 4%

profile of v2, /device:TPU:1, one launch (start us, length us, event | category | flops | bytes accessed | tf_op | source)
XLA Modules:
  0.0 177.0 jit_solution(11636809744303767402)
XLA Ops:
  6.5 1.1 fusion.3
  7.9 19.3 %all_to_all.25 = bf16[8,8,4096]{2,1,0:T(8,128)(2,1)} all-to-all(bf16[8,8,4096]{2,1,0:T(8,128)(2,1)S(1)} %bitcast.45), channel_id=1, replica_groups=mesh['x'=4,'y'=8,'c'=2,'z'=8] {'x','c'}, dimensions={0} | all-to-all | bytes 1048576 | tf_op jit(solution)/shard_map/all_to_all | solution.py:23
  27.3 6.4 %collective-permute-start = (bf16[256,512]{1,0:T(8,128)(2,1)S(1)}, bf16[256,512]{1,0:T(8,128)(2,1)}, u32[]{:S(2)}, u32[]{:S(2)}) collective-permute-start(bf16[256,512]{1,0:T(8,128)(2,1)S(1)} %copy-done.4), channel_id=1, source_target_pairs={{0,7},{1,0},{2,1},{3,2},{4,3},{5,4},{6,5},{7,6},{8,15},{9,8},{10,9... | collective-permute-start | bytes 786440 | tf_op jit(solution)/shard_map/ppermute | solution.py:169
  33.7 1.9 %collective-permute-start.3 = (bf16[256,512]{1,0:T(8,128)(2,1)S(1)}, bf16[256,512]{1,0:T(8,128)(2,1)S(1)}, u32[]{:S(2)}, u32[]{:S(2)}) collective-permute-start(bf16[256,512]{1,0:T(8,128)(2,1)S(1)} %copy-done.4), channel_id=1, source_target_pairs={{0,1},{1,2},{2,3},{3,4},{4,5},{5,6},{6,7},{7,0},{8,9},{9,10},{10,1... | collective-permute-start | bytes 786440 | tf_op jit(solution)/shard_map/ppermute | solution.py:167
  35.6 2.6 %collective-permute-done = bf16[256,512]{1,0:T(8,128)(2,1)} collective-permute-done((bf16[256,512]{1,0:T(8,128)(2,1)S(1)}, bf16[256,512]{1,0:T(8,128)(2,1)}, u32[]{:S(2)}, u32[]{:S(2)}) %collective-permute-start) | collective-permute-done | bytes 262176 | tf_op jit(solution)/shard_map/ppermute | solution.py:169
  38.2 5.4 %collective-permute-start.1 = (bf16[256,512]{1,0:T(8,128)(2,1)}, bf16[256,512]{1,0:T(8,128)(2,1)}, u32[]{:S(2)}, u32[]{:S(2)}) collective-permute-start(bf16[256,512]{1,0:T(8,128)(2,1)} %collective-permute-done), channel_id=1, source_target_pairs={{0,7},{1,0},{2,1},{3,2},{4,3},{5,4},{6,5},{7,6},{8,15},{9,8},{10,9... | collective-permute-start | bytes 786440 | tf_op jit(solution)/shard_map/ppermute | solution.py:169
  43.7 1.9 %collective-permute-start.4 = (bf16[256,512]{1,0:T(8,128)(2,1)S(1)}, bf16[256,512]{1,0:T(8,128)(2,1)S(1)}, u32[]{:S(2)}, u32[]{:S(2)}) collective-permute-start(bf16[256,512]{1,0:T(8,128)(2,1)S(1)} %collective-permute-done.3), channel_id=1, source_target_pairs={{0,1},{1,2},{2,3},{3,4},{4,5},{5,6},{6,7},{7,0},{8,9},{9,10},{10,1... | collective-permute-start | bytes 786440 | tf_op jit(solution)/shard_map/ppermute | solution.py:167
  45.9 1.0 broadcast_in_dim.34
  46.9 9.4 %all-to-all-start.1 = ((bf16[16,4,4096]{2,1,0:T(4,128)(2,1)}), bf16[16,4,4096]{2,1,0:T(4,128)(2,1)S(1)}, u32[]{:S(2)}, u32[]{:S(2)}) async-start(bf16[16,4,4096]{2,1,0:T(4,128)(2,1)} %bitcast.18), calls=%async_computation.1 | async-start | bytes 1048576 | tf_op jit(solution)/shard_map/all_to_all | solution.py:23
  56.2 1.9 %collective-permute-start.5 = (bf16[256,512]{1,0:T(8,128)(2,1)S(1)}, bf16[256,512]{1,0:T(8,128)(2,1)S(1)}, u32[]{:S(2)}, u32[]{:S(2)}) collective-permute-start(bf16[256,512]{1,0:T(8,128)(2,1)S(1)} %collective-permute-done.4), channel_id=1, source_target_pairs={{0,1},{1,2},{2,3},{3,4},{4,5},{5,6},{6,7},{7,0},{8,9},{9,10},{10,1... | collective-permute-start | bytes 786440 | tf_op jit(solution)/shard_map/ppermute | solution.py:167
  58.2 4.9 %collective-permute-start.2 = (bf16[256,512]{1,0:T(8,128)(2,1)}, bf16[256,512]{1,0:T(8,128)(2,1)S(1)}, u32[]{:S(2)}, u32[]{:S(2)}) collective-permute-start(bf16[256,512]{1,0:T(8,128)(2,1)} %collective-permute-done.1), channel_id=1, source_target_pairs={{0,7},{1,0},{2,1},{3,2},{4,3},{5,4},{6,5},{7,6},{8,15},{9,8},{10,9... | collective-permute-start | bytes 786440 | tf_op jit(solution)/shard_map/ppermute | solution.py:169
  63.1 1.0 bitcast_dynamic-update-slice_fusion.6
  64.1 3.7 %collective-permute-done.5 = bf16[256,512]{1,0:T(8,128)(2,1)S(1)} collective-permute-done((bf16[256,512]{1,0:T(8,128)(2,1)S(1)}, bf16[256,512]{1,0:T(8,128)(2,1)S(1)}, u32[]{:S(2)}, u32[]{:S(2)}) %collective-permute-start.5) | collective-permute-done | bytes 262176 | tf_op jit(solution)/shard_map/ppermute | solution.py:167
  67.8 1.9 %collective-permute-start.6 = (bf16[256,512]{1,0:T(8,128)(2,1)S(1)}, bf16[256,512]{1,0:T(8,128)(2,1)S(1)}, u32[]{:S(2)}, u32[]{:S(2)}) collective-permute-start(bf16[256,512]{1,0:T(8,128)(2,1)S(1)} %collective-permute-done.5), channel_id=1, source_target_pairs={{0,1},{1,2},{2,3},{3,4},{4,5},{5,6},{6,7},{7,0},{8,9},{9,10},{10,1... | collective-permute-start | bytes 786440 | tf_op jit(solution)/shard_map/ppermute | solution.py:167
  69.7 1.0 bitcast_dynamic-update-slice_fusion.5
  70.7 7.6 %collective-permute-done.6 = bf16[256,512]{1,0:T(8,128)(2,1)S(1)} collective-permute-done((bf16[256,512]{1,0:T(8,128)(2,1)S(1)}, bf16[256,512]{1,0:T(8,128)(2,1)S(1)}, u32[]{:S(2)}, u32[]{:S(2)}) %collective-permute-start.6) | collective-permute-done | bytes 262176 | tf_op jit(solution)/shard_map/ppermute | solution.py:167
  78.4 3.2 %collective-permute-start.7 = (bf16[8,256,512]{2,1,0:T(8,128)(2,1)S(1)}, bf16[8,256,512]{2,1,0:T(8,128)(2,1)}, u32[]{:S(2)}, u32[]{:S(2)}) collective-permute-start(bf16[8,256,512]{2,1,0:T(8,128)(2,1)S(1)} %bitcast_dynamic-update-slice_fusion.own_ref), channel_id=1, source_target_pairs={{0,8},{8,0},{1,9},{9,1},{2,10},{10,2},{3,11},{11,3},{4,12},{12,4},... | collective-permute-start | bytes 6291464 | tf_op jit(solution)/shard_map/ppermute | solution.py:186
  81.7 1.6 broadcast_in_dim.36
  83.4 4.5 %all-to-all-start.2 = ((bf16[4,64,4096]{2,1,0:T(8,128)(2,1)}), bf16[4,64,4096]{2,1,0:T(8,128)(2,1)}, u32[]{:S(2)}, u32[]{:S(2)}) async-start(bf16[4,64,4096]{2,1,0:T(8,128)(2,1)} %broadcast_in_dim.36), calls=%async_computation.2 | async-start | bytes 4194304 | tf_op jit(solution)/shard_map/all_to_all | solution.py:23
  88.2 26.2 %all-to-all-done.2 = bf16[4,64,4096]{2,1,0:T(8,128)(2,1)} async-done(((bf16[4,64,4096]{2,1,0:T(8,128)(2,1)}), bf16[4,64,4096]{2,1,0:T(8,128)(2,1)}, u32[]{:S(2)}, u32[]{:S(2)}) %all-to-all-start.2) | async-done | bytes 2097184 | tf_op jit(solution)/shard_map/all_to_all | solution.py:23
  114.4 6.5 %shard_map.37.query_ref = bf16[2,2,256,128]{3,2,1,0:T(8,128)(2,1)S(1)} custom-call(s32[1]{0:T(128)} %bitcast.8.z_ref, bf16[8,256,512]{2,1,0:T(8,128)(2,1)S(1)} %bitcast_dynamic-update-slice_fusion.own_ref, bf16[8,256,512]{2,1,0:T(8,128)(2,1)} %collective-permute-done.7.other_ref, bf16[256,4096]{1,0:T(8,128)(2,1)} %bitcast.19.weight_ref, ...), custom_call_target="tpu_custom_call" | custom-call | tf_op jit(solution)/shard_map/pallas_call | solution.py:101
  120.9 8.4 %shard_map.38 = (bf16[2,2,2,256,128]{4,3,2,1,0:T(8,128)(2,1)S(1)}, f32[2,2,128,128]{3,2,1,0:T(8,128)S(1)}, bf16[2,128,128]{2,1,0:T(8,128)(2,1)S(1)}) custom-call(s32[1]{0:T(128)} %bitcast.8.z_ref, bf16[8,256,512]{2,1,0:T(8,128)(2,1)S(1)} %bitcast_dynamic-update-slice_fusion.own_ref, bf16[8,256,512]{2,1,0:T(8,128)(2,1)} %collective-permute-done.7.other_ref, ...), custom_call_target="tpu_custom_call" | custom-call | tf_op jit(solution)/shard_map/pallas_call | solution.py:101
  129.3 0.8 copy-done
  130.1 0.7 broadcast_in_dim.37
  130.8 3.4 %all-to-all-start.3 = ((bf16[4,2,128,128]{3,2,1,0:T(8,128)(2,1)}), bf16[4,2,128,128]{3,2,1,0:T(8,128)(2,1)S(1)}, u32[]{:S(2)}, u32[]{:S(2)}) async-start(bf16[4,2,128,128]{3,2,1,0:T(8,128)(2,1)} %broadcast_in_dim.37), calls=%async_computation.3 | async-start | bytes 524288 | tf_op jit(solution)/shard_map/all_to_all | solution.py:23
  134.3 5.6 %all-to-all-done.3 = bf16[4,2,128,128]{3,2,1,0:T(8,128)(2,1)S(1)} async-done(((bf16[4,2,128,128]{3,2,1,0:T(8,128)(2,1)}), bf16[4,2,128,128]{3,2,1,0:T(8,128)(2,1)S(1)}, u32[]{:S(2)}, u32[]{:S(2)}) %all-to-all-start.3) | async-done | bytes 262176 | tf_op jit(solution)/shard_map/all_to_all | solution.py:23
  140.0 1.0 add_convert_fusion
  141.0 6.4 %all-to-all-start.4 = ((bf16[8,2,128,128]{3,2,1,0:T(8,128)(2,1)}), bf16[8,2,128,128]{3,2,1,0:T(8,128)(2,1)S(1)}, u32[]{:S(2)}, u32[]{:S(2)}) async-start(bf16[8,2,128,128]{3,2,1,0:T(8,128)(2,1)} %add_convert_fusion), calls=%async_computation.4 | async-start | bytes 1048576 | tf_op jit(solution)/shard_map/all_to_all | solution.py:23
  148.0 14.6 %all-to-all-done.4.partial_ref = bf16[8,2,128,128]{3,2,1,0:T(8,128)(2,1)S(1)} async-done(((bf16[8,2,128,128]{3,2,1,0:T(8,128)(2,1)}), bf16[8,2,128,128]{3,2,1,0:T(8,128)(2,1)S(1)}, u32[]{:S(2)}, u32[]{:S(2)}) %all-to-all-start.4) | async-done | bytes 524320 | tf_op jit(solution)/shard_map/all_to_all | solution.py:23
  163.1 5.1 %collective-permute-start.8 = (bf16[2,256,128]{2,1,0:T(8,128)(2,1)S(1)}, bf16[2,256,128]{2,1,0:T(8,128)(2,1)S(1)}, u32[]{:S(2)}, u32[]{:S(2)}) collective-permute-start(bf16[2,256,128]{2,1,0:T(8,128)(2,1)S(1)} %slice_bitcast_fusion), channel_id=1, source_target_pairs={{0,8},{8,0},{1,9},{9,1},{2,10},{10,2},{3,11},{11,3},{4,12},{12,4},... | collective-permute-start | bytes 393224 | tf_op jit(solution)/shard_map/ppermute | solution.py:214
  168.2 1.0 collective-permute-done.8
  169.2 1.0 copy.14
  (44 shorter events, 2.3 us)
Async XLA Ops:
  6.5 39.1 %copy-start.3 = (bf16[3,4096,2,2]{1,3,2,0:T(2,128)(2,1)S(1)}, bf16[3,4096,2,2]{1,3,2,0:T(2,128)(2,1)}, u32[]{:S(2)}) copy-start(bf16[3,4096,2,2]{1,3,2,0:T(2,128)(2,1)} %param.4) | copy-start | bytes 294916
  6.5 39.1 %copy-start.2 = (bf16[3,4096,2,2]{1,3,2,0:T(2,128)(2,1)S(1)}, bf16[3,4096,2,2]{1,3,2,0:T(2,128)(2,1)}, u32[]{:S(2)}) copy-start(bf16[3,4096,2,2]{1,3,2,0:T(2,128)(2,1)} %param.5) | copy-start | bytes 294916
  6.5 20.7 %copy-start.4 = (bf16[256,512]{1,0:T(8,128)(2,1)S(1)}, bf16[256,512]{1,0:T(8,128)(2,1)}, u32[]{:S(2)}) copy-start(bf16[256,512]{1,0:T(8,128)(2,1)} %param.3) | copy-start | bytes 786436
  6.5 114.4 %all-gather.2.cloned.1.call-start = ((), (), s32[]{:S(2)}) async-start(), calls=%async_computation.5 | async-start | bytes 4718592 | tf_op jit(solution)/shard_map/all_gather | solution.py:184
  27.3 11.0 %collective-permute-start = (bf16[256,512]{1,0:T(8,128)(2,1)S(1)}, bf16[256,512]{1,0:T(8,128)(2,1)}, u32[]{:S(2)}, u32[]{:S(2)}) collective-permute-start(bf16[256,512]{1,0:T(8,128)(2,1)S(1)} %copy-done.4), channel_id=1, source_target_pairs={{0,7},{1,0},{2,1},{3,2},{4,3},{5,4},{6,5},{7,6},{8,15},{9,8},{10,9... | collective-permute-start | bytes 786440 | tf_op jit(solution)/shard_map/ppermute | solution.py:169
  33.7 10.0 %collective-permute-start.3 = (bf16[256,512]{1,0:T(8,128)(2,1)S(1)}, bf16[256,512]{1,0:T(8,128)(2,1)S(1)}, u32[]{:S(2)}, u32[]{:S(2)}) collective-permute-start(bf16[256,512]{1,0:T(8,128)(2,1)S(1)} %copy-done.4), channel_id=1, source_target_pairs={{0,1},{1,2},{2,3},{3,4},{4,5},{5,6},{6,7},{7,0},{8,9},{9,10},{10,1... | collective-permute-start | bytes 786440 | tf_op jit(solution)/shard_map/ppermute | solution.py:167
  38.2 20.0 %collective-permute-start.1 = (bf16[256,512]{1,0:T(8,128)(2,1)}, bf16[256,512]{1,0:T(8,128)(2,1)}, u32[]{:S(2)}, u32[]{:S(2)}) collective-permute-start(bf16[256,512]{1,0:T(8,128)(2,1)} %collective-permute-done), channel_id=1, source_target_pairs={{0,7},{1,0},{2,1},{3,2},{4,3},{5,4},{6,5},{7,6},{8,15},{9,8},{10,9... | collective-permute-start | bytes 786440 | tf_op jit(solution)/shard_map/ppermute | solution.py:169
  43.7 12.6 %collective-permute-start.4 = (bf16[256,512]{1,0:T(8,128)(2,1)S(1)}, bf16[256,512]{1,0:T(8,128)(2,1)S(1)}, u32[]{:S(2)}, u32[]{:S(2)}) collective-permute-start(bf16[256,512]{1,0:T(8,128)(2,1)S(1)} %collective-permute-done.3), channel_id=1, source_target_pairs={{0,1},{1,2},{2,3},{3,4},{4,5},{5,6},{6,7},{7,0},{8,9},{9,10},{10,1... | collective-permute-start | bytes 786440 | tf_op jit(solution)/shard_map/ppermute | solution.py:167
  46.9 34.7 %all-to-all-start.1 = ((bf16[16,4,4096]{2,1,0:T(4,128)(2,1)}), bf16[16,4,4096]{2,1,0:T(4,128)(2,1)S(1)}, u32[]{:S(2)}, u32[]{:S(2)}) async-start(bf16[16,4,4096]{2,1,0:T(4,128)(2,1)} %bitcast.18), calls=%async_computation.1 | async-start | bytes 1048576 | tf_op jit(solution)/shard_map/all_to_all | solution.py:23
  56.2 11.5 %collective-permute-start.5 = (bf16[256,512]{1,0:T(8,128)(2,1)S(1)}, bf16[256,512]{1,0:T(8,128)(2,1)S(1)}, u32[]{:S(2)}, u32[]{:S(2)}) collective-permute-start(bf16[256,512]{1,0:T(8,128)(2,1)S(1)} %collective-permute-done.4), channel_id=1, source_target_pairs={{0,1},{1,2},{2,3},{3,4},{4,5},{5,6},{6,7},{7,0},{8,9},{9,10},{10,1... | collective-permute-start | bytes 786440 | tf_op jit(solution)/shard_map/ppermute | solution.py:167
  58.2 12.5 %collective-permute-start.2 = (bf16[256,512]{1,0:T(8,128)(2,1)}, bf16[256,512]{1,0:T(8,128)(2,1)S(1)}, u32[]{:S(2)}, u32[]{:S(2)}) collective-permute-start(bf16[256,512]{1,0:T(8,128)(2,1)} %collective-permute-done.1), channel_id=1, source_target_pairs={{0,7},{1,0},{2,1},{3,2},{4,3},{5,4},{6,5},{7,6},{8,15},{9,8},{10,9... | collective-permute-start | bytes 786440 | tf_op jit(solution)/shard_map/ppermute | solution.py:169
  67.8 10.5 %collective-permute-start.6 = (bf16[256,512]{1,0:T(8,128)(2,1)S(1)}, bf16[256,512]{1,0:T(8,128)(2,1)S(1)}, u32[]{:S(2)}, u32[]{:S(2)}) collective-permute-start(bf16[256,512]{1,0:T(8,128)(2,1)S(1)} %collective-permute-done.5), channel_id=1, source_target_pairs={{0,1},{1,2},{2,3},{3,4},{4,5},{5,6},{6,7},{7,0},{8,9},{9,10},{10,1... | collective-permute-start | bytes 786440 | tf_op jit(solution)/shard_map/ppermute | solution.py:167
  78.4 36.0 %collective-permute-start.7 = (bf16[8,256,512]{2,1,0:T(8,128)(2,1)S(1)}, bf16[8,256,512]{2,1,0:T(8,128)(2,1)}, u32[]{:S(2)}, u32[]{:S(2)}) collective-permute-start(bf16[8,256,512]{2,1,0:T(8,128)(2,1)S(1)} %bitcast_dynamic-update-slice_fusion.own_ref), channel_id=1, source_target_pairs={{0,8},{8,0},{1,9},{9,1},{2,10},{10,2},{3,11},{11,3},{4,12},{12,4},... | collective-permute-start | bytes 6291464 | tf_op jit(solution)/shard_map/ppermute | solution.py:186
  83.4 31.0 %all-to-all-start.2 = ((bf16[4,64,4096]{2,1,0:T(8,128)(2,1)}), bf16[4,64,4096]{2,1,0:T(8,128)(2,1)}, u32[]{:S(2)}, u32[]{:S(2)}) async-start(bf16[4,64,4096]{2,1,0:T(8,128)(2,1)} %broadcast_in_dim.36), calls=%async_computation.2 | async-start | bytes 4194304 | tf_op jit(solution)/shard_map/all_to_all | solution.py:23
  129.3 0.8 copy-start
  130.1 17.3 %copy-start.1 = (bf16[2,2,2,256,128]{4,3,2,1,0:T(8,128)(2,1)S(1)}, bf16[2,2,2,256,128]{4,3,2,1,0:T(8,128)(2,1)}, u32[]{:S(2)}) copy-start(bf16[2,2,2,256,128]{4,3,2,1,0:T(8,128)(2,1)} %copy-done) | copy-start | bytes 1572868
  130.8 9.0 %all-to-all-start.3 = ((bf16[4,2,128,128]{3,2,1,0:T(8,128)(2,1)}), bf16[4,2,128,128]{3,2,1,0:T(8,128)(2,1)S(1)}, u32[]{:S(2)}, u32[]{:S(2)}) async-start(bf16[4,2,128,128]{3,2,1,0:T(8,128)(2,1)} %broadcast_in_dim.37), calls=%async_computation.3 | async-start | bytes 524288 | tf_op jit(solution)/shard_map/all_to_all | solution.py:23
  141.0 21.7 %all-to-all-start.4 = ((bf16[8,2,128,128]{3,2,1,0:T(8,128)(2,1)}), bf16[8,2,128,128]{3,2,1,0:T(8,128)(2,1)S(1)}, u32[]{:S(2)}, u32[]{:S(2)}) async-start(bf16[8,2,128,128]{3,2,1,0:T(8,128)(2,1)} %add_convert_fusion), calls=%async_computation.4 | async-start | bytes 1048576 | tf_op jit(solution)/shard_map/all_to_all | solution.py:23
  163.1 6.0 %collective-permute-start.8 = (bf16[2,256,128]{2,1,0:T(8,128)(2,1)S(1)}, bf16[2,256,128]{2,1,0:T(8,128)(2,1)S(1)}, u32[]{:S(2)}, u32[]{:S(2)}) collective-permute-start(bf16[2,256,128]{2,1,0:T(8,128)(2,1)S(1)} %slice_bitcast_fusion), channel_id=1, source_target_pairs={{0,8},{8,0},{1,9},{9,1},{2,10},{10,2},{3,11},{11,3},{4,12},{12,4},... | collective-permute-start | bytes 393224 | tf_op jit(solution)/shard_map/ppermute | solution.py:214
Sparse Core Ops, SparseCore 0:
  27.4 67.2 all-gather.1

commit v3 on v2

v3 whole, which is shorter than its diff:
```python
import functools

import jax
import jax.numpy as jnp
from jax import lax
from jax.experimental import pallas as pl
from jax.experimental.pallas import tpu as pltpu
from jax.sharding import Mesh
from jax.sharding import PartitionSpec as P

NX, NY, NC, NZ = 4, 8, 2, 8
TOK, HD, PIECE = 256, 128, 512
D = NZ * PIECE
STEP = 0.1 * D ** (-0.5)
F32, BF16 = jnp.float32, jnp.bfloat16


def replicate(x, n):
    return jnp.broadcast_to(x[None], (n,) + x.shape)


def exchange(x, axes):
    return lax.all_to_all(x, axes, 0, 0, tiled=True)


def column_order(kinds, first_x=None):
    cols = kinds * 2 * HD
    row = lax.broadcasted_iota(jnp.int32, (cols, cols), 0)
    col = lax.broadcasted_iota(jnp.int32, (cols, cols), 1)
    j = row & 1
    sign = (row >> 1) & 1
    kind = (row >> 2) & (kinds - 1)
    rest = row >> (2 + (kinds - 1))
    core = rest & 1
    chip = rest >> 1
    if first_x is None:
        chip = (chip & (NX - 1)) * NY + (chip >> 2)
    else:
        chip = (chip + first_x * NY) & (NX * NY - 1)
    target = (kind * 2 + sign) * HD + (chip * 2 + core) * 2 + j
    return (col == target).astype(BF16)


def signs_and_order(acc, order):
    cols = acc.shape[1]
    lane = lax.broadcasted_iota(jnp.int32, acc.shape, 1)
    left = pltpu.roll(acc, cols - 2, 1)
    right = pltpu.roll(acc, 2, 1)
    step = jnp.float32(STEP)
    signed = jnp.where((lane & 3) < 2, acc + step * left, right + (-step) * acc).astype(BF16)
    return jnp.dot(signed, order, preferred_element_type=F32).astype(BF16)


NT = (((1,), (1,)), ((), ()))
TN = (((0,), (0,)), ((), ()))


CHUNKS = 4
PER = NZ // CHUNKS


def multiply(z_ref, own_ref, other_ref, weight_hbm, weight, acc, sem):
    copies = []
    for k in range(NZ):
        start = pl.multiple_of(((z_ref[0] + k) & (NZ - 1)) * PIECE, PIECE)
        copies.append(
            pltpu.make_async_copy(
                weight_hbm.at[:, pl.ds(start, PIECE)],
                weight.at[k // PER, :, pl.ds((k % PER) * PIECE, PIECE)],
                sem.at[k],
            )
        )
    for copy in copies:
        copy.start()
    for k in range(CHUNKS):
        pieces = range(k * PER, (k + 1) * PER)
        for i in pieces:
            copies[i].wait()
        tokens = jnp.concatenate(
            [jnp.concatenate([ref[i] for i in pieces], 1) for ref in (own_ref, other_ref)], 0
        )
        part = lax.dot_general(tokens, weight[k], NT, preferred_element_type=F32)
        if k == 0:
            acc[...] = part
        else:
            acc[...] += part


def query_kernel(z_ref, own_ref, other_ref, weight_hbm, order_ref, out_ref, weight, acc, sem):
    multiply(z_ref, own_ref, other_ref, weight_hbm, weight, acc, sem)
    rows = signs_and_order(acc[...], order_ref[...])
    for block in range(2):
        for s in range(2):
            out_ref[block, s] = rows[block * TOK : (block + 1) * TOK, s * HD : (s + 1) * HD]


def key_value_kernel(
    z_ref, own_ref, other_ref, weight_hbm, order_ref, out_ref, state_ref, total_ref, weight, acc, sem
):
    multiply(z_ref, own_ref, other_ref, weight_hbm, weight, acc, sem)
    rows = signs_and_order(acc[...], order_ref[...])
    for s in range(2):
        for block in range(2):
            part = rows[block * TOK : (block + 1) * TOK]
            key = part[:, s * HD : (s + 1) * HD]
            value = part[:, (2 + s) * HD : (3 + s) * HD]
            out_ref[0, block, s] = key
            out_ref[1, block, s] = value
            state_ref[block, s] = lax.dot_general(key, value, TN, preferred_element_type=F32)
        total = (state_ref[0, s] + state_ref[1, s]).reshape(NX * NY // 2, 8, HD)
        total_ref[s * NX * NY // 2 : (s + 1) * NX * NY // 2] = total.astype(BF16)


def project(kernel, z, own, other, weight, order, out_shape):
    rows = weight.shape[0]
    vmem = pl.BlockSpec(memory_space=pltpu.VMEM)
    return pl.pallas_call(
        kernel,
        in_specs=[
            pl.BlockSpec(memory_space=pltpu.SMEM),
            vmem,
            vmem,
            pl.BlockSpec(memory_space=pltpu.HBM),
            vmem,
        ],
        out_specs=jax.tree.map(lambda s: vmem, out_shape),
        scratch_shapes=[
            pltpu.VMEM((CHUNKS, rows, PER * PIECE), BF16),
            pltpu.VMEM((2 * TOK, rows), F32),
            pltpu.SemaphoreType.DMA((NZ,)),
        ],
        out_shape=out_shape,
        compiler_params=pltpu.CompilerParams(vmem_limit_bytes=24 << 20),
    )(z, own, other, pltpu.with_memory_space_constraint(weight, pltpu.HBM), order)


def prefix_kernel(total_ref, out_ref):
    run = jnp.zeros(total_ref.shape[1:], F32)
    for chip in range(NX * NY):
        out_ref[chip] = run.astype(BF16)
        run = run + total_ref[chip].astype(F32)


def inner_kernel(query_ref, kv_ref, out_ref):
    row = lax.broadcasted_iota(jnp.int32, (TOK, TOK), 0)
    col = lax.broadcasted_iota(jnp.int32, (TOK, TOK), 1)
    for block in range(2):
        for s in range(2):
            scores = lax.dot_general(
                query_ref[block, s], kv_ref[0, block, s], NT, preferred_element_type=F32
            )
            weights = jnp.where(col <= row, scores, 0.0).astype(BF16)
            out_ref[block, s] = jnp.dot(weights, kv_ref[1, block, s], preferred_element_type=F32)


def cross_kernel(query_ref, inner_ref, state_ref, prior_ref, out_ref):
    core = lax.axis_index("c")
    prior = prior_ref[...].astype(F32).reshape(2, HD, HD)
    for block in range(2):
        later = jnp.where(core == (1 - block), jnp.float32(1.0), jnp.float32(0.0))
        for s in range(2):
            carried = (prior[s] + later * state_ref[1 - block, s]).astype(BF16)
            combined = inner_ref[block, s] + jnp.dot(
                query_ref[block, s], carried, preferred_element_type=F32
            )
            scale = lax.rsqrt(jnp.mean(combined * combined, axis=-1, keepdims=True) + 1e-05)
            out_ref[block, s] = (combined * scale).astype(BF16)


def call(kernel, out_shape, *args):
    return pl.pallas_call(
        kernel,
        out_shape=out_shape,
        in_specs=[pl.BlockSpec(memory_space=pltpu.VMEM)] * len(args),
        out_specs=pl.BlockSpec(memory_space=pltpu.VMEM),
        compiler_params=pltpu.CompilerParams(vmem_limit_bytes=12 << 20),
    )(*args)


def shape(*dims, dtype=BF16):
    return jax.ShapeDtypeStruct(dims, dtype)


def token_ring(piece):
    up = [(i, (i + 1) % NZ) for i in range(NZ)]
    down = [(i, (i - 1) % NZ) for i in range(NZ)]
    below, above = [piece], [piece]
    for hop in range(NZ // 2):
        below.append(lax.ppermute(below[-1], "z", up))
        if hop < NZ // 2 - 1:
            above.append(lax.ppermute(above[-1], "z", down))
    return jnp.stack(above + below[:0:-1])


def on_device(hidden_in, proj_weights, directions):
    x, c, z = (lax.axis_index(name) for name in "xcz")
    swap = [(0, 1), (1, 0)]

    both = jnp.stack(
        [jnp.transpose(proj_weights, (0, 2, 3, 1)), jnp.transpose(directions, (0, 2, 3, 1))], axis=2
    )
    kv_rows = jnp.transpose(both[1:], (1, 0, 2, 3, 4)).reshape(NC, 8, D)
    q_rows = both[0].reshape(NC, 4, D)

    kv_part = exchange(replicate(kv_rows, NX).reshape(NX * NC, 8, D), ("x", "c"))
    kv_weight = lax.all_gather(kv_part.reshape(64, D), "y", axis=0, tiled=True)
    own = token_ring(hidden_in)
    other = lax.ppermute(own, "c", swap)
    q_part = exchange(replicate(q_rows, NY).reshape(NY * NC, 4, D), ("y", "c"))
    q_mine = q_part.reshape(64, D)
    q_weight = jnp.concatenate(
        [q_mine] + [lax.ppermute(q_mine, "x", [(i, (i - k) % NX) for i in range(NX)]) for k in (1, 2, 3)]
    )

    where = z.astype(jnp.int32).reshape(1)
    query = project(
        query_kernel, where, own, other, q_weight, column_order(1, x), shape(2, 2, TOK, HD)
    )
    kv, state, total = project(
        key_value_kernel,
        where,
        own,
        other,
        kv_weight,
        column_order(2),
        (shape(2, 2, 2, TOK, HD), shape(2, 2, HD, HD, dtype=F32), shape(NX * NY, 8, HD)),
    )

    slices = call(prefix_kernel, shape(NX * NY, 8, HD), exchange(total, ("x", "y")))
    prior = exchange(slices, ("x", "y"))

    inner = call(inner_kernel, shape(2, 2, TOK, HD, dtype=F32), query, kv)
    out = call(cross_kernel, shape(2, 2, TOK, HD), query, inner, state, prior)
    mine, theirs = out[0], lax.ppermute(out[1], "c", swap)
    first = jnp.where(c == 0, mine, theirs)
    second = jnp.where(c == 0, theirs, mine)
    return jnp.stack([first, second], axis=2)


def solution(mesh):
    mesh4 = Mesh(mesh.devices.reshape(NX, NY, NC, NZ), ("x", "y", "c", "z"))
    ctx = ("x", "y", "c")
    return jax.shard_map(
        on_device,
        mesh=mesh4,
        in_specs=(P(ctx, "z"), P(None, None, "z", ctx), P(None, None, "z", ctx)),
        out_specs=P(None, ctx, "z", None),
        check_vma=False,
    )
```

time: 178 us -> 159 us (0.89)
  waiting for transfers between devices: 61.4 us -> 42.7 us
  local copies, waits for them, and re-layouts: 7.73 us -> 3.45 us
  starting transfers between devices: 56.2 us -> 59.5 us
  other arithmetic: 2.7 us -> 4.6 us
    all_to_all x4 -> x3, waiting for transfers between devices: 46.5 us -> 26.3 us  [exchange(): return lax.all_to_all(x, axes, 0, 0, tiled=True)]
    ppermute x0 -> x3, starting transfers between devices: none -> 8.66 us  [on_device(): lax.ppermute(q_mine, 'x', [(i, (i - k) % NX) for i in range(NX)])]
    all_to_all x4 -> x3, starting transfers between devices: 23.6 us -> 17.4 us  [exchange(): return lax.all_to_all(x, axes, 0, 0, tiled=True)]
    ppermute x4, waiting for transfers between devices: 11.3 us -> 15.4 us  [token_ring(): below.append(lax.ppermute(below[-1], 'z', up))]
    concatenate x0 -> x1, other arithmetic: none -> 3.07 us  [on_device(): jnp.concatenate([q_mine] + [lax.ppermute(q_mine, 'x', [(i, (i - k) % NX)...]
    unnamed x17 -> x13, local copies, waits for them, and re-layouts: 2.85 us -> 0.15 us
    ppermute x1, starting transfers between devices: 3.24 us -> 5.87 us  [on_device(): other = lax.ppermute(own, 'c', swap)]
    ppermute x3, waiting for transfers between devices: 2.61 us -> 0.01 us  [token_ring(): above.append(lax.ppermute(above[-1], 'z', down))]
  transfers between devices with their start and end apart: 14 -> 16, of which waited for: 7 -> 7; matrix products, arithmetic and copies ran while one was open for 3% -> 4% of each run, Pallas kernels for 4% -> 9%
where the time goes in v3:
time: 159 us; the launch traced here: 158 us
  starting transfers between devices  59.5 us (37%)
  waiting for transfers between devices  42.7 us (27%)
  blocking collectives  19.3 us (12%)
  Pallas kernels  14.3 us (9%)
  between operations  13.8 us (9%)
  other arithmetic  4.6 us (3%)
  local copies, waits for them, and re-layouts  3.45 us (2%)
    all_to_all x3, waiting for transfers between devices, exchange(): return lax.all_to_all(x, axes, 0, 0, tiled=True)  26.3 us
    all_to_all x1, blocking collectives, exchange(): return lax.all_to_all(x, axes, 0, 0, tiled=True)  19.3 us
    all_to_all x3, starting transfers between devices, exchange(): return lax.all_to_all(x, axes, 0, 0, tiled=True)  17.4 us
    ppermute x3, starting transfers between devices, token_ring(): above.append(lax.ppermute(above[-1], 'z', down))  15.6 us
    ppermute x4, waiting for transfers between devices, token_ring(): below.append(lax.ppermute(below[-1], 'z', up))  15.4 us
    pallas_call x2, Pallas kernels, project(): pl.pallas_call(kernel, in_specs=[pl.BlockSpec(memory_space=pltpu.SMEM), v...  12.6 us
    ppermute x3, starting transfers between devices, on_device(): lax.ppermute(q_mine, 'x', [(i, (i - k) % NX) for i in range(NX)])  8.66 us
    ppermute x4, starting transfers between devices, token_ring(): below.append(lax.ppermute(below[-1], 'z', up))  7.78 us
  transfers between devices with their start and end apart: 16, of which 7 were waited for; matrix products, arithmetic and copies ran while one was open for 4% of the time, Pallas kernels for 9%

profile of v3, /device:TPU:1, one launch (start us, length us, event | category | flops | bytes accessed | tf_op | source)
XLA Modules:
  0.0 157.7 jit_solution(10505164357121908292)
XLA Ops:
  6.5 1.1 fusion.2
  7.9 19.3 %all_to_all.20 = bf16[8,8,4096]{2,1,0:T(8,128)(2,1)} all-to-all(bf16[8,8,4096]{2,1,0:T(8,128)(2,1)S(1)} %bitcast.42), channel_id=1, replica_groups=mesh['x'=4,'y'=8,'c'=2,'z'=8] {'x','c'}, dimensions={0} | all-to-all | bytes 1048576 | tf_op jit(solution)/shard_map/all_to_all | solution.py:23
  27.3 2.1 %collective-permute-start.3 = (bf16[256,512]{1,0:T(8,128)(2,1)S(1)}, bf16[256,512]{1,0:T(8,128)(2,1)S(1)}, u32[]{:S(2)}, u32[]{:S(2)}) collective-permute-start(bf16[256,512]{1,0:T(8,128)(2,1)S(1)} %copy-done.2), channel_id=1, source_target_pairs={{0,1},{1,2},{2,3},{3,4},{4,5},{5,6},{6,7},{7,0},{8,9},{9,10},{10,1... | collective-permute-start | bytes 786440 | tf_op jit(solution)/shard_map/ppermute | solution.py:189
  29.4 6.4 %collective-permute-start = (bf16[256,512]{1,0:T(8,128)(2,1)S(1)}, bf16[256,512]{1,0:T(8,128)(2,1)S(1)}, u32[]{:S(2)}, u32[]{:S(2)}) collective-permute-start(bf16[256,512]{1,0:T(8,128)(2,1)S(1)} %copy-done.2), channel_id=1, source_target_pairs={{0,7},{1,0},{2,1},{3,2},{4,3},{5,4},{6,5},{7,6},{8,15},{9,8},{10,9... | collective-permute-start | bytes 786440 | tf_op jit(solution)/shard_map/ppermute | solution.py:191
  35.8 3.7 %collective-permute-done.3 = bf16[256,512]{1,0:T(8,128)(2,1)S(1)} collective-permute-done((bf16[256,512]{1,0:T(8,128)(2,1)S(1)}, bf16[256,512]{1,0:T(8,128)(2,1)S(1)}, u32[]{:S(2)}, u32[]{:S(2)}) %collective-permute-start.3) | collective-permute-done | bytes 262176 | tf_op jit(solution)/shard_map/ppermute | solution.py:189
  39.5 1.9 %collective-permute-start.4 = (bf16[256,512]{1,0:T(8,128)(2,1)S(1)}, bf16[256,512]{1,0:T(8,128)(2,1)S(1)}, u32[]{:S(2)}, u32[]{:S(2)}) collective-permute-start(bf16[256,512]{1,0:T(8,128)(2,1)S(1)} %collective-permute-done.3), channel_id=1, source_target_pairs={{0,1},{1,2},{2,3},{3,4},{4,5},{5,6},{6,7},{7,0},{8,9},{9,10},{10,1... | collective-permute-start | bytes 786440 | tf_op jit(solution)/shard_map/ppermute | solution.py:189
  41.4 4.6 %collective-permute-start.1 = (bf16[256,512]{1,0:T(8,128)(2,1)S(1)}, bf16[256,512]{1,0:T(8,128)(2,1)S(1)}, u32[]{:S(2)}, u32[]{:S(2)}) collective-permute-start(bf16[256,512]{1,0:T(8,128)(2,1)S(1)} %collective-permute-done), channel_id=1, source_target_pairs={{0,7},{1,0},{2,1},{3,2},{4,3},{5,4},{6,5},{7,6},{8,15},{9,8},{10,9... | collective-permute-start | bytes 786440 | tf_op jit(solution)/shard_map/ppermute | solution.py:191
  46.0 2.8 %collective-permute-done.4 = bf16[256,512]{1,0:T(8,128)(2,1)S(1)} collective-permute-done((bf16[256,512]{1,0:T(8,128)(2,1)S(1)}, bf16[256,512]{1,0:T(8,128)(2,1)S(1)}, u32[]{:S(2)}, u32[]{:S(2)}) %collective-permute-start.4) | collective-permute-done | bytes 262176 | tf_op jit(solution)/shard_map/ppermute | solution.py:189
  48.8 1.9 %collective-permute-start.5 = (bf16[256,512]{1,0:T(8,128)(2,1)S(1)}, bf16[256,512]{1,0:T(8,128)(2,1)S(1)}, u32[]{:S(2)}, u32[]{:S(2)}) collective-permute-start(bf16[256,512]{1,0:T(8,128)(2,1)S(1)} %collective-permute-done.4), channel_id=1, source_target_pairs={{0,1},{1,2},{2,3},{3,4},{4,5},{5,6},{6,7},{7,0},{8,9},{9,10},{10,1... | collective-permute-start | bytes 786440 | tf_op jit(solution)/shard_map/ppermute | solution.py:189
  50.8 4.6 %collective-permute-start.2 = (bf16[256,512]{1,0:T(8,128)(2,1)S(1)}, bf16[256,512]{1,0:T(8,128)(2,1)S(1)}, u32[]{:S(2)}, u32[]{:S(2)}) collective-permute-start(bf16[256,512]{1,0:T(8,128)(2,1)S(1)} %collective-permute-done.1), channel_id=1, source_target_pairs={{0,7},{1,0},{2,1},{3,2},{4,3},{5,4},{6,5},{7,6},{8,15},{9,8},{10,9... | collective-permute-start | bytes 786440 | tf_op jit(solution)/shard_map/ppermute | solution.py:191
  55.4 2.2 %collective-permute-done.5 = bf16[256,512]{1,0:T(8,128)(2,1)S(1)} collective-permute-done((bf16[256,512]{1,0:T(8,128)(2,1)S(1)}, bf16[256,512]{1,0:T(8,128)(2,1)S(1)}, u32[]{:S(2)}, u32[]{:S(2)}) %collective-permute-start.5) | collective-permute-done | bytes 262176 | tf_op jit(solution)/shard_map/ppermute | solution.py:189
  57.5 1.9 %collective-permute-start.6 = (bf16[256,512]{1,0:T(8,128)(2,1)S(1)}, bf16[256,512]{1,0:T(8,128)(2,1)S(1)}, u32[]{:S(2)}, u32[]{:S(2)}) collective-permute-start(bf16[256,512]{1,0:T(8,128)(2,1)S(1)} %collective-permute-done.5), channel_id=1, source_target_pairs={{0,1},{1,2},{2,3},{3,4},{4,5},{5,6},{6,7},{7,0},{8,9},{9,10},{10,1... | collective-permute-start | bytes 786440 | tf_op jit(solution)/shard_map/ppermute | solution.py:189
  59.5 6.7 %collective-permute-done.6 = bf16[256,512]{1,0:T(8,128)(2,1)S(1)} collective-permute-done((bf16[256,512]{1,0:T(8,128)(2,1)S(1)}, bf16[256,512]{1,0:T(8,128)(2,1)S(1)}, u32[]{:S(2)}, u32[]{:S(2)}) %collective-permute-start.6) | collective-permute-done | bytes 262176 | tf_op jit(solution)/shard_map/ppermute | solution.py:189
  66.3 5.9 %collective-permute-start.7 = (bf16[8,256,512]{2,1,0:T(8,128)(2,1)S(1)}, bf16[8,256,512]{2,1,0:T(8,128)(2,1)}, u32[]{:S(2)}, u32[]{:S(2)}) collective-permute-start(bf16[8,256,512]{2,1,0:T(8,128)(2,1)S(1)} %bitcast_dynamic-update-slice_fusion.own_ref), channel_id=1, source_target_pairs={{0,8},{8,0},{1,9},{9,1},{2,10},{10,2},{3,11},{11,3},{4,12},{12,4},... | collective-permute-start | bytes 6291464 | tf_op jit(solution)/shard_map/ppermute | solution.py:208
  72.5 1.0 broadcast_in_dim.15
  73.5 7.2 %all-to-all-start = ((bf16[16,4,4096]{2,1,0:T(4,128)(2,1)}), bf16[16,4,4096]{2,1,0:T(4,128)(2,1)S(1)}, u32[]{:S(2)}, u32[]{:S(2)}) async-start(bf16[16,4,4096]{2,1,0:T(4,128)(2,1)} %bitcast.14), calls=%async_computation | async-start | bytes 1048576 | tf_op jit(solution)/shard_map/all_to_all | solution.py:23
  80.7 17.3 %all-to-all-done = bf16[16,4,4096]{2,1,0:T(4,128)(2,1)S(1)} async-done(((bf16[16,4,4096]{2,1,0:T(4,128)(2,1)}), bf16[16,4,4096]{2,1,0:T(4,128)(2,1)S(1)}, u32[]{:S(2)}, u32[]{:S(2)}) %all-to-all-start) | async-done | bytes 524320 | tf_op jit(solution)/shard_map/all_to_all | solution.py:23
  98.0 0.9 reshape.19
  98.9 2.2 %collective-permute-start.10 = (bf16[64,4096]{1,0:T(8,128)(2,1)}, bf16[64,4096]{1,0:T(8,128)(2,1)}, u32[]{:S(2)}, u32[]{:S(2)}) collective-permute-start(bf16[64,4096]{1,0:T(8,128)(2,1)} %reshape.19), channel_id=1, source_target_pairs={{0,128},{128,256},{256,384},{384,0},{1,129},{129,257},{257,385},{3... | collective-permute-start | bytes 1572872 | tf_op jit(solution)/shard_map/ppermute | solution.py:212
  101.1 4.3 %collective-permute-start.8 = (bf16[64,4096]{1,0:T(8,128)(2,1)}, bf16[64,4096]{1,0:T(8,128)(2,1)}, u32[]{:S(2)}, u32[]{:S(2)}) collective-permute-start(bf16[64,4096]{1,0:T(8,128)(2,1)} %reshape.19), channel_id=1, source_target_pairs={{0,384},{128,0},{256,128},{384,256},{1,385},{129,1},{257,129},{385... | collective-permute-start | bytes 1572872 | tf_op jit(solution)/shard_map/ppermute | solution.py:212
  105.4 2.2 %collective-permute-start.9 = (bf16[64,4096]{1,0:T(8,128)(2,1)}, bf16[64,4096]{1,0:T(8,128)(2,1)}, u32[]{:S(2)}, u32[]{:S(2)}) collective-permute-start(bf16[64,4096]{1,0:T(8,128)(2,1)} %reshape.19), channel_id=1, source_target_pairs={{0,256},{128,384},{256,0},{384,128},{1,257},{129,385},{257,1},{385... | collective-permute-start | bytes 1572872 | tf_op jit(solution)/shard_map/ppermute | solution.py:212
  107.8 7.0 %shard_map.38 = (bf16[2,2,2,256,128]{4,3,2,1,0:T(8,128)(2,1)S(1)}, f32[2,2,128,128]{3,2,1,0:T(8,128)S(1)}, bf16[32,8,128]{2,1,0:T(8,128)(2,1)}) custom-call(s32[1]{0:T(128)} %bitcast.z_ref, bf16[8,256,512]{2,1,0:T(8,128)(2,1)S(1)} %bitcast_dynamic-update-slice_fusion.own_ref, bf16[8,256,512]{2,1,0:T(8,128)(2,1)} %collective-permute-done.7.other_ref, ...), custom_call_target="tpu_custom_call" | custom-call | tf_op jit(solution)/shard_map/pallas_call | solution.py:117
  114.8 5.0 %all-to-all-start.2 = ((bf16[32,8,128]{2,1,0:T(8,128)(2,1)}), bf16[32,8,128]{2,1,0:T(8,128)(2,1)S(1)}, u32[]{:S(2)}, u32[]{:S(2)}) async-start(bf16[32,8,128]{2,1,0:T(8,128)(2,1)} %get-tuple-element.10), calls=%async_computation.2 | async-start | bytes 131072 | tf_op jit(solution)/shard_map/all_to_all | solution.py:23
  120.0 9.0 %all-to-all-done.2.total_ref = bf16[32,8,128]{2,1,0:T(8,128)(2,1)S(1)} async-done(((bf16[32,8,128]{2,1,0:T(8,128)(2,1)}), bf16[32,8,128]{2,1,0:T(8,128)(2,1)S(1)}, u32[]{:S(2)}, u32[]{:S(2)}) %all-to-all-start.2) | async-done | bytes 65568 | tf_op jit(solution)/shard_map/all_to_all | solution.py:23
  129.0 0.7 shard_map.40
  129.6 5.1 %all-to-all-start.3 = ((bf16[32,8,128]{2,1,0:T(8,128)(2,1)}), bf16[32,8,128]{2,1,0:T(8,128)(2,1)S(1)}, u32[]{:S(2)}, u32[]{:S(2)}) async-start(bf16[32,8,128]{2,1,0:T(8,128)(2,1)} %shard_map.40), calls=%async_computation.3 | async-start | bytes 131072 | tf_op jit(solution)/shard_map/all_to_all | solution.py:23
  134.8 3.1 %pad_maximum_fusion.weight_hbm = bf16[256,4096]{1,0:T(8,128)(2,1)} fusion(bf16[64,4096]{1,0:T(8,128)(2,1)} %collective-permute-done.10, bf16[64,4096]{1,0:T(8,128)(2,1)} %collective-permute-done.9, bf16[64,4096]{1,0:T(8,128)(2,1)} %collective-permute-done.8, bf16[64,4096]{1,0:T(8,128)(2,1)} %reshape.19), kind=kLoop, calls=%fused_computation | loop fusion | flops 8388608 | bytes 4194304 | tf_op jit(solution)/shard_map/concatenate | solution.py:211
  137.9 5.6 %shard_map.37.query_ref = bf16[2,2,256,128]{3,2,1,0:T(8,128)(2,1)S(1)} custom-call(s32[1]{0:T(128)} %bitcast.z_ref, bf16[8,256,512]{2,1,0:T(8,128)(2,1)S(1)} %bitcast_dynamic-update-slice_fusion.own_ref, bf16[8,256,512]{2,1,0:T(8,128)(2,1)} %collective-permute-done.7.other_ref, bf16[256,4096]{1,0:T(8,128)(2,1)} %pad_maximum_fusion.weight_hbm, ...), custom_call_target="tpu_custom_call" | custom-call | tf_op jit(solution)/shard_map/pallas_call | solution.py:117
  143.5 0.7 shard_map.39.inner_ref
  144.6 4.3 %collective-permute-start.11 = (bf16[2,256,128]{2,1,0:T(8,128)(2,1)S(1)}, bf16[2,256,128]{2,1,0:T(8,128)(2,1)S(1)}, u32[]{:S(2)}, u32[]{:S(2)}) collective-permute-start(bf16[2,256,128]{2,1,0:T(8,128)(2,1)S(1)} %slice_bitcast_fusion), channel_id=1, source_target_pairs={{0,8},{8,0},{1,9},{9,1},{2,10},{10,2},{3,11},{11,3},{4,12},{12,4},... | collective-permute-start | bytes 393224 | tf_op jit(solution)/shard_map/ppermute | solution.py:234
  148.9 1.0 collective-permute-done.11
  149.9 1.0 copy.9
  (39 shorter events, 1.4 us)
Async XLA Ops:
  6.5 20.7 %copy-start.2 = (bf16[256,512]{1,0:T(8,128)(2,1)S(1)}, bf16[256,512]{1,0:T(8,128)(2,1)}, u32[]{:S(2)}) copy-start(bf16[256,512]{1,0:T(8,128)(2,1)} %param.3) | copy-start | bytes 786436
  6.5 101.3 %all-gather.2.cloned.1.call-start = ((), (), s32[]{:S(2)}) async-start(), calls=%async_computation.4 | async-start | bytes 4718592 | tf_op jit(solution)/shard_map/all_gather | solution.py:206
  27.3 44.9 %copy-start = (bf16[3,4096,2,2]{1,3,2,0:T(2,128)(2,1)S(1)}, bf16[3,4096,2,2]{1,3,2,0:T(2,128)(2,1)}, u32[]{:S(2)}) copy-start(bf16[3,4096,2,2]{1,3,2,0:T(2,128)(2,1)} %param.5) | copy-start | bytes 294916
  27.3 44.9 %copy-start.1 = (bf16[3,4096,2,2]{1,3,2,0:T(2,128)(2,1)S(1)}, bf16[3,4096,2,2]{1,3,2,0:T(2,128)(2,1)}, u32[]{:S(2)}) copy-start(bf16[3,4096,2,2]{1,3,2,0:T(2,128)(2,1)} %param.4) | copy-start | bytes 294916
  27.3 12.2 %collective-permute-start.3 = (bf16[256,512]{1,0:T(8,128)(2,1)S(1)}, bf16[256,512]{1,0:T(8,128)(2,1)S(1)}, u32[]{:S(2)}, u32[]{:S(2)}) collective-permute-start(bf16[256,512]{1,0:T(8,128)(2,1)S(1)} %copy-done.2), channel_id=1, source_target_pairs={{0,1},{1,2},{2,3},{3,4},{4,5},{5,6},{6,7},{7,0},{8,9},{9,10},{10,1... | collective-permute-start | bytes 786440 | tf_op jit(solution)/shard_map/ppermute | solution.py:189
  29.4 12.0 %collective-permute-start = (bf16[256,512]{1,0:T(8,128)(2,1)S(1)}, bf16[256,512]{1,0:T(8,128)(2,1)S(1)}, u32[]{:S(2)}, u32[]{:S(2)}) collective-permute-start(bf16[256,512]{1,0:T(8,128)(2,1)S(1)} %copy-done.2), channel_id=1, source_target_pairs={{0,7},{1,0},{2,1},{3,2},{4,3},{5,4},{6,5},{7,6},{8,15},{9,8},{10,9... | collective-permute-start | bytes 786440 | tf_op jit(solution)/shard_map/ppermute | solution.py:191
  39.5 9.4 %collective-permute-start.4 = (bf16[256,512]{1,0:T(8,128)(2,1)S(1)}, bf16[256,512]{1,0:T(8,128)(2,1)S(1)}, u32[]{:S(2)}, u32[]{:S(2)}) collective-permute-start(bf16[256,512]{1,0:T(8,128)(2,1)S(1)} %collective-permute-done.3), channel_id=1, source_target_pairs={{0,1},{1,2},{2,3},{3,4},{4,5},{5,6},{6,7},{7,0},{8,9},{9,10},{10,1... | collective-permute-start | bytes 786440 | tf_op jit(solution)/shard_map/ppermute | solution.py:189
  41.4 9.4 %collective-permute-start.1 = (bf16[256,512]{1,0:T(8,128)(2,1)S(1)}, bf16[256,512]{1,0:T(8,128)(2,1)S(1)}, u32[]{:S(2)}, u32[]{:S(2)}) collective-permute-start(bf16[256,512]{1,0:T(8,128)(2,1)S(1)} %collective-permute-done), channel_id=1, source_target_pairs={{0,7},{1,0},{2,1},{3,2},{4,3},{5,4},{6,5},{7,6},{8,15},{9,8},{10,9... | collective-permute-start | bytes 786440 | tf_op jit(solution)/shard_map/ppermute | solution.py:191
  48.8 8.7 %collective-permute-start.5 = (bf16[256,512]{1,0:T(8,128)(2,1)S(1)}, bf16[256,512]{1,0:T(8,128)(2,1)S(1)}, u32[]{:S(2)}, u32[]{:S(2)}) collective-permute-start(bf16[256,512]{1,0:T(8,128)(2,1)S(1)} %collective-permute-done.4), channel_id=1, source_target_pairs={{0,1},{1,2},{2,3},{3,4},{4,5},{5,6},{6,7},{7,0},{8,9},{9,10},{10,1... | collective-permute-start | bytes 786440 | tf_op jit(solution)/shard_map/ppermute | solution.py:189
  50.8 8.7 %collective-permute-start.2 = (bf16[256,512]{1,0:T(8,128)(2,1)S(1)}, bf16[256,512]{1,0:T(8,128)(2,1)S(1)}, u32[]{:S(2)}, u32[]{:S(2)}) collective-permute-start(bf16[256,512]{1,0:T(8,128)(2,1)S(1)} %collective-permute-done.1), channel_id=1, source_target_pairs={{0,7},{1,0},{2,1},{3,2},{4,3},{5,4},{6,5},{7,6},{8,15},{9,8},{10,9... | collective-permute-start | bytes 786440 | tf_op jit(solution)/shard_map/ppermute | solution.py:191
  57.5 8.7 %collective-permute-start.6 = (bf16[256,512]{1,0:T(8,128)(2,1)S(1)}, bf16[256,512]{1,0:T(8,128)(2,1)S(1)}, u32[]{:S(2)}, u32[]{:S(2)}) collective-permute-start(bf16[256,512]{1,0:T(8,128)(2,1)S(1)} %collective-permute-done.5), channel_id=1, source_target_pairs={{0,1},{1,2},{2,3},{3,4},{4,5},{5,6},{6,7},{7,0},{8,9},{9,10},{10,1... | collective-permute-start | bytes 786440 | tf_op jit(solution)/shard_map/ppermute | solution.py:189
  66.3 41.5 %collective-permute-start.7 = (bf16[8,256,512]{2,1,0:T(8,128)(2,1)S(1)}, bf16[8,256,512]{2,1,0:T(8,128)(2,1)}, u32[]{:S(2)}, u32[]{:S(2)}) collective-permute-start(bf16[8,256,512]{2,1,0:T(8,128)(2,1)S(1)} %bitcast_dynamic-update-slice_fusion.own_ref), channel_id=1, source_target_pairs={{0,8},{8,0},{1,9},{9,1},{2,10},{10,2},{3,11},{11,3},{4,12},{12,4},... | collective-permute-start | bytes 6291464 | tf_op jit(solution)/shard_map/ppermute | solution.py:208
  73.5 24.5 %all-to-all-start = ((bf16[16,4,4096]{2,1,0:T(4,128)(2,1)}), bf16[16,4,4096]{2,1,0:T(4,128)(2,1)S(1)}, u32[]{:S(2)}, u32[]{:S(2)}) async-start(bf16[16,4,4096]{2,1,0:T(4,128)(2,1)} %bitcast.14), calls=%async_computation | async-start | bytes 1048576 | tf_op jit(solution)/shard_map/all_to_all | solution.py:23
  98.9 35.8 %collective-permute-start.10 = (bf16[64,4096]{1,0:T(8,128)(2,1)}, bf16[64,4096]{1,0:T(8,128)(2,1)}, u32[]{:S(2)}, u32[]{:S(2)}) collective-permute-start(bf16[64,4096]{1,0:T(8,128)(2,1)} %reshape.19), channel_id=1, source_target_pairs={{0,128},{128,256},{256,384},{384,0},{1,129},{129,257},{257,385},{3... | collective-permute-start | bytes 1572872 | tf_op jit(solution)/shard_map/ppermute | solution.py:212
  101.1 33.7 %collective-permute-start.8 = (bf16[64,4096]{1,0:T(8,128)(2,1)}, bf16[64,4096]{1,0:T(8,128)(2,1)}, u32[]{:S(2)}, u32[]{:S(2)}) collective-permute-start(bf16[64,4096]{1,0:T(8,128)(2,1)} %reshape.19), channel_id=1, source_target_pairs={{0,384},{128,0},{256,128},{384,256},{1,385},{129,1},{257,129},{385... | collective-permute-start | bytes 1572872 | tf_op jit(solution)/shard_map/ppermute | solution.py:212
  105.4 29.4 %collective-permute-start.9 = (bf16[64,4096]{1,0:T(8,128)(2,1)}, bf16[64,4096]{1,0:T(8,128)(2,1)}, u32[]{:S(2)}, u32[]{:S(2)}) collective-permute-start(bf16[64,4096]{1,0:T(8,128)(2,1)} %reshape.19), channel_id=1, source_target_pairs={{0,256},{128,384},{256,0},{384,128},{1,257},{129,385},{257,1},{385... | collective-permute-start | bytes 1572872 | tf_op jit(solution)/shard_map/ppermute | solution.py:212
  114.8 14.2 %all-to-all-start.2 = ((bf16[32,8,128]{2,1,0:T(8,128)(2,1)}), bf16[32,8,128]{2,1,0:T(8,128)(2,1)S(1)}, u32[]{:S(2)}, u32[]{:S(2)}) async-start(bf16[32,8,128]{2,1,0:T(8,128)(2,1)} %get-tuple-element.10), calls=%async_computation.2 | async-start | bytes 131072 | tf_op jit(solution)/shard_map/all_to_all | solution.py:23
  129.6 14.5 %all-to-all-start.3 = ((bf16[32,8,128]{2,1,0:T(8,128)(2,1)}), bf16[32,8,128]{2,1,0:T(8,128)(2,1)S(1)}, u32[]{:S(2)}, u32[]{:S(2)}) async-start(bf16[32,8,128]{2,1,0:T(8,128)(2,1)} %shard_map.40), calls=%async_computation.3 | async-start | bytes 131072 | tf_op jit(solution)/shard_map/all_to_all | solution.py:23
  144.6 5.3 %collective-permute-start.11 = (bf16[2,256,128]{2,1,0:T(8,128)(2,1)S(1)}, bf16[2,256,128]{2,1,0:T(8,128)(2,1)S(1)}, u32[]{:S(2)}, u32[]{:S(2)}) collective-permute-start(bf16[2,256,128]{2,1,0:T(8,128)(2,1)S(1)} %slice_bitcast_fusion), channel_id=1, source_target_pairs={{0,8},{8,0},{1,9},{9,1},{2,10},{10,2},{3,11},{11,3},{4,12},{12,4},... | collective-permute-start | bytes 393224 | tf_op jit(solution)/shard_map/ppermute | solution.py:234
Sparse Core Ops, SparseCore 0:
  27.4 56.0 all-gather.1

commit v4 on v3

--- a/solution.py
+++ b/solution.py
@@ -59,25 +59,31 @@
 PER = NZ // CHUNKS
 
 
-def multiply(z_ref, own_ref, other_ref, weight_hbm, weight, acc, sem):
+def multiply(z_ref, own_ref, other_hbm, weights_hbm, other, weight, acc, sem):
     copies = []
     for k in range(NZ):
         start = pl.multiple_of(((z_ref[0] + k) & (NZ - 1)) * PIECE, PIECE)
-        copies.append(
-            pltpu.make_async_copy(
-                weight_hbm.at[:, pl.ds(start, PIECE)],
-                weight.at[k // PER, :, pl.ds((k % PER) * PIECE, PIECE)],
-                sem.at[k],
+        columns = pl.ds((k % PER) * PIECE, PIECE)
+        group = [pltpu.make_async_copy(other_hbm.at[k], other.at[k], sem.at[k, 0])]
+        for i, part in enumerate(weights_hbm):
+            rows = part.shape[0]
+            group.append(
+                pltpu.make_async_copy(
+                    part.at[:, pl.ds(start, PIECE)],
+                    weight.at[k // PER, pl.ds(i * rows, rows), columns],
+                    sem.at[k, i + 1],
+                )
             )
-        )
-    for copy in copies:
-        copy.start()
+        for copy in group:
+            copy.start()
+        copies.append(group)
     for k in range(CHUNKS):
         pieces = range(k * PER, (k + 1) * PER)
         for i in pieces:
-            copies[i].wait()
+            for copy in copies[i]:
+                copy.wait()
         tokens = jnp.concatenate(
-            [jnp.concatenate([ref[i] for i in pieces], 1) for ref in (own_ref, other_ref)], 0
+            [jnp.concatenate([ref[i] for i in pieces], 1) for ref in (own_ref, other)], 0
         )
         part = lax.dot_general(tokens, weight[k], NT, preferred_element_type=F32)
         if k == 0:
@@ -86,18 +92,18 @@
             acc[...] += part
 
 
-def query_kernel(z_ref, own_ref, other_ref, weight_hbm, order_ref, out_ref, weight, acc, sem):
-    multiply(z_ref, own_ref, other_ref, weight_hbm, weight, acc, sem)
+def query_kernel(z_ref, own_ref, order_ref, other_hbm, *refs):
+    weights_hbm, (out_ref, other, weight, acc, sem) = refs[:-5], refs[-5:]
+    multiply(z_ref, own_ref, other_hbm, weights_hbm, other, weight, acc, sem)
     rows = signs_and_order(acc[...], order_ref[...])
     for block in range(2):
         for s in range(2):
             out_ref[block, s] = rows[block * TOK : (block + 1) * TOK, s * HD : (s + 1) * HD]
 
 
-def key_value_kernel(
-    z_ref, own_ref, other_ref, weight_hbm, order_ref, out_ref, state_ref, total_ref, weight, acc, sem
-):
-    multiply(z_ref, own_ref, other_ref, weight_hbm, weight, acc, sem)
+def key_value_kernel(z_ref, own_ref, order_ref, other_hbm, *refs):
+    weights_hbm, (out_ref, state_ref, total_ref, other, weight, acc, sem) = refs[:-7], refs[-7:]
+    multiply(z_ref, own_ref, other_hbm, weights_hbm, other, weight, acc, sem)
     rows = signs_and_order(acc[...], order_ref[...])
     for s in range(2):
         for block in range(2):
@@ -111,27 +117,24 @@
         total_ref[s * NX * NY // 2 : (s + 1) * NX * NY // 2] = total.astype(BF16)
 
 
-def project(kernel, z, own, other, weight, order, out_shape):
-    rows = weight.shape[0]
+def project(kernel, z, own, other, weights, order, out_shape):
+    rows = sum(weight.shape[0] for weight in weights)
     vmem = pl.BlockSpec(memory_space=pltpu.VMEM)
+    far = [pltpu.with_memory_space_constraint(a, pltpu.HBM) for a in (other, *weights)]
     return pl.pallas_call(
         kernel,
-        in_specs=[
-            pl.BlockSpec(memory_space=pltpu.SMEM),
-            vmem,
-            vmem,
-            pl.BlockSpec(memory_space=pltpu.HBM),
-            vmem,
-        ],
+        in_specs=[pl.BlockSpec(memory_space=pltpu.SMEM), vmem, vmem]
+        + [pl.BlockSpec(memory_space=pltpu.HBM)] * len(far),
         out_specs=jax.tree.map(lambda s: vmem, out_shape),
         scratch_shapes=[
+            pltpu.VMEM(other.shape, BF16),
             pltpu.VMEM((CHUNKS, rows, PER * PIECE), BF16),
             pltpu.VMEM((2 * TOK, rows), F32),
-            pltpu.SemaphoreType.DMA((NZ,)),
+            pltpu.SemaphoreType.DMA((NZ, len(far))),
         ],
         out_shape=out_shape,
         compiler_params=pltpu.CompilerParams(vmem_limit_bytes=24 << 20),
-    )(z, own, other, pltpu.with_memory_space_constraint(weight, pltpu.HBM), order)
+    )(z, own, order, *far)
 
 
 def prefix_kernel(total_ref, out_ref):
@@ -181,7 +184,7 @@
     return jax.ShapeDtypeStruct(dims, dtype)
 
 
-def token_ring(piece):
+def token_ring(piece, q_part):
     up = [(i, (i + 1) % NZ) for i in range(NZ)]
     down = [(i, (i - 1) % NZ) for i in range(NZ)]
     below, above = [piece], [piece]
@@ -189,7 +192,9 @@
         below.append(lax.ppermute(below[-1], "z", up))
         if hop < NZ // 2 - 1:
             above.append(lax.ppermute(above[-1], "z", down))
-    return jnp.stack(above + below[:0:-1])
+        if hop == 0:
+            below[1], above[1], q_part = lax.optimization_barrier((below[1], above[1], q_part))
+    return jnp.stack(above + below[:0:-1]), q_part
 
 
 def on_device(hidden_in, proj_weights, directions):
@@ -204,24 +209,24 @@
 
     kv_part = exchange(replicate(kv_rows, NX).reshape(NX * NC, 8, D), ("x", "c"))
     kv_weight = lax.all_gather(kv_part.reshape(64, D), "y", axis=0, tiled=True)
-    own = token_ring(hidden_in)
+    q_part = exchange(replicate(q_rows, NY).reshape(NY * NC, 4, D), ("y", "c"))
+    own, q_part = token_ring(hidden_in, q_part)
     other = lax.ppermute(own, "c", swap)
-    q_part = exchange(replicate(q_rows, NY).reshape(NY * NC, 4, D), ("y", "c"))
     q_mine = q_part.reshape(64, D)
-    q_weight = jnp.concatenate(
-        [q_mine] + [lax.ppermute(q_mine, "x", [(i, (i - k) % NX) for i in range(NX)]) for k in (1, 2, 3)]
-    )
+    q_weights = [q_mine] + [
+        lax.ppermute(q_mine, "x", [(i, (i - k) % NX) for i in range(NX)]) for k in range(1, NX)
+    ]
 
     where = z.astype(jnp.int32).reshape(1)
     query = project(
-        query_kernel, where, own, other, q_weight, column_order(1, x), shape(2, 2, TOK, HD)
+        query_kernel, where, own, other, q_weights, column_order(1, x), shape(2, 2, TOK, HD)
     )
     kv, state, total = project(
         key_value_kernel,
         where,
         own,
         other,
-        kv_weight,
+        [kv_weight],
         column_order(2),
         (shape(2, 2, 2, TOK, HD), shape(2, 2, HD, HD, dtype=F32), shape(NX * NY, 8, HD)),
     )

time: 159 us -> 157 us (0.987)
  starting transfers between devices: 59.5 us -> 69 us
  waiting for transfers between devices: 42.7 us -> 37.5 us
  other arithmetic: 4.6 us -> 1.52 us
  Pallas kernels: 14.3 us -> 11.8 us
    all_to_all x3, waiting for transfers between devices: 26.3 us -> 13.9 us  [exchange(): return lax.all_to_all(x, axes, 0, 0, tiled=True)]
    ppermute x3, starting transfers between devices: 15.6 us -> 23.7 us  [token_ring(): above.append(lax.ppermute(above[-1], 'z', down))]
    ppermute x4, waiting for transfers between devices: 15.4 us -> 21.7 us  [token_ring(): below.append(lax.ppermute(below[-1], 'z', up))]
    ppermute x1, starting transfers between devices: 5.87 us -> 2.36 us  [on_device(): other = lax.ppermute(own, 'c', swap)]
    ppermute x4, starting transfers between devices: 7.78 us -> 10.9 us  [token_ring(): below.append(lax.ppermute(below[-1], 'z', up))]
    concatenate x1 -> x0, other arithmetic: 3.07 us -> none  [on_device(): jnp.concatenate([q_mine] + [lax.ppermute(q_mine, 'x', [(i, (i - k) % NX)...]
    pallas_call x2, Pallas kernels: 12.6 us -> 10.2 us  [project(): pl.pallas_call(kernel, in_specs=[pl.BlockSpec(memory_space=pltpu.SMEM), v...]
    all_to_all x3, starting transfers between devices: 17.4 us -> 19.1 us  [exchange(): return lax.all_to_all(x, axes, 0, 0, tiled=True)]
  transfers between devices with their start and end apart: 16 -> 16, of which waited for: 7 -> 9; matrix products, arithmetic and copies ran while one was open for 4% -> 2% of each run, Pallas kernels for 9% -> 7%
where the time goes in v4:
time: 157 us
  starting transfers between devices  69 us (44%)
  waiting for transfers between devices  37.5 us (24%)
  blocking collectives  19.4 us (12%)
  between operations  13.8 us (9%)
  Pallas kernels  11.8 us (8%)
  local copies, waits for them, and re-layouts  3.45 us (2%)
    ppermute x3, starting transfers between devices, token_ring(): above.append(lax.ppermute(above[-1], 'z', down))  23.7 us
    ppermute x4, waiting for transfers between devices, token_ring(): below.append(lax.ppermute(below[-1], 'z', up))  21.7 us
    all_to_all x1, blocking collectives, exchange(): return lax.all_to_all(x, axes, 0, 0, tiled=True)  19.4 us
    all_to_all x3, starting transfers between devices, exchange(): return lax.all_to_all(x, axes, 0, 0, tiled=True)  19.1 us
    all_to_all x3, waiting for transfers between devices, exchange(): return lax.all_to_all(x, axes, 0, 0, tiled=True)  13.9 us
    ppermute x4, starting transfers between devices, token_ring(): below.append(lax.ppermute(below[-1], 'z', up))  10.9 us
    pallas_call x2, Pallas kernels, project(): pl.pallas_call(kernel, in_specs=[pl.BlockSpec(memory_space=pltpu.SMEM), v...  10.2 us
    ppermute x3, starting transfers between devices, on_device(): lax.ppermute(q_mine, 'x', [(i, (i - k) % NX) for i in range(NX)])  8.4 us
  transfers between devices with their start and end apart: 16, of which 9 were waited for; matrix products, arithmetic and copies ran while one was open for 2% of the time, Pallas kernels for 7%

profile of v4, /device:TPU:1, one launch (start us, length us, event | category | flops | bytes accessed | tf_op | source)
XLA Modules:
  0.0 156.5 jit_solution(3760477363643316405)
XLA Ops:
  6.5 1.1 fusion.2
  7.9 19.4 %all_to_all.20 = bf16[8,8,4096]{2,1,0:T(8,128)(2,1)} all-to-all(bf16[8,8,4096]{2,1,0:T(8,128)(2,1)S(1)} %bitcast.42), channel_id=1, replica_groups=mesh['x'=4,'y'=8,'c'=2,'z'=8] {'x','c'}, dimensions={0} | all-to-all | bytes 1048576 | tf_op jit(solution)/shard_map/all_to_all | solution.py:23
  27.7 1.0 broadcast_in_dim.15
  28.7 4.4 %all-to-all-start = ((bf16[16,4,4096]{2,1,0:T(4,128)(2,1)}), bf16[16,4,4096]{2,1,0:T(4,128)(2,1)S(1)}, u32[]{:S(2)}, u32[]{:S(2)}) async-start(bf16[16,4,4096]{2,1,0:T(4,128)(2,1)} %bitcast.7), calls=%async_computation | async-start | bytes 1048576 | tf_op jit(solution)/shard_map/all_to_all | solution.py:23
  33.1 3.5 %collective-permute-start = (bf16[256,512]{1,0:T(8,128)(2,1)S(1)}, bf16[256,512]{1,0:T(8,128)(2,1)S(1)}, u32[]{:S(2)}, u32[]{:S(2)}) collective-permute-start(bf16[256,512]{1,0:T(8,128)(2,1)S(1)} %copy-done.2), channel_id=1, source_target_pairs={{0,1},{1,2},{2,3},{3,4},{4,5},{5,6},{6,7},{7,0},{8,9},{9,10},{10,1... | collective-permute-start | bytes 786440 | tf_op jit(solution)/shard_map/ppermute | solution.py:192
  36.6 8.6 %collective-permute-start.1 = (bf16[256,512]{1,0:T(8,128)(2,1)S(1)}, bf16[256,512]{1,0:T(8,128)(2,1)S(1)}, u32[]{:S(2)}, u32[]{:S(2)}) collective-permute-start(bf16[256,512]{1,0:T(8,128)(2,1)S(1)} %copy-done.2), channel_id=1, source_target_pairs={{0,7},{1,0},{2,1},{3,2},{4,3},{5,4},{6,5},{7,6},{8,15},{9,8},{10,9... | collective-permute-start | bytes 786440 | tf_op jit(solution)/shard_map/ppermute | solution.py:194
  45.2 4.7 %collective-permute-done = bf16[256,512]{1,0:T(8,128)(2,1)S(1)} collective-permute-done((bf16[256,512]{1,0:T(8,128)(2,1)S(1)}, bf16[256,512]{1,0:T(8,128)(2,1)S(1)}, u32[]{:S(2)}, u32[]{:S(2)}) %collective-permute-start) | collective-permute-done | bytes 262176 | tf_op jit(solution)/shard_map/ppermute | solution.py:192
  49.9 0.9 collective-permute-done.1
  50.8 1.5 all-to-all-done
  52.3 3.6 %collective-permute-start.4 = (bf16[256,512]{1,0:T(8,128)(2,1)S(1)}, bf16[256,512]{1,0:T(8,128)(2,1)S(1)}, u32[]{:S(2)}, u32[]{:S(2)}) collective-permute-start(bf16[256,512]{1,0:T(8,128)(2,1)S(1)} %collective-permute-done), channel_id=1, source_target_pairs={{0,1},{1,2},{2,3},{3,4},{4,5},{5,6},{6,7},{7,0},{8,9},{9,10},{10,1... | collective-permute-start | bytes 786440 | tf_op jit(solution)/shard_map/ppermute | solution.py:192
  55.9 10.3 %collective-permute-start.2 = (bf16[256,512]{1,0:T(8,128)(2,1)S(1)}, bf16[256,512]{1,0:T(8,128)(2,1)S(1)}, u32[]{:S(2)}, u32[]{:S(2)}) collective-permute-start(bf16[256,512]{1,0:T(8,128)(2,1)S(1)} %collective-permute-done.1), channel_id=1, source_target_pairs={{0,7},{1,0},{2,1},{3,2},{4,3},{5,4},{6,5},{7,6},{8,15},{9,8},{10,9... | collective-permute-start | bytes 786440 | tf_op jit(solution)/shard_map/ppermute | solution.py:194
  66.3 3.6 %collective-permute-done.4 = bf16[256,512]{1,0:T(8,128)(2,1)S(1)} collective-permute-done((bf16[256,512]{1,0:T(8,128)(2,1)S(1)}, bf16[256,512]{1,0:T(8,128)(2,1)S(1)}, u32[]{:S(2)}, u32[]{:S(2)}) %collective-permute-start.4) | collective-permute-done | bytes 262176 | tf_op jit(solution)/shard_map/ppermute | solution.py:192
  69.9 1.9 %collective-permute-start.5 = (bf16[256,512]{1,0:T(8,128)(2,1)S(1)}, bf16[256,512]{1,0:T(8,128)(2,1)S(1)}, u32[]{:S(2)}, u32[]{:S(2)}) collective-permute-start(bf16[256,512]{1,0:T(8,128)(2,1)S(1)} %collective-permute-done.4), channel_id=1, source_target_pairs={{0,1},{1,2},{2,3},{3,4},{4,5},{5,6},{6,7},{7,0},{8,9},{9,10},{10,1... | collective-permute-start | bytes 786440 | tf_op jit(solution)/shard_map/ppermute | solution.py:192
  71.8 4.8 %collective-permute-start.3 = (bf16[256,512]{1,0:T(8,128)(2,1)S(1)}, bf16[256,512]{1,0:T(8,128)(2,1)S(1)}, u32[]{:S(2)}, u32[]{:S(2)}) collective-permute-start(bf16[256,512]{1,0:T(8,128)(2,1)S(1)} %collective-permute-done.2), channel_id=1, source_target_pairs={{0,7},{1,0},{2,1},{3,2},{4,3},{5,4},{6,5},{7,6},{8,15},{9,8},{10,9... | collective-permute-start | bytes 786440 | tf_op jit(solution)/shard_map/ppermute | solution.py:194
  76.7 4.0 %collective-permute-done.5 = bf16[256,512]{1,0:T(8,128)(2,1)S(1)} collective-permute-done((bf16[256,512]{1,0:T(8,128)(2,1)S(1)}, bf16[256,512]{1,0:T(8,128)(2,1)S(1)}, u32[]{:S(2)}, u32[]{:S(2)}) %collective-permute-start.5) | collective-permute-done | bytes 262176 | tf_op jit(solution)/shard_map/ppermute | solution.py:192
  80.7 1.9 %collective-permute-start.6 = (bf16[256,512]{1,0:T(8,128)(2,1)S(1)}, bf16[256,512]{1,0:T(8,128)(2,1)S(1)}, u32[]{:S(2)}, u32[]{:S(2)}) collective-permute-start(bf16[256,512]{1,0:T(8,128)(2,1)S(1)} %collective-permute-done.5), channel_id=1, source_target_pairs={{0,1},{1,2},{2,3},{3,4},{4,5},{5,6},{6,7},{7,0},{8,9},{9,10},{10,1... | collective-permute-start | bytes 786440 | tf_op jit(solution)/shard_map/ppermute | solution.py:192
  82.6 9.4 %collective-permute-done.6 = bf16[256,512]{1,0:T(8,128)(2,1)S(1)} collective-permute-done((bf16[256,512]{1,0:T(8,128)(2,1)S(1)}, bf16[256,512]{1,0:T(8,128)(2,1)S(1)}, u32[]{:S(2)}, u32[]{:S(2)}) %collective-permute-start.6) | collective-permute-done | bytes 262176 | tf_op jit(solution)/shard_map/ppermute | solution.py:192
  92.1 2.4 %collective-permute-start.7 = (bf16[8,256,512]{2,1,0:T(8,128)(2,1)S(1)}, bf16[8,256,512]{2,1,0:T(8,128)(2,1)}, u32[]{:S(2)}, u32[]{:S(2)}) collective-permute-start(bf16[8,256,512]{2,1,0:T(8,128)(2,1)S(1)} %bitcast_dynamic-update-slice_fusion.own_ref), channel_id=1, source_target_pairs={{0,8},{8,0},{1,9},{9,1},{2,10},{10,2},{3,11},{11,3},{4,12},{12,4},... | collective-permute-start | bytes 6291464 | tf_op jit(solution)/shard_map/ppermute | solution.py:214
  94.5 0.9 reshape.19.refs_0_
  95.4 1.9 %collective-permute-start.10 = (bf16[64,4096]{1,0:T(8,128)(2,1)}, bf16[64,4096]{1,0:T(8,128)(2,1)}, u32[]{:S(2)}, u32[]{:S(2)}) collective-permute-start(bf16[64,4096]{1,0:T(8,128)(2,1)} %reshape.19.refs_0_), channel_id=1, source_target_pairs={{0,128},{128,256},{256,384},{384,0},{1,129},{129,257},{257,385},{3... | collective-permute-start | bytes 1572872 | tf_op jit(solution)/shard_map/ppermute | solution.py:217
  97.3 4.6 %collective-permute-start.8 = (bf16[64,4096]{1,0:T(8,128)(2,1)}, bf16[64,4096]{1,0:T(8,128)(2,1)}, u32[]{:S(2)}, u32[]{:S(2)}) collective-permute-start(bf16[64,4096]{1,0:T(8,128)(2,1)} %reshape.19.refs_0_), channel_id=1, source_target_pairs={{0,384},{128,0},{256,128},{384,256},{1,385},{129,1},{257,129},{385... | collective-permute-start | bytes 1572872 | tf_op jit(solution)/shard_map/ppermute | solution.py:217
  101.9 1.9 %collective-permute-start.9 = (bf16[64,4096]{1,0:T(8,128)(2,1)}, bf16[64,4096]{1,0:T(8,128)(2,1)}, u32[]{:S(2)}, u32[]{:S(2)}) collective-permute-start(bf16[64,4096]{1,0:T(8,128)(2,1)} %reshape.19.refs_0_), channel_id=1, source_target_pairs={{0,256},{128,384},{256,0},{384,128},{1,257},{129,385},{257,1},{385... | collective-permute-start | bytes 1572872 | tf_op jit(solution)/shard_map/ppermute | solution.py:217
  104.1 5.6 %shard_map.38 = (bf16[2,2,2,256,128]{4,3,2,1,0:T(8,128)(2,1)S(1)}, f32[2,2,128,128]{3,2,1,0:T(8,128)S(1)}, bf16[32,8,128]{2,1,0:T(8,128)(2,1)}) custom-call(s32[1]{0:T(128)} %bitcast.z_ref, bf16[8,256,512]{2,1,0:T(8,128)(2,1)S(1)} %bitcast_dynamic-update-slice_fusion.own_ref, bf16[512,512]{1,0:T(8,128)(2,1)S(1)} %fusion.order_ref, ...), custom_call_target="tpu_custom_call" | custom-call | tf_op jit(solution)/shard_map/pallas_call | solution.py:124
  109.7 7.7 %all-to-all-start.2 = ((bf16[32,8,128]{2,1,0:T(8,128)(2,1)}), bf16[32,8,128]{2,1,0:T(8,128)(2,1)S(1)}, u32[]{:S(2)}, u32[]{:S(2)}) async-start(bf16[32,8,128]{2,1,0:T(8,128)(2,1)} %get-tuple-element.16), calls=%async_computation.2 | async-start | bytes 131072 | tf_op jit(solution)/shard_map/all_to_all | solution.py:23
  117.4 8.8 %all-to-all-done.2.total_ref = bf16[32,8,128]{2,1,0:T(8,128)(2,1)S(1)} async-done(((bf16[32,8,128]{2,1,0:T(8,128)(2,1)}), bf16[32,8,128]{2,1,0:T(8,128)(2,1)S(1)}, u32[]{:S(2)}, u32[]{:S(2)}) %all-to-all-start.2) | async-done | bytes 65568 | tf_op jit(solution)/shard_map/all_to_all | solution.py:23
  126.2 0.7 shard_map.40
  126.9 7.1 %all-to-all-start.3 = ((bf16[32,8,128]{2,1,0:T(8,128)(2,1)}), bf16[32,8,128]{2,1,0:T(8,128)(2,1)S(1)}, u32[]{:S(2)}, u32[]{:S(2)}) async-start(bf16[32,8,128]{2,1,0:T(8,128)(2,1)} %shard_map.40), calls=%async_computation.3 | async-start | bytes 131072 | tf_op jit(solution)/shard_map/all_to_all | solution.py:23
  134.1 4.5 %shard_map.37.query_ref = bf16[2,2,256,128]{3,2,1,0:T(8,128)(2,1)S(1)} custom-call(s32[1]{0:T(128)} %bitcast.z_ref, bf16[8,256,512]{2,1,0:T(8,128)(2,1)S(1)} %bitcast_dynamic-update-slice_fusion.own_ref, bf16[256,256]{1,0:T(8,128)(2,1)S(1)} %fusion.1.order_ref, bf16[8,256,512]{2,1,0:T(8,128)(2,1)} %collective-permute-done.7.other_hbm, ...), custom_call_target="tpu_custom_call" | custom-call | tf_op jit(solution)/shard_map/pallas_call | solution.py:124
  139.3 3.5 %all-to-all-done.3.prior_ref = bf16[32,8,128]{2,1,0:T(8,128)(2,1)S(1)} async-done(((bf16[32,8,128]{2,1,0:T(8,128)(2,1)}), bf16[32,8,128]{2,1,0:T(8,128)(2,1)S(1)}, u32[]{:S(2)}, u32[]{:S(2)}) %all-to-all-start.3) | async-done | bytes 65568 | tf_op jit(solution)/shard_map/all_to_all | solution.py:23
  143.2 4.4 %collective-permute-start.11 = (bf16[2,256,128]{2,1,0:T(8,128)(2,1)S(1)}, bf16[2,256,128]{2,1,0:T(8,128)(2,1)S(1)}, u32[]{:S(2)}, u32[]{:S(2)}) collective-permute-start(bf16[2,256,128]{2,1,0:T(8,128)(2,1)S(1)} %slice_bitcast_fusion), channel_id=1, source_target_pairs={{0,8},{8,0},{1,9},{9,1},{2,10},{10,2},{3,11},{11,3},{4,12},{12,4},... | collective-permute-start | bytes 393224 | tf_op jit(solution)/shard_map/ppermute | solution.py:239
  147.7 1.0 collective-permute-done.11
  148.7 1.0 copy.9
  (38 shorter events, 2.1 us)
Async XLA Ops:
  6.5 20.9 %copy-start.1 = (bf16[3,4096,2,2]{1,3,2,0:T(2,128)(2,1)S(1)}, bf16[3,4096,2,2]{1,3,2,0:T(2,128)(2,1)}, u32[]{:S(2)}) copy-start(bf16[3,4096,2,2]{1,3,2,0:T(2,128)(2,1)} %param.4) | copy-start | bytes 294916
  6.5 20.9 %copy-start = (bf16[3,4096,2,2]{1,3,2,0:T(2,128)(2,1)S(1)}, bf16[3,4096,2,2]{1,3,2,0:T(2,128)(2,1)}, u32[]{:S(2)}) copy-start(bf16[3,4096,2,2]{1,3,2,0:T(2,128)(2,1)} %param.5) | copy-start | bytes 294916
  6.5 97.5 %all-gather.2.cloned.1.call-start = ((), (), s32[]{:S(2)}) async-start(), calls=%async_computation.4 | async-start | bytes 4718592 | tf_op jit(solution)/shard_map/all_gather | solution.py:211
  7.9 25.2 %copy-start.2 = (bf16[256,512]{1,0:T(8,128)(2,1)S(1)}, bf16[256,512]{1,0:T(8,128)(2,1)}, u32[]{:S(2)}) copy-start(bf16[256,512]{1,0:T(8,128)(2,1)} %param.3) | copy-start | bytes 786436
  28.7 23.6 %all-to-all-start = ((bf16[16,4,4096]{2,1,0:T(4,128)(2,1)}), bf16[16,4,4096]{2,1,0:T(4,128)(2,1)S(1)}, u32[]{:S(2)}, u32[]{:S(2)}) async-start(bf16[16,4,4096]{2,1,0:T(4,128)(2,1)} %bitcast.7), calls=%async_computation | async-start | bytes 1048576 | tf_op jit(solution)/shard_map/all_to_all | solution.py:23
  33.1 16.8 %collective-permute-start = (bf16[256,512]{1,0:T(8,128)(2,1)S(1)}, bf16[256,512]{1,0:T(8,128)(2,1)S(1)}, u32[]{:S(2)}, u32[]{:S(2)}) collective-permute-start(bf16[256,512]{1,0:T(8,128)(2,1)S(1)} %copy-done.2), channel_id=1, source_target_pairs={{0,1},{1,2},{2,3},{3,4},{4,5},{5,6},{6,7},{7,0},{8,9},{9,10},{10,1... | collective-permute-start | bytes 786440 | tf_op jit(solution)/shard_map/ppermute | solution.py:192
  36.6 14.2 %collective-permute-start.1 = (bf16[256,512]{1,0:T(8,128)(2,1)S(1)}, bf16[256,512]{1,0:T(8,128)(2,1)S(1)}, u32[]{:S(2)}, u32[]{:S(2)}) collective-permute-start(bf16[256,512]{1,0:T(8,128)(2,1)S(1)} %copy-done.2), channel_id=1, source_target_pairs={{0,7},{1,0},{2,1},{3,2},{4,3},{5,4},{6,5},{7,6},{8,15},{9,8},{10,9... | collective-permute-start | bytes 786440 | tf_op jit(solution)/shard_map/ppermute | solution.py:194
  52.3 17.6 %collective-permute-start.4 = (bf16[256,512]{1,0:T(8,128)(2,1)S(1)}, bf16[256,512]{1,0:T(8,128)(2,1)S(1)}, u32[]{:S(2)}, u32[]{:S(2)}) collective-permute-start(bf16[256,512]{1,0:T(8,128)(2,1)S(1)} %collective-permute-done), channel_id=1, source_target_pairs={{0,1},{1,2},{2,3},{3,4},{4,5},{5,6},{6,7},{7,0},{8,9},{9,10},{10,1... | collective-permute-start | bytes 786440 | tf_op jit(solution)/shard_map/ppermute | solution.py:192
  55.9 15.9 %collective-permute-start.2 = (bf16[256,512]{1,0:T(8,128)(2,1)S(1)}, bf16[256,512]{1,0:T(8,128)(2,1)S(1)}, u32[]{:S(2)}, u32[]{:S(2)}) collective-permute-start(bf16[256,512]{1,0:T(8,128)(2,1)S(1)} %collective-permute-done.1), channel_id=1, source_target_pairs={{0,7},{1,0},{2,1},{3,2},{4,3},{5,4},{6,5},{7,6},{8,15},{9,8},{10,9... | collective-permute-start | bytes 786440 | tf_op jit(solution)/shard_map/ppermute | solution.py:194
  69.9 10.8 %collective-permute-start.5 = (bf16[256,512]{1,0:T(8,128)(2,1)S(1)}, bf16[256,512]{1,0:T(8,128)(2,1)S(1)}, u32[]{:S(2)}, u32[]{:S(2)}) collective-permute-start(bf16[256,512]{1,0:T(8,128)(2,1)S(1)} %collective-permute-done.4), channel_id=1, source_target_pairs={{0,1},{1,2},{2,3},{3,4},{4,5},{5,6},{6,7},{7,0},{8,9},{9,10},{10,1... | collective-permute-start | bytes 786440 | tf_op jit(solution)/shard_map/ppermute | solution.py:192
  71.8 10.8 %collective-permute-start.3 = (bf16[256,512]{1,0:T(8,128)(2,1)S(1)}, bf16[256,512]{1,0:T(8,128)(2,1)S(1)}, u32[]{:S(2)}, u32[]{:S(2)}) collective-permute-start(bf16[256,512]{1,0:T(8,128)(2,1)S(1)} %collective-permute-done.2), channel_id=1, source_target_pairs={{0,7},{1,0},{2,1},{3,2},{4,3},{5,4},{6,5},{7,6},{8,15},{9,8},{10,9... | collective-permute-start | bytes 786440 | tf_op jit(solution)/shard_map/ppermute | solution.py:194
  80.7 11.4 %collective-permute-start.6 = (bf16[256,512]{1,0:T(8,128)(2,1)S(1)}, bf16[256,512]{1,0:T(8,128)(2,1)S(1)}, u32[]{:S(2)}, u32[]{:S(2)}) collective-permute-start(bf16[256,512]{1,0:T(8,128)(2,1)S(1)} %collective-permute-done.5), channel_id=1, source_target_pairs={{0,1},{1,2},{2,3},{3,4},{4,5},{5,6},{6,7},{7,0},{8,9},{9,10},{10,1... | collective-permute-start | bytes 786440 | tf_op jit(solution)/shard_map/ppermute | solution.py:192
  92.1 11.9 %collective-permute-start.7 = (bf16[8,256,512]{2,1,0:T(8,128)(2,1)S(1)}, bf16[8,256,512]{2,1,0:T(8,128)(2,1)}, u32[]{:S(2)}, u32[]{:S(2)}) collective-permute-start(bf16[8,256,512]{2,1,0:T(8,128)(2,1)S(1)} %bitcast_dynamic-update-slice_fusion.own_ref), channel_id=1, source_target_pairs={{0,8},{8,0},{1,9},{9,1},{2,10},{10,2},{3,11},{11,3},{4,12},{12,4},... | collective-permute-start | bytes 6291464 | tf_op jit(solution)/shard_map/ppermute | solution.py:214
  95.4 38.6 %collective-permute-start.10 = (bf16[64,4096]{1,0:T(8,128)(2,1)}, bf16[64,4096]{1,0:T(8,128)(2,1)}, u32[]{:S(2)}, u32[]{:S(2)}) collective-permute-start(bf16[64,4096]{1,0:T(8,128)(2,1)} %reshape.19.refs_0_), channel_id=1, source_target_pairs={{0,128},{128,256},{256,384},{384,0},{1,129},{129,257},{257,385},{3... | collective-permute-start | bytes 1572872 | tf_op jit(solution)/shard_map/ppermute | solution.py:217
  97.3 36.7 %collective-permute-start.8 = (bf16[64,4096]{1,0:T(8,128)(2,1)}, bf16[64,4096]{1,0:T(8,128)(2,1)}, u32[]{:S(2)}, u32[]{:S(2)}) collective-permute-start(bf16[64,4096]{1,0:T(8,128)(2,1)} %reshape.19.refs_0_), channel_id=1, source_target_pairs={{0,384},{128,0},{256,128},{384,256},{1,385},{129,1},{257,129},{385... | collective-permute-start | bytes 1572872 | tf_op jit(solution)/shard_map/ppermute | solution.py:217
  101.9 32.2 %collective-permute-start.9 = (bf16[64,4096]{1,0:T(8,128)(2,1)}, bf16[64,4096]{1,0:T(8,128)(2,1)}, u32[]{:S(2)}, u32[]{:S(2)}) collective-permute-start(bf16[64,4096]{1,0:T(8,128)(2,1)} %reshape.19.refs_0_), channel_id=1, source_target_pairs={{0,256},{128,384},{256,0},{384,128},{1,257},{129,385},{257,1},{385... | collective-permute-start | bytes 1572872 | tf_op jit(solution)/shard_map/ppermute | solution.py:217
  109.7 16.5 %all-to-all-start.2 = ((bf16[32,8,128]{2,1,0:T(8,128)(2,1)}), bf16[32,8,128]{2,1,0:T(8,128)(2,1)S(1)}, u32[]{:S(2)}, u32[]{:S(2)}) async-start(bf16[32,8,128]{2,1,0:T(8,128)(2,1)} %get-tuple-element.16), calls=%async_computation.2 | async-start | bytes 131072 | tf_op jit(solution)/shard_map/all_to_all | solution.py:23
  126.9 15.9 %all-to-all-start.3 = ((bf16[32,8,128]{2,1,0:T(8,128)(2,1)}), bf16[32,8,128]{2,1,0:T(8,128)(2,1)S(1)}, u32[]{:S(2)}, u32[]{:S(2)}) async-start(bf16[32,8,128]{2,1,0:T(8,128)(2,1)} %shard_map.40), calls=%async_computation.3 | async-start | bytes 131072 | tf_op jit(solution)/shard_map/all_to_all | solution.py:23
  143.2 5.4 %collective-permute-start.11 = (bf16[2,256,128]{2,1,0:T(8,128)(2,1)S(1)}, bf16[2,256,128]{2,1,0:T(8,128)(2,1)S(1)}, u32[]{:S(2)}, u32[]{:S(2)}) collective-permute-start(bf16[2,256,128]{2,1,0:T(8,128)(2,1)S(1)} %slice_bitcast_fusion), channel_id=1, source_target_pairs={{0,8},{8,0},{1,9},{9,1},{2,10},{10,2},{3,11},{11,3},{4,12},{12,4},... | collective-permute-start | bytes 393224 | tf_op jit(solution)/shard_map/ppermute | solution.py:239
Sparse Core Ops, SparseCore 0:
  27.5 60.7 all-gather.1

commit v5 on v4

--- a/solution.py
+++ b/solution.py
@@ -184,16 +184,19 @@
     return jax.ShapeDtypeStruct(dims, dtype)
 
 
-def token_ring(piece, q_part):
+def token_ring(piece, q_rows):
     up = [(i, (i + 1) % NZ) for i in range(NZ)]
     down = [(i, (i - 1) % NZ) for i in range(NZ)]
     below, above = [piece], [piece]
     for hop in range(NZ // 2):
+        if hop == NZ // 2 - 1:
+            below[hop], above[hop], q_part = lax.optimization_barrier((below[hop], above[hop], q_part))
         below.append(lax.ppermute(below[-1], "z", up))
         if hop < NZ // 2 - 1:
             above.append(lax.ppermute(above[-1], "z", down))
         if hop == 0:
-            below[1], above[1], q_part = lax.optimization_barrier((below[1], above[1], q_part))
+            below[1], above[1], q_rows = lax.optimization_barrier((below[1], above[1], q_rows))
+            q_part = exchange(replicate(q_rows, NY).reshape(NY * NC, 4, D), ("y", "c"))
     return jnp.stack(above + below[:0:-1]), q_part
 
 
@@ -209,8 +212,7 @@
 
     kv_part = exchange(replicate(kv_rows, NX).reshape(NX * NC, 8, D), ("x", "c"))
     kv_weight = lax.all_gather(kv_part.reshape(64, D), "y", axis=0, tiled=True)
-    q_part = exchange(replicate(q_rows, NY).reshape(NY * NC, 4, D), ("y", "c"))
-    own, q_part = token_ring(hidden_in, q_part)
+    own, q_part = token_ring(hidden_in, q_rows)
     other = lax.ppermute(own, "c", swap)
     q_mine = q_part.reshape(64, D)
     q_weights = [q_mine] + [

time: 157 us -> 154 us (0.981)
  waiting for transfers between devices: 37.5 us -> 32.1 us
  local copies, waits for them, and re-layouts: 3.45 us -> 7.98 us
  starting transfers between devices: 69 us -> 66.1 us
    ppermute x3, starting transfers between devices: 23.7 us -> 16.3 us  [token_ring(): above.append(lax.ppermute(above[-1], 'z', down))]
    all_to_all x3, starting transfers between devices: 19.1 us -> 25.9 us  [exchange(): return lax.all_to_all(x, axes, 0, 0, tiled=True)]
    unnamed x13 -> x19, local copies, waits for them, and re-layouts: 0.15 us -> 4.66 us
    ppermute x4, waiting for transfers between devices: 21.7 us -> 17.4 us  [token_ring(): below.append(lax.ppermute(below[-1], 'z', up))]
    ppermute x4, starting transfers between devices: 10.9 us -> 8.04 us  [token_ring(): below.append(lax.ppermute(below[-1], 'z', up))]
    ppermute x1, starting transfers between devices: 2.36 us -> 4.21 us  [on_device(): other = lax.ppermute(own, 'c', swap)]
  transfers between devices with their start and end apart: 16 -> 16, of which waited for: 9 -> 9; matrix products, arithmetic and copies ran while one was open for 2% -> 4% of each run, Pallas kernels for 7% -> 8%
where the time goes in v5:
time: 154 us; the launch traced here: 153 us
  starting transfers between devices  66.1 us (43%)
  waiting for transfers between devices  32.1 us (21%)
  blocking collectives  19.3 us (13%)
  between operations  13.8 us (9%)
  Pallas kernels  11.8 us (8%)
  local copies, waits for them, and re-layouts  7.98 us (5%)
  other arithmetic  1.54 us (1%)
    all_to_all x3, starting transfers between devices, exchange(): return lax.all_to_all(x, axes, 0, 0, tiled=True)  25.9 us
    all_to_all x1, blocking collectives, exchange(): return lax.all_to_all(x, axes, 0, 0, tiled=True)  19.3 us
    ppermute x4, waiting for transfers between devices, token_ring(): below.append(lax.ppermute(below[-1], 'z', up))  17.4 us
    ppermute x3, starting transfers between devices, token_ring(): above.append(lax.ppermute(above[-1], 'z', down))  16.3 us
    all_to_all x3, waiting for transfers between devices, exchange(): return lax.all_to_all(x, axes, 0, 0, tiled=True)  12.7 us
    pallas_call x2, Pallas kernels, project(): pl.pallas_call(kernel, in_specs=[pl.BlockSpec(memory_space=pltpu.SMEM), v...  10.1 us
    ppermute x4, starting transfers between devices, token_ring(): below.append(lax.ppermute(below[-1], 'z', up))  8.04 us
    ppermute x3, starting transfers between devices, on_device(): lax.ppermute(q_mine, 'x', [(i, (i - k) % NX) for i in range(NX)])  7.8 us
  transfers between devices with their start and end apart: 16, of which 9 were waited for; matrix products, arithmetic and copies ran while one was open for 4% of the time, Pallas kernels for 8%

profile of v5, /device:TPU:1, one launch (start us, length us, event | category | flops | bytes accessed | tf_op | source)
XLA Modules:
  0.0 152.7 jit_solution(5190495218349988581)
XLA Ops:
  6.5 1.1 fusion.2
  7.9 19.3 %all_to_all.20 = bf16[8,8,4096]{2,1,0:T(8,128)(2,1)} all-to-all(bf16[8,8,4096]{2,1,0:T(8,128)(2,1)S(1)} %bitcast.42), channel_id=1, replica_groups=mesh['x'=4,'y'=8,'c'=2,'z'=8] {'x','c'}, dimensions={0} | all-to-all | bytes 1048576 | tf_op jit(solution)/shard_map/all_to_all | solution.py:23
  27.3 1.9 %collective-permute-start = (bf16[256,512]{1,0:T(8,128)(2,1)S(1)}, bf16[256,512]{1,0:T(8,128)(2,1)S(1)}, u32[]{:S(2)}, u32[]{:S(2)}) collective-permute-start(bf16[256,512]{1,0:T(8,128)(2,1)S(1)} %copy-done.2), channel_id=1, source_target_pairs={{0,1},{1,2},{2,3},{3,4},{4,5},{5,6},{6,7},{7,0},{8,9},{9,10},{10,1... | collective-permute-start | bytes 786440 | tf_op jit(solution)/shard_map/ppermute | solution.py:194
  29.2 6.4 %collective-permute-start.1 = (bf16[256,512]{1,0:T(8,128)(2,1)S(1)}, bf16[256,512]{1,0:T(8,128)(2,1)S(1)}, u32[]{:S(2)}, u32[]{:S(2)}) collective-permute-start(bf16[256,512]{1,0:T(8,128)(2,1)S(1)} %copy-done.2), channel_id=1, source_target_pairs={{0,7},{1,0},{2,1},{3,2},{4,3},{5,4},{6,5},{7,6},{8,15},{9,8},{10,9... | collective-permute-start | bytes 786440 | tf_op jit(solution)/shard_map/ppermute | solution.py:196
  35.8 3.5 %collective-permute-done = bf16[256,512]{1,0:T(8,128)(2,1)S(1)} collective-permute-done((bf16[256,512]{1,0:T(8,128)(2,1)S(1)}, bf16[256,512]{1,0:T(8,128)(2,1)S(1)}, u32[]{:S(2)}, u32[]{:S(2)}) %collective-permute-start) | collective-permute-done | bytes 262176 | tf_op jit(solution)/shard_map/ppermute | solution.py:194
  40.2 1.0 broadcast_in_dim.6
  41.3 9.1 %all-to-all-start = ((bf16[16,4,4096]{2,1,0:T(4,128)(2,1)}), bf16[16,4,4096]{2,1,0:T(4,128)(2,1)S(1)}, u32[]{:S(2)}, u32[]{:S(2)}) async-start(bf16[16,4,4096]{2,1,0:T(4,128)(2,1)} %bitcast.9), calls=%async_computation | async-start | bytes 1048576 | tf_op jit(solution)/shard_map/all_to_all | solution.py:23
  50.3 1.9 %collective-permute-start.3 = (bf16[256,512]{1,0:T(8,128)(2,1)S(1)}, bf16[256,512]{1,0:T(8,128)(2,1)S(1)}, u32[]{:S(2)}, u32[]{:S(2)}) collective-permute-start(bf16[256,512]{1,0:T(8,128)(2,1)S(1)} %collective-permute-done), channel_id=1, source_target_pairs={{0,1},{1,2},{2,3},{3,4},{4,5},{5,6},{6,7},{7,0},{8,9},{9,10},{10,1... | collective-permute-start | bytes 786440 | tf_op jit(solution)/shard_map/ppermute | solution.py:194
  52.2 5.4 %collective-permute-start.2 = (bf16[256,512]{1,0:T(8,128)(2,1)S(1)}, bf16[256,512]{1,0:T(8,128)(2,1)S(1)}, u32[]{:S(2)}, u32[]{:S(2)}) collective-permute-start(bf16[256,512]{1,0:T(8,128)(2,1)S(1)} %collective-permute-done.1), channel_id=1, source_target_pairs={{0,7},{1,0},{2,1},{3,2},{4,3},{5,4},{6,5},{7,6},{8,15},{9,8},{10,9... | collective-permute-start | bytes 786440 | tf_op jit(solution)/shard_map/ppermute | solution.py:196
  57.6 4.7 %collective-permute-done.3 = bf16[256,512]{1,0:T(8,128)(2,1)S(1)} collective-permute-done((bf16[256,512]{1,0:T(8,128)(2,1)S(1)}, bf16[256,512]{1,0:T(8,128)(2,1)S(1)}, u32[]{:S(2)}, u32[]{:S(2)}) %collective-permute-start.3) | collective-permute-done | bytes 262176 | tf_op jit(solution)/shard_map/ppermute | solution.py:194
  62.3 1.9 %collective-permute-start.4 = (bf16[256,512]{1,0:T(8,128)(2,1)S(1)}, bf16[256,512]{1,0:T(8,128)(2,1)S(1)}, u32[]{:S(2)}, u32[]{:S(2)}) collective-permute-start(bf16[256,512]{1,0:T(8,128)(2,1)S(1)} %collective-permute-done.3), channel_id=1, source_target_pairs={{0,1},{1,2},{2,3},{3,4},{4,5},{5,6},{6,7},{7,0},{8,9},{9,10},{10,1... | collective-permute-start | bytes 786440 | tf_op jit(solution)/shard_map/ppermute | solution.py:194
  64.3 4.6 %collective-permute-start.5 = (bf16[256,512]{1,0:T(8,128)(2,1)S(1)}, bf16[256,512]{1,0:T(8,128)(2,1)}, u32[]{:S(2)}, u32[]{:S(2)}) collective-permute-start(bf16[256,512]{1,0:T(8,128)(2,1)S(1)} %collective-permute-done.2), channel_id=1, source_target_pairs={{0,7},{1,0},{2,1},{3,2},{4,3},{5,4},{6,5},{7,6},{8,15},{9,8},{10,9... | collective-permute-start | bytes 786440 | tf_op jit(solution)/shard_map/ppermute | solution.py:196
  68.9 1.0 bitcast_dynamic-update-slice_fusion.6
  69.8 2.9 %collective-permute-done.4 = bf16[256,512]{1,0:T(8,128)(2,1)S(1)} collective-permute-done((bf16[256,512]{1,0:T(8,128)(2,1)S(1)}, bf16[256,512]{1,0:T(8,128)(2,1)S(1)}, u32[]{:S(2)}, u32[]{:S(2)}) %collective-permute-start.4) | collective-permute-done | bytes 262176 | tf_op jit(solution)/shard_map/ppermute | solution.py:194
  73.6 2.3 %collective-permute-start.6 = (bf16[256,512]{1,0:T(8,128)(2,1)}, bf16[256,512]{1,0:T(8,128)(2,1)S(1)}, u32[]{:S(2)}, u32[]{:S(2)}) collective-permute-start(bf16[256,512]{1,0:T(8,128)(2,1)} %copy-done.4), channel_id=1, source_target_pairs={{0,1},{1,2},{2,3},{3,4},{4,5},{5,6},{6,7},{7,0},{8,9},{9,10},{10,1... | collective-permute-start | bytes 786440 | tf_op jit(solution)/shard_map/ppermute | solution.py:194
  75.9 1.0 bitcast_dynamic-update-slice_fusion.5
  76.8 1.0 bitcast_dynamic-update-slice_fusion.4
  77.8 6.3 %collective-permute-done.6 = bf16[256,512]{1,0:T(8,128)(2,1)S(1)} collective-permute-done((bf16[256,512]{1,0:T(8,128)(2,1)}, bf16[256,512]{1,0:T(8,128)(2,1)S(1)}, u32[]{:S(2)}, u32[]{:S(2)}) %collective-permute-start.6) | collective-permute-done | bytes 262176 | tf_op jit(solution)/shard_map/ppermute | solution.py:194
  84.2 1.0 bitcast_dynamic-update-slice_fusion.2
  85.2 4.2 %collective-permute-start.7 = (bf16[8,256,512]{2,1,0:T(8,128)(2,1)S(1)}, bf16[8,256,512]{2,1,0:T(8,128)(2,1)}, u32[]{:S(2)}, u32[]{:S(2)}) collective-permute-start(bf16[8,256,512]{2,1,0:T(8,128)(2,1)S(1)} %bitcast_dynamic-update-slice_fusion.own_ref), channel_id=1, source_target_pairs={{0,8},{8,0},{1,9},{9,1},{2,10},{10,2},{3,11},{11,3},{4,12},{12,4},... | collective-permute-start | bytes 6291464 | tf_op jit(solution)/shard_map/ppermute | solution.py:216
  90.4 2.8 %collective-permute-start.8 = (bf16[64,4096]{1,0:T(8,128)(2,1)}, bf16[64,4096]{1,0:T(8,128)(2,1)}, u32[]{:S(2)}, u32[]{:S(2)}) collective-permute-start(bf16[64,4096]{1,0:T(8,128)(2,1)} %reshape.19.refs_0_), channel_id=1, source_target_pairs={{0,384},{128,0},{256,128},{384,256},{1,385},{129,1},{257,129},{385... | collective-permute-start | bytes 1572872 | tf_op jit(solution)/shard_map/ppermute | solution.py:219
  93.1 3.1 %collective-permute-start.9 = (bf16[64,4096]{1,0:T(8,128)(2,1)}, bf16[64,4096]{1,0:T(8,128)(2,1)}, u32[]{:S(2)}, u32[]{:S(2)}) collective-permute-start(bf16[64,4096]{1,0:T(8,128)(2,1)} %reshape.19.refs_0_), channel_id=1, source_target_pairs={{0,256},{128,384},{256,0},{384,128},{1,257},{129,385},{257,1},{385... | collective-permute-start | bytes 1572872 | tf_op jit(solution)/shard_map/ppermute | solution.py:219
  96.3 1.9 %collective-permute-start.10 = (bf16[64,4096]{1,0:T(8,128)(2,1)}, bf16[64,4096]{1,0:T(8,128)(2,1)}, u32[]{:S(2)}, u32[]{:S(2)}) collective-permute-start(bf16[64,4096]{1,0:T(8,128)(2,1)} %reshape.19.refs_0_), channel_id=1, source_target_pairs={{0,128},{128,256},{256,384},{384,0},{1,129},{129,257},{257,385},{3... | collective-permute-start | bytes 1572872 | tf_op jit(solution)/shard_map/ppermute | solution.py:219
  98.4 5.6 %shard_map.38 = (bf16[2,2,2,256,128]{4,3,2,1,0:T(8,128)(2,1)S(1)}, f32[2,2,128,128]{3,2,1,0:T(8,128)S(1)}, bf16[32,8,128]{2,1,0:T(8,128)(2,1)}) custom-call(s32[1]{0:T(128)} %bitcast.z_ref, bf16[8,256,512]{2,1,0:T(8,128)(2,1)S(1)} %bitcast_dynamic-update-slice_fusion.own_ref, bf16[512,512]{1,0:T(8,128)(2,1)S(1)} %fusion.order_ref, ...), custom_call_target="tpu_custom_call" | custom-call | tf_op jit(solution)/shard_map/pallas_call | solution.py:124
  104.0 9.3 %all-to-all-start.2 = ((bf16[32,8,128]{2,1,0:T(8,128)(2,1)}), bf16[32,8,128]{2,1,0:T(8,128)(2,1)S(1)}, u32[]{:S(2)}, u32[]{:S(2)}) async-start(bf16[32,8,128]{2,1,0:T(8,128)(2,1)} %get-tuple-element.22), calls=%async_computation.2 | async-start | bytes 131072 | tf_op jit(solution)/shard_map/all_to_all | solution.py:23
  113.3 9.2 %all-to-all-done.2.total_ref = bf16[32,8,128]{2,1,0:T(8,128)(2,1)S(1)} async-done(((bf16[32,8,128]{2,1,0:T(8,128)(2,1)}), bf16[32,8,128]{2,1,0:T(8,128)(2,1)S(1)}, u32[]{:S(2)}, u32[]{:S(2)}) %all-to-all-start.2) | async-done | bytes 65568 | tf_op jit(solution)/shard_map/all_to_all | solution.py:23
  123.2 7.6 %all-to-all-start.3 = ((bf16[32,8,128]{2,1,0:T(8,128)(2,1)}), bf16[32,8,128]{2,1,0:T(8,128)(2,1)S(1)}, u32[]{:S(2)}, u32[]{:S(2)}) async-start(bf16[32,8,128]{2,1,0:T(8,128)(2,1)} %shard_map.40), calls=%async_computation.3 | async-start | bytes 131072 | tf_op jit(solution)/shard_map/all_to_all | solution.py:23
  130.9 4.5 %shard_map.37.query_ref = bf16[2,2,256,128]{3,2,1,0:T(8,128)(2,1)S(1)} custom-call(s32[1]{0:T(128)} %bitcast.z_ref, bf16[8,256,512]{2,1,0:T(8,128)(2,1)S(1)} %bitcast_dynamic-update-slice_fusion.own_ref, bf16[256,256]{1,0:T(8,128)(2,1)S(1)} %fusion.1.order_ref, bf16[8,256,512]{2,1,0:T(8,128)(2,1)} %collective-permute-done.7.other_hbm, ...), custom_call_target="tpu_custom_call" | custom-call | tf_op jit(solution)/shard_map/pallas_call | solution.py:124
  136.1 3.5 %all-to-all-done.3.prior_ref = bf16[32,8,128]{2,1,0:T(8,128)(2,1)S(1)} async-done(((bf16[32,8,128]{2,1,0:T(8,128)(2,1)}), bf16[32,8,128]{2,1,0:T(8,128)(2,1)S(1)}, u32[]{:S(2)}, u32[]{:S(2)}) %all-to-all-start.3) | async-done | bytes 65568 | tf_op jit(solution)/shard_map/all_to_all | solution.py:23
  140.0 3.8 %collective-permute-start.11 = (bf16[2,256,128]{2,1,0:T(8,128)(2,1)S(1)}, bf16[2,256,128]{2,1,0:T(8,128)(2,1)S(1)}, u32[]{:S(2)}, u32[]{:S(2)}) collective-permute-start(bf16[2,256,128]{2,1,0:T(8,128)(2,1)S(1)} %slice_bitcast_fusion), channel_id=1, source_target_pairs={{0,8},{8,0},{1,9},{9,1},{2,10},{10,2},{3,11},{11,3},{4,12},{12,4},... | collective-permute-start | bytes 393224 | tf_op jit(solution)/shard_map/ppermute | solution.py:241
  143.9 1.0 collective-permute-done.11
  144.9 1.0 copy.9
  (44 shorter events, 5.2 us)
Async XLA Ops:
  6.5 29.1 %copy-start = (bf16[3,4096,2,2]{1,3,2,0:T(2,128)(2,1)S(1)}, bf16[3,4096,2,2]{1,3,2,0:T(2,128)(2,1)}, u32[]{:S(2)}) copy-start(bf16[3,4096,2,2]{1,3,2,0:T(2,128)(2,1)} %param.5) | copy-start | bytes 294916
  6.5 29.1 %copy-start.1 = (bf16[3,4096,2,2]{1,3,2,0:T(2,128)(2,1)S(1)}, bf16[3,4096,2,2]{1,3,2,0:T(2,128)(2,1)}, u32[]{:S(2)}) copy-start(bf16[3,4096,2,2]{1,3,2,0:T(2,128)(2,1)} %param.4) | copy-start | bytes 294916
  6.5 20.8 %copy-start.2 = (bf16[256,512]{1,0:T(8,128)(2,1)S(1)}, bf16[256,512]{1,0:T(8,128)(2,1)}, u32[]{:S(2)}) copy-start(bf16[256,512]{1,0:T(8,128)(2,1)} %param.3) | copy-start | bytes 786436
  6.5 91.8 %all-gather.2.cloned.1.call-start = ((), (), s32[]{:S(2)}) async-start(), calls=%async_computation.4 | async-start | bytes 4718592 | tf_op jit(solution)/shard_map/all_gather | solution.py:214
  27.3 12.0 %collective-permute-start = (bf16[256,512]{1,0:T(8,128)(2,1)S(1)}, bf16[256,512]{1,0:T(8,128)(2,1)S(1)}, u32[]{:S(2)}, u32[]{:S(2)}) collective-permute-start(bf16[256,512]{1,0:T(8,128)(2,1)S(1)} %copy-done.2), channel_id=1, source_target_pairs={{0,1},{1,2},{2,3},{3,4},{4,5},{5,6},{6,7},{7,0},{8,9},{9,10},{10,1... | collective-permute-start | bytes 786440 | tf_op jit(solution)/shard_map/ppermute | solution.py:194
  29.2 10.9 %collective-permute-start.1 = (bf16[256,512]{1,0:T(8,128)(2,1)S(1)}, bf16[256,512]{1,0:T(8,128)(2,1)S(1)}, u32[]{:S(2)}, u32[]{:S(2)}) collective-permute-start(bf16[256,512]{1,0:T(8,128)(2,1)S(1)} %copy-done.2), channel_id=1, source_target_pairs={{0,7},{1,0},{2,1},{3,2},{4,3},{5,4},{6,5},{7,6},{8,15},{9,8},{10,9... | collective-permute-start | bytes 786440 | tf_op jit(solution)/shard_map/ppermute | solution.py:196
  40.2 24.1 %copy-start.3 = (bf16[256,512]{1,0:T(8,128)(2,1)}, bf16[256,512]{1,0:T(8,128)(2,1)S(1)}, u32[]{:S(2)}) copy-start(bf16[256,512]{1,0:T(8,128)(2,1)S(1)} %collective-permute-done.1) | copy-start | bytes 786436
  41.3 32.3 %all-to-all-start = ((bf16[16,4,4096]{2,1,0:T(4,128)(2,1)}), bf16[16,4,4096]{2,1,0:T(4,128)(2,1)S(1)}, u32[]{:S(2)}, u32[]{:S(2)}) async-start(bf16[16,4,4096]{2,1,0:T(4,128)(2,1)} %bitcast.9), calls=%async_computation | async-start | bytes 1048576 | tf_op jit(solution)/shard_map/all_to_all | solution.py:23
  50.3 12.0 %collective-permute-start.3 = (bf16[256,512]{1,0:T(8,128)(2,1)S(1)}, bf16[256,512]{1,0:T(8,128)(2,1)S(1)}, u32[]{:S(2)}, u32[]{:S(2)}) collective-permute-start(bf16[256,512]{1,0:T(8,128)(2,1)S(1)} %collective-permute-done), channel_id=1, source_target_pairs={{0,1},{1,2},{2,3},{3,4},{4,5},{5,6},{6,7},{7,0},{8,9},{9,10},{10,1... | collective-permute-start | bytes 786440 | tf_op jit(solution)/shard_map/ppermute | solution.py:194
  52.2 12.0 %collective-permute-start.2 = (bf16[256,512]{1,0:T(8,128)(2,1)S(1)}, bf16[256,512]{1,0:T(8,128)(2,1)S(1)}, u32[]{:S(2)}, u32[]{:S(2)}) collective-permute-start(bf16[256,512]{1,0:T(8,128)(2,1)S(1)} %collective-permute-done.1), channel_id=1, source_target_pairs={{0,7},{1,0},{2,1},{3,2},{4,3},{5,4},{6,5},{7,6},{8,15},{9,8},{10,9... | collective-permute-start | bytes 786440 | tf_op jit(solution)/shard_map/ppermute | solution.py:196
  62.3 10.5 %collective-permute-start.4 = (bf16[256,512]{1,0:T(8,128)(2,1)S(1)}, bf16[256,512]{1,0:T(8,128)(2,1)S(1)}, u32[]{:S(2)}, u32[]{:S(2)}) collective-permute-start(bf16[256,512]{1,0:T(8,128)(2,1)S(1)} %collective-permute-done.3), channel_id=1, source_target_pairs={{0,1},{1,2},{2,3},{3,4},{4,5},{5,6},{6,7},{7,0},{8,9},{9,10},{10,1... | collective-permute-start | bytes 786440 | tf_op jit(solution)/shard_map/ppermute | solution.py:194
  64.2 8.5 %copy-start.5 = (bf16[256,512]{1,0:T(8,128)(2,1)}, bf16[256,512]{1,0:T(8,128)(2,1)S(1)}, u32[]{:S(2)}) copy-start(bf16[256,512]{1,0:T(8,128)(2,1)S(1)} %collective-permute-done.2) | copy-start | bytes 786436
  64.3 9.3 %collective-permute-start.5 = (bf16[256,512]{1,0:T(8,128)(2,1)S(1)}, bf16[256,512]{1,0:T(8,128)(2,1)}, u32[]{:S(2)}, u32[]{:S(2)}) collective-permute-start(bf16[256,512]{1,0:T(8,128)(2,1)S(1)} %collective-permute-done.2), channel_id=1, source_target_pairs={{0,7},{1,0},{2,1},{3,2},{4,3},{5,4},{6,5},{7,6},{8,15},{9,8},{10,9... | collective-permute-start | bytes 786440 | tf_op jit(solution)/shard_map/ppermute | solution.py:196
  72.8 0.7 copy-start.4
  73.6 10.6 %collective-permute-start.6 = (bf16[256,512]{1,0:T(8,128)(2,1)}, bf16[256,512]{1,0:T(8,128)(2,1)S(1)}, u32[]{:S(2)}, u32[]{:S(2)}) collective-permute-start(bf16[256,512]{1,0:T(8,128)(2,1)} %copy-done.4), channel_id=1, source_target_pairs={{0,1},{1,2},{2,3},{3,4},{4,5},{5,6},{6,7},{7,0},{8,9},{9,10},{10,1... | collective-permute-start | bytes 786440 | tf_op jit(solution)/shard_map/ppermute | solution.py:194
  85.2 13.1 %collective-permute-start.7 = (bf16[8,256,512]{2,1,0:T(8,128)(2,1)S(1)}, bf16[8,256,512]{2,1,0:T(8,128)(2,1)}, u32[]{:S(2)}, u32[]{:S(2)}) collective-permute-start(bf16[8,256,512]{2,1,0:T(8,128)(2,1)S(1)} %bitcast_dynamic-update-slice_fusion.own_ref), channel_id=1, source_target_pairs={{0,8},{8,0},{1,9},{9,1},{2,10},{10,2},{3,11},{11,3},{4,12},{12,4},... | collective-permute-start | bytes 6291464 | tf_op jit(solution)/shard_map/ppermute | solution.py:216
  90.4 40.5 %collective-permute-start.8 = (bf16[64,4096]{1,0:T(8,128)(2,1)}, bf16[64,4096]{1,0:T(8,128)(2,1)}, u32[]{:S(2)}, u32[]{:S(2)}) collective-permute-start(bf16[64,4096]{1,0:T(8,128)(2,1)} %reshape.19.refs_0_), channel_id=1, source_target_pairs={{0,384},{128,0},{256,128},{384,256},{1,385},{129,1},{257,129},{385... | collective-permute-start | bytes 1572872 | tf_op jit(solution)/shard_map/ppermute | solution.py:219
  93.1 37.7 %collective-permute-start.9 = (bf16[64,4096]{1,0:T(8,128)(2,1)}, bf16[64,4096]{1,0:T(8,128)(2,1)}, u32[]{:S(2)}, u32[]{:S(2)}) collective-permute-start(bf16[64,4096]{1,0:T(8,128)(2,1)} %reshape.19.refs_0_), channel_id=1, source_target_pairs={{0,256},{128,384},{256,0},{384,128},{1,257},{129,385},{257,1},{385... | collective-permute-start | bytes 1572872 | tf_op jit(solution)/shard_map/ppermute | solution.py:219
  96.3 34.7 %collective-permute-start.10 = (bf16[64,4096]{1,0:T(8,128)(2,1)}, bf16[64,4096]{1,0:T(8,128)(2,1)}, u32[]{:S(2)}, u32[]{:S(2)}) collective-permute-start(bf16[64,4096]{1,0:T(8,128)(2,1)} %reshape.19.refs_0_), channel_id=1, source_target_pairs={{0,128},{128,256},{256,384},{384,0},{1,129},{129,257},{257,385},{3... | collective-permute-start | bytes 1572872 | tf_op jit(solution)/shard_map/ppermute | solution.py:219
  104.0 18.5 %all-to-all-start.2 = ((bf16[32,8,128]{2,1,0:T(8,128)(2,1)}), bf16[32,8,128]{2,1,0:T(8,128)(2,1)S(1)}, u32[]{:S(2)}, u32[]{:S(2)}) async-start(bf16[32,8,128]{2,1,0:T(8,128)(2,1)} %get-tuple-element.22), calls=%async_computation.2 | async-start | bytes 131072 | tf_op jit(solution)/shard_map/all_to_all | solution.py:23
  123.2 16.5 %all-to-all-start.3 = ((bf16[32,8,128]{2,1,0:T(8,128)(2,1)}), bf16[32,8,128]{2,1,0:T(8,128)(2,1)S(1)}, u32[]{:S(2)}, u32[]{:S(2)}) async-start(bf16[32,8,128]{2,1,0:T(8,128)(2,1)} %shard_map.40), calls=%async_computation.3 | async-start | bytes 131072 | tf_op jit(solution)/shard_map/all_to_all | solution.py:23
  140.0 4.8 %collective-permute-start.11 = (bf16[2,256,128]{2,1,0:T(8,128)(2,1)S(1)}, bf16[2,256,128]{2,1,0:T(8,128)(2,1)S(1)}, u32[]{:S(2)}, u32[]{:S(2)}) collective-permute-start(bf16[2,256,128]{2,1,0:T(8,128)(2,1)S(1)} %slice_bitcast_fusion), channel_id=1, source_target_pairs={{0,8},{8,0},{1,9},{9,1},{2,10},{10,2},{3,11},{11,3},{4,12},{12,4},... | collective-permute-start | bytes 393224 | tf_op jit(solution)/shard_map/ppermute | solution.py:241
Sparse Core Ops, SparseCore 0:
  27.4 67.2 all-gather.1

commit v6 on v4

--- a/solution.py
+++ b/solution.py
@@ -23,7 +23,7 @@
     return lax.all_to_all(x, axes, 0, 0, tiled=True)
 
 
-def column_order(kinds, first_x=None):
+def column_order(kinds, first_x=None, first_core=None):
     cols = kinds * 2 * HD
     row = lax.broadcasted_iota(jnp.int32, (cols, cols), 0)
     col = lax.broadcasted_iota(jnp.int32, (cols, cols), 1)
@@ -37,6 +37,7 @@
         chip = (chip & (NX - 1)) * NY + (chip >> 2)
     else:
         chip = (chip + first_x * NY) & (NX * NY - 1)
+        core = core ^ first_core
     target = (kind * 2 + sign) * HD + (chip * 2 + core) * 2 + j
     return (col == target).astype(BF16)
 
@@ -59,17 +60,16 @@
 PER = NZ // CHUNKS
 
 
-def multiply(z_ref, own_ref, other_hbm, weights_hbm, other, weight, acc, sem):
+def multiply(own_ref, other_hbm, weights_hbm, other, weight, acc, sem):
     copies = []
     for k in range(NZ):
-        start = pl.multiple_of(((z_ref[0] + k) & (NZ - 1)) * PIECE, PIECE)
         columns = pl.ds((k % PER) * PIECE, PIECE)
         group = [pltpu.make_async_copy(other_hbm.at[k], other.at[k], sem.at[k, 0])]
         for i, part in enumerate(weights_hbm):
             rows = part.shape[0]
             group.append(
                 pltpu.make_async_copy(
-                    part.at[:, pl.ds(start, PIECE)],
+                    part.at[:, pl.ds(k * PIECE, PIECE)],
                     weight.at[k // PER, pl.ds(i * rows, rows), columns],
                     sem.at[k, i + 1],
                 )
@@ -92,18 +92,18 @@
             acc[...] += part
 
 
-def query_kernel(z_ref, own_ref, order_ref, other_hbm, *refs):
+def query_kernel(own_ref, order_ref, other_hbm, *refs):
     weights_hbm, (out_ref, other, weight, acc, sem) = refs[:-5], refs[-5:]
-    multiply(z_ref, own_ref, other_hbm, weights_hbm, other, weight, acc, sem)
+    multiply(own_ref, other_hbm, weights_hbm, other, weight, acc, sem)
     rows = signs_and_order(acc[...], order_ref[...])
     for block in range(2):
         for s in range(2):
             out_ref[block, s] = rows[block * TOK : (block + 1) * TOK, s * HD : (s + 1) * HD]
 
 
-def key_value_kernel(z_ref, own_ref, order_ref, other_hbm, *refs):
+def key_value_kernel(own_ref, order_ref, other_hbm, *refs):
     weights_hbm, (out_ref, state_ref, total_ref, other, weight, acc, sem) = refs[:-7], refs[-7:]
-    multiply(z_ref, own_ref, other_hbm, weights_hbm, other, weight, acc, sem)
+    multiply(own_ref, other_hbm, weights_hbm, other, weight, acc, sem)
     rows = signs_and_order(acc[...], order_ref[...])
     for s in range(2):
         for block in range(2):
@@ -117,13 +117,13 @@
         total_ref[s * NX * NY // 2 : (s + 1) * NX * NY // 2] = total.astype(BF16)
 
 
-def project(kernel, z, own, other, weights, order, out_shape):
+def project(kernel, own, other, weights, order, out_shape):
     rows = sum(weight.shape[0] for weight in weights)
     vmem = pl.BlockSpec(memory_space=pltpu.VMEM)
     far = [pltpu.with_memory_space_constraint(a, pltpu.HBM) for a in (other, *weights)]
     return pl.pallas_call(
         kernel,
-        in_specs=[pl.BlockSpec(memory_space=pltpu.SMEM), vmem, vmem]
+        in_specs=[vmem, vmem]
         + [pl.BlockSpec(memory_space=pltpu.HBM)] * len(far),
         out_specs=jax.tree.map(lambda s: vmem, out_shape),
         scratch_shapes=[
@@ -134,7 +134,7 @@
         ],
         out_shape=out_shape,
         compiler_params=pltpu.CompilerParams(vmem_limit_bytes=24 << 20),
-    )(z, own, order, *far)
+    )(own, order, *far)
 
 
 def prefix_kernel(total_ref, out_ref):
@@ -184,21 +184,8 @@
     return jax.ShapeDtypeStruct(dims, dtype)
 
 
-def token_ring(piece, q_part):
-    up = [(i, (i + 1) % NZ) for i in range(NZ)]
-    down = [(i, (i - 1) % NZ) for i in range(NZ)]
-    below, above = [piece], [piece]
-    for hop in range(NZ // 2):
-        below.append(lax.ppermute(below[-1], "z", up))
-        if hop < NZ // 2 - 1:
-            above.append(lax.ppermute(above[-1], "z", down))
-        if hop == 0:
-            below[1], above[1], q_part = lax.optimization_barrier((below[1], above[1], q_part))
-    return jnp.stack(above + below[:0:-1]), q_part
-
-
 def on_device(hidden_in, proj_weights, directions):
-    x, c, z = (lax.axis_index(name) for name in "xcz")
+    x, c = lax.axis_index("x"), lax.axis_index("c")
     swap = [(0, 1), (1, 0)]
 
     both = jnp.stack(
@@ -209,21 +196,23 @@
 
     kv_part = exchange(replicate(kv_rows, NX).reshape(NX * NC, 8, D), ("x", "c"))
     kv_weight = lax.all_gather(kv_part.reshape(64, D), "y", axis=0, tiled=True)
-    q_part = exchange(replicate(q_rows, NY).reshape(NY * NC, 4, D), ("y", "c"))
-    own, q_part = token_ring(hidden_in, q_part)
+    own = exchange(replicate(hidden_in, NZ), "z")
+
+    q_first, q_second = q_rows[0], q_rows[1]
+    q_mine = jnp.where(c == 0, q_first, q_second)
+    q_theirs = lax.ppermute(jnp.where(c == 0, q_second, q_first), "c", swap)
+    q_part = lax.all_gather(jnp.concatenate([q_mine, q_theirs]), "y", axis=0, tiled=True)
+    q_weights = [q_part] + [
+        lax.ppermute(q_part, "x", [(i, (i - k) % NX) for i in range(NX)]) for k in range(1, NX)
+    ]
+    own, q_weights = lax.optimization_barrier((own, q_weights))
     other = lax.ppermute(own, "c", swap)
-    q_mine = q_part.reshape(64, D)
-    q_weights = [q_mine] + [
-        lax.ppermute(q_mine, "x", [(i, (i - k) % NX) for i in range(NX)]) for k in range(1, NX)
-    ]
-
-    where = z.astype(jnp.int32).reshape(1)
+
     query = project(
-        query_kernel, where, own, other, q_weights, column_order(1, x), shape(2, 2, TOK, HD)
+        query_kernel, own, other, q_weights, column_order(1, x, c), shape(2, 2, TOK, HD)
     )
     kv, state, total = project(
         key_value_kernel,
-        where,
         own,
         other,
         [kv_weight],

time: 157 us -> 151 us (0.962)
  starting transfers between devices: 69 us -> 35 us
  blocking collectives: 19.4 us -> 44.3 us
  waiting for transfers between devices: 37.5 us -> 40.1 us
    ppermute x10 -> x4, starting transfers between devices: 43.1 us -> 11.3 us  [the longest x3 8.05 us: on_device(): lax.ppermute(q_part, 'x', [(i, (i - k) % NX) for i in range(NX)])]
    all_gather x0 -> x1, blocking collectives: none -> 25 us  [on_device(): lax.all_gather(jnp.concatenate([q_mine, q_theirs]), 'y', axis=0, tiled=True)]
    ppermute x1, waiting for transfers between devices: 0.01 us -> 3.72 us  [on_device(): other = lax.ppermute(own, 'c', swap)]
    all_to_all x3, starting transfers between devices: 19.1 us -> 16.1 us  [exchange(): return lax.all_to_all(x, axes, 0, 0, tiled=True)]
    ppermute x10 -> x4, waiting for transfers between devices: 22.6 us -> 22.9 us  [the longest x3 22.1 us: on_device(): lax.ppermute(q_part, 'x', [(i, (i - k) % NX) for i in range(NX)])]
  transfers between devices with their start and end apart: 16 -> 10, of which waited for: 9 -> 8; matrix products, arithmetic and copies ran while one was open for 2% -> 1% of each run, Pallas kernels for 7% -> 3%
where the time goes in v6:
time: 151 us; the launch traced here: 150 us
  blocking collectives  44.3 us (29%)
  waiting for transfers between devices  40.1 us (27%)
  starting transfers between devices  35 us (23%)
  between operations  13.6 us (9%)
  Pallas kernels  11.8 us (8%)
  local copies, waits for them, and re-layouts  3.66 us (2%)
  other arithmetic  1.62 us (1%)
    all_gather x1, blocking collectives, on_device(): lax.all_gather(jnp.concatenate([q_mine, q_theirs]), 'y', axis=0, tiled=True)  25 us
    ppermute x3, waiting for transfers between devices, on_device(): lax.ppermute(q_part, 'x', [(i, (i - k) % NX) for i in range(NX)])  22.1 us
    all_to_all x1, blocking collectives, exchange(): return lax.all_to_all(x, axes, 0, 0, tiled=True)  19.3 us
    all_to_all x3, starting transfers between devices, exchange(): return lax.all_to_all(x, axes, 0, 0, tiled=True)  16.1 us
    all_to_all x3, waiting for transfers between devices, exchange(): return lax.all_to_all(x, axes, 0, 0, tiled=True)  12.5 us
    pallas_call x2, Pallas kernels, project(): pl.pallas_call(kernel, in_specs=[vmem, vmem] + [pl.BlockSpec(memory_space...  10.1 us
    ppermute x3, starting transfers between devices, on_device(): lax.ppermute(q_part, 'x', [(i, (i - k) % NX) for i in range(NX)])  8.05 us
    ppermute x1, starting transfers between devices, on_device(): mine, theirs = (out[0], lax.ppermute(out[1], 'c', swap))  4.82 us
  transfers between devices with their start and end apart: 10, of which 8 were waited for; matrix products, arithmetic and copies ran while one was open for 1% of the time, Pallas kernels for 3%

profile of v6, /device:TPU:1, one launch (start us, length us, event | category | flops | bytes accessed | tf_op | source)
XLA Modules:
  0.0 150.1 jit_solution(1205797370110191488)
XLA Ops:
  6.5 1.1 fusion.2
  7.6 0.1 copy.5
  7.9 19.3 %all_to_all.20 = bf16[8,8,4096]{2,1,0:T(8,128)(2,1)} all-to-all(bf16[8,8,4096]{2,1,0:T(8,128)(2,1)S(1)} %bitcast.27), channel_id=1, replica_groups=mesh['x'=4,'y'=8,'c'=2,'z'=8] {'x','c'}, dimensions={0} | all-to-all | bytes 1048576 | tf_op jit(solution)/shard_map/all_to_all | solution.py:23
  27.3 1.5 %broadcast_in_dim.6 = bf16[8,256,512]{2,1,0:T(8,128)(2,1)} broadcast(bf16[256,512]{1,0:T(8,128)(2,1)S(1)} %copy-done.5), dimensions={1,2} | broadcast | bytes 2359296 | tf_op jit(solution)/shard_map/broadcast_in_dim | solution.py:19
  28.8 5.9 %all-to-all-start = ((bf16[8,256,512]{2,1,0:T(8,128)(2,1)}), bf16[8,256,512]{2,1,0:T(8,128)(2,1)S(1)}, u32[]{:S(2)}, u32[]{:S(2)}) async-start(bf16[8,256,512]{2,1,0:T(8,128)(2,1)} %broadcast_in_dim.6), calls=%async_computation | async-start | bytes 4194304 | tf_op jit(solution)/shard_map/all_to_all | solution.py:23
  34.7 0.1 broadcast_select_fusion.1
  34.9 3.2 %collective-permute-start = (bf16[4,4096]{1,0:T(4,128)(2,1)S(1)}, bf16[4,4096]{1,0:T(4,128)(2,1)S(1)}, u32[]{:S(2)}, u32[]{:S(2)}) collective-permute-start(bf16[4,4096]{1,0:T(4,128)(2,1)S(1)} %select_n.35), channel_id=1, source_target_pairs={{0,8},{8,0},{1,9},{9,1},{2,10},{10,2},{3,11},{11,3},{4,12},{12,4},... | collective-permute-start | bytes 98312 | tf_op jit(solution)/shard_map/ppermute | solution.py:203
  38.2 0.8 collective-permute-done
  39.0 25.0 %all_gather.6.refs_0_ = bf16[64,4096]{1,0:T(8,128)(2,1)S(1)} all-gather(bf16[8,4096]{1,0:T(8,128)(2,1)S(1)} %pad_maximum_fusion.2), channel_id=1, replica_groups=mesh['x'=4,'y'=8,'c'=2,'z'=8] {'y'}, dimensions={0}, use_global_device_ids=true | all-gather | bytes 589824 | tf_op jit(solution)/shard_map/all_gather | solution.py:204
  64.0 2.9 %collective-permute-start.1 = (bf16[64,4096]{1,0:T(8,128)(2,1)S(1)}, bf16[64,4096]{1,0:T(8,128)(2,1)S(1)}, u32[]{:S(2)}, u32[]{:S(2)}) collective-permute-start(bf16[64,4096]{1,0:T(8,128)(2,1)S(1)} %all_gather.6.refs_0_), channel_id=1, source_target_pairs={{0,384},{128,0},{256,128},{384,256},{1,385},{129,1},{257,129},{385... | collective-permute-start | bytes 1572872 | tf_op jit(solution)/shard_map/ppermute | solution.py:206
  66.9 3.3 %collective-permute-start.2 = (bf16[64,4096]{1,0:T(8,128)(2,1)S(1)}, bf16[64,4096]{1,0:T(8,128)(2,1)S(1)}, u32[]{:S(2)}, u32[]{:S(2)}) collective-permute-start(bf16[64,4096]{1,0:T(8,128)(2,1)S(1)} %all_gather.6.refs_0_), channel_id=1, source_target_pairs={{0,256},{128,384},{256,0},{384,128},{1,257},{129,385},{257,1},{385... | collective-permute-start | bytes 1572872 | tf_op jit(solution)/shard_map/ppermute | solution.py:206
  70.1 1.9 %collective-permute-start.3 = (bf16[64,4096]{1,0:T(8,128)(2,1)S(1)}, bf16[64,4096]{1,0:T(8,128)(2,1)}, u32[]{:S(2)}, u32[]{:S(2)}) collective-permute-start(bf16[64,4096]{1,0:T(8,128)(2,1)S(1)} %all_gather.6.refs_0_), channel_id=1, source_target_pairs={{0,128},{128,256},{256,384},{384,0},{1,129},{129,257},{257,385},{3... | collective-permute-start | bytes 1572872 | tf_op jit(solution)/shard_map/ppermute | solution.py:206
  72.1 3.3 %collective-permute-done.1.refs_1_ = bf16[64,4096]{1,0:T(8,128)(2,1)S(1)} collective-permute-done((bf16[64,4096]{1,0:T(8,128)(2,1)S(1)}, bf16[64,4096]{1,0:T(8,128)(2,1)S(1)}, u32[]{:S(2)}, u32[]{:S(2)}) %collective-permute-start.1) | collective-permute-done | bytes 524320 | tf_op jit(solution)/shard_map/ppermute | solution.py:206
  75.4 4.3 %collective-permute-done.2.refs_2_ = bf16[64,4096]{1,0:T(8,128)(2,1)S(1)} collective-permute-done((bf16[64,4096]{1,0:T(8,128)(2,1)S(1)}, bf16[64,4096]{1,0:T(8,128)(2,1)S(1)}, u32[]{:S(2)}, u32[]{:S(2)}) %collective-permute-start.2) | collective-permute-done | bytes 524320 | tf_op jit(solution)/shard_map/ppermute | solution.py:206
  79.6 0.8 copy-done.2
  80.5 14.5 %collective-permute-done.3.refs_3_ = bf16[64,4096]{1,0:T(8,128)(2,1)} collective-permute-done((bf16[64,4096]{1,0:T(8,128)(2,1)S(1)}, bf16[64,4096]{1,0:T(8,128)(2,1)}, u32[]{:S(2)}, u32[]{:S(2)}) %collective-permute-start.3) | collective-permute-done | bytes 524320 | tf_op jit(solution)/shard_map/ppermute | solution.py:206
  95.0 2.9 %collective-permute-start.4 = (bf16[8,256,512]{2,1,0:T(8,128)(2,1)S(1)}, bf16[8,256,512]{2,1,0:T(8,128)(2,1)}, u32[]{:S(2)}, u32[]{:S(2)}) collective-permute-start(bf16[8,256,512]{2,1,0:T(8,128)(2,1)S(1)} %all-to-all-done.own_ref), channel_id=1, source_target_pairs={{0,8},{8,0},{1,9},{9,1},{2,10},{10,2},{3,11},{11,3},{4,12},{12,4},... | collective-permute-start | bytes 6291464 | tf_op jit(solution)/shard_map/ppermute | solution.py:209
  97.9 0.2 fusion.order_ref
  98.0 3.7 %collective-permute-done.4.other_hbm = bf16[8,256,512]{2,1,0:T(8,128)(2,1)} collective-permute-done((bf16[8,256,512]{2,1,0:T(8,128)(2,1)S(1)}, bf16[8,256,512]{2,1,0:T(8,128)(2,1)}, u32[]{:S(2)}, u32[]{:S(2)}) %collective-permute-start.4) | collective-permute-done | bytes 2097184 | tf_op jit(solution)/shard_map/ppermute | solution.py:209
  101.8 5.6 %shard_map.38 = (bf16[2,2,2,256,128]{4,3,2,1,0:T(8,128)(2,1)S(1)}, f32[2,2,128,128]{3,2,1,0:T(8,128)S(1)}, bf16[32,8,128]{2,1,0:T(8,128)(2,1)}) custom-call(bf16[8,256,512]{2,1,0:T(8,128)(2,1)S(1)} %all-to-all-done.own_ref, bf16[512,512]{1,0:T(8,128)(2,1)S(1)} %fusion.order_ref, bf16[8,256,512]{2,1,0:T(8,128)(2,1)} %collective-permute-done.4.other_hbm, ...), custom_call_target="tpu_custom_call" | custom-call | tf_op jit(solution)/shard_map/pallas_call | solution.py:124
  107.4 6.3 %all-to-all-start.2 = ((bf16[32,8,128]{2,1,0:T(8,128)(2,1)}), bf16[32,8,128]{2,1,0:T(8,128)(2,1)S(1)}, u32[]{:S(2)}, u32[]{:S(2)}) async-start(bf16[32,8,128]{2,1,0:T(8,128)(2,1)} %get-tuple-element.20), calls=%async_computation.2 | async-start | bytes 131072 | tf_op jit(solution)/shard_map/all_to_all | solution.py:23
  113.7 8.9 %all-to-all-done.2.total_ref = bf16[32,8,128]{2,1,0:T(8,128)(2,1)S(1)} async-done(((bf16[32,8,128]{2,1,0:T(8,128)(2,1)}), bf16[32,8,128]{2,1,0:T(8,128)(2,1)S(1)}, u32[]{:S(2)}, u32[]{:S(2)}) %all-to-all-start.2) | async-done | bytes 65568 | tf_op jit(solution)/shard_map/all_to_all | solution.py:23
  122.7 0.7 shard_map.40
  123.3 3.9 %all-to-all-start.3 = ((bf16[32,8,128]{2,1,0:T(8,128)(2,1)}), bf16[32,8,128]{2,1,0:T(8,128)(2,1)S(1)}, u32[]{:S(2)}, u32[]{:S(2)}) async-start(bf16[32,8,128]{2,1,0:T(8,128)(2,1)} %shard_map.40), calls=%async_computation.3 | async-start | bytes 131072 | tf_op jit(solution)/shard_map/all_to_all | solution.py:23
  127.2 0.1 fusion.1.order_ref
  127.3 4.5 %shard_map.37.query_ref = bf16[2,2,256,128]{3,2,1,0:T(8,128)(2,1)S(1)} custom-call(bf16[8,256,512]{2,1,0:T(8,128)(2,1)S(1)} %all-to-all-done.own_ref, bf16[256,256]{1,0:T(8,128)(2,1)S(1)} %fusion.1.order_ref, bf16[8,256,512]{2,1,0:T(8,128)(2,1)} %collective-permute-done.4.other_hbm, bf16[64,4096]{1,0:T(8,128)(2,1)} %copy-done, bf16[64,4096]{1,0:T(8,128)(2,1)} %copy-done.1, ...), custom_call_target="tpu_custom_call" | custom-call | tf_op jit(solution)/shard_map/pallas_call | solution.py:124
  131.8 0.7 shard_map.39.inner_ref
  132.5 3.6 %all-to-all-done.3.prior_ref = bf16[32,8,128]{2,1,0:T(8,128)(2,1)S(1)} async-done(((bf16[32,8,128]{2,1,0:T(8,128)(2,1)}), bf16[32,8,128]{2,1,0:T(8,128)(2,1)S(1)}, u32[]{:S(2)}, u32[]{:S(2)}) %all-to-all-start.3) | async-done | bytes 65568 | tf_op jit(solution)/shard_map/all_to_all | solution.py:23
  136.0 0.4 shard_map.41
  136.4 4.8 %collective-permute-start.5 = (bf16[2,256,128]{2,1,0:T(8,128)(2,1)S(1)}, bf16[2,256,128]{2,1,0:T(8,128)(2,1)S(1)}, u32[]{:S(2)}, u32[]{:S(2)}) collective-permute-start(bf16[2,256,128]{2,1,0:T(8,128)(2,1)S(1)} %slice_bitcast_fusion), channel_id=1, source_target_pairs={{0,8},{8,0},{1,9},{9,1},{2,10},{10,2},{3,11},{11,3},{4,12},{12,4},... | collective-permute-start | bytes 393224 | tf_op jit(solution)/shard_map/ppermute | solution.py:228
  141.3 1.0 collective-permute-done.5
  142.3 1.0 copy.7
  (26 shorter events, 0.4 us)
Async XLA Ops:
  6.5 20.7 %copy-start.5 = (bf16[256,512]{1,0:T(8,128)(2,1)S(1)}, bf16[256,512]{1,0:T(8,128)(2,1)}, u32[]{:S(2)}) copy-start(bf16[256,512]{1,0:T(8,128)(2,1)} %param.3) | copy-start | bytes 786436
  6.5 95.2 %all-gather.2.cloned.1.call-start = ((), (), s32[]{:S(2)}) async-start(), calls=%async_computation.4 | async-start | bytes 4718592 | tf_op jit(solution)/shard_map/all_gather | solution.py:198
  28.8 5.9 %copy-start.3 = (bf16[3,4096,2,2]{1,3,2,0:T(2,128)(2,1)S(1)}, bf16[3,4096,2,2]{1,3,2,0:T(2,128)(2,1)}, u32[]{:S(2)}) copy-start(bf16[3,4096,2,2]{1,3,2,0:T(2,128)(2,1)} %param.5) | copy-start | bytes 294916
  28.8 5.9 %copy-start.4 = (bf16[3,4096,2,2]{1,3,2,0:T(2,128)(2,1)S(1)}, bf16[3,4096,2,2]{1,3,2,0:T(2,128)(2,1)}, u32[]{:S(2)}) copy-start(bf16[3,4096,2,2]{1,3,2,0:T(2,128)(2,1)} %param.4) | copy-start | bytes 294916
  28.8 66.2 %all-to-all-start = ((bf16[8,256,512]{2,1,0:T(8,128)(2,1)}), bf16[8,256,512]{2,1,0:T(8,128)(2,1)S(1)}, u32[]{:S(2)}, u32[]{:S(2)}) async-start(bf16[8,256,512]{2,1,0:T(8,128)(2,1)} %broadcast_in_dim.6), calls=%async_computation | async-start | bytes 4194304 | tf_op jit(solution)/shard_map/all_to_all | solution.py:23
  34.9 4.1 %collective-permute-start = (bf16[4,4096]{1,0:T(4,128)(2,1)S(1)}, bf16[4,4096]{1,0:T(4,128)(2,1)S(1)}, u32[]{:S(2)}, u32[]{:S(2)}) collective-permute-start(bf16[4,4096]{1,0:T(4,128)(2,1)S(1)} %select_n.35), channel_id=1, source_target_pairs={{0,8},{8,0},{1,9},{9,1},{2,10},{10,2},{3,11},{11,3},{4,12},{12,4},... | collective-permute-start | bytes 98312 | tf_op jit(solution)/shard_map/ppermute | solution.py:203
  64.0 15.6 %copy-start = (bf16[64,4096]{1,0:T(8,128)(2,1)}, bf16[64,4096]{1,0:T(8,128)(2,1)S(1)}, u32[]{:S(2)}) copy-start(bf16[64,4096]{1,0:T(8,128)(2,1)S(1)} %all_gather.6.refs_0_) | copy-start | bytes 1572868
  64.0 11.4 %collective-permute-start.1 = (bf16[64,4096]{1,0:T(8,128)(2,1)S(1)}, bf16[64,4096]{1,0:T(8,128)(2,1)S(1)}, u32[]{:S(2)}, u32[]{:S(2)}) collective-permute-start(bf16[64,4096]{1,0:T(8,128)(2,1)S(1)} %all_gather.6.refs_0_), channel_id=1, source_target_pairs={{0,384},{128,0},{256,128},{384,256},{1,385},{129,1},{257,129},{385... | collective-permute-start | bytes 1572872 | tf_op jit(solution)/shard_map/ppermute | solution.py:206
  66.9 12.8 %collective-permute-start.2 = (bf16[64,4096]{1,0:T(8,128)(2,1)S(1)}, bf16[64,4096]{1,0:T(8,128)(2,1)S(1)}, u32[]{:S(2)}, u32[]{:S(2)}) collective-permute-start(bf16[64,4096]{1,0:T(8,128)(2,1)S(1)} %all_gather.6.refs_0_), channel_id=1, source_target_pairs={{0,256},{128,384},{256,0},{384,128},{1,257},{129,385},{257,1},{385... | collective-permute-start | bytes 1572872 | tf_op jit(solution)/shard_map/ppermute | solution.py:206
  70.1 24.9 %collective-permute-start.3 = (bf16[64,4096]{1,0:T(8,128)(2,1)S(1)}, bf16[64,4096]{1,0:T(8,128)(2,1)}, u32[]{:S(2)}, u32[]{:S(2)}) collective-permute-start(bf16[64,4096]{1,0:T(8,128)(2,1)S(1)} %all_gather.6.refs_0_), channel_id=1, source_target_pairs={{0,128},{128,256},{256,384},{384,0},{1,129},{129,257},{257,385},{3... | collective-permute-start | bytes 1572872 | tf_op jit(solution)/shard_map/ppermute | solution.py:206
  75.4 4.3 %copy-start.1 = (bf16[64,4096]{1,0:T(8,128)(2,1)}, bf16[64,4096]{1,0:T(8,128)(2,1)S(1)}, u32[]{:S(2)}) copy-start(bf16[64,4096]{1,0:T(8,128)(2,1)S(1)} %collective-permute-done.1.refs_1_) | copy-start | bytes 1572868
  79.6 0.8 copy-start.2
  95.0 6.8 %collective-permute-start.4 = (bf16[8,256,512]{2,1,0:T(8,128)(2,1)S(1)}, bf16[8,256,512]{2,1,0:T(8,128)(2,1)}, u32[]{:S(2)}, u32[]{:S(2)}) collective-permute-start(bf16[8,256,512]{2,1,0:T(8,128)(2,1)S(1)} %all-to-all-done.own_ref), channel_id=1, source_target_pairs={{0,8},{8,0},{1,9},{9,1},{2,10},{10,2},{3,11},{11,3},{4,12},{12,4},... | collective-permute-start | bytes 6291464 | tf_op jit(solution)/shard_map/ppermute | solution.py:209
  107.4 15.3 %all-to-all-start.2 = ((bf16[32,8,128]{2,1,0:T(8,128)(2,1)}), bf16[32,8,128]{2,1,0:T(8,128)(2,1)S(1)}, u32[]{:S(2)}, u32[]{:S(2)}) async-start(bf16[32,8,128]{2,1,0:T(8,128)(2,1)} %get-tuple-element.20), calls=%async_computation.2 | async-start | bytes 131072 | tf_op jit(solution)/shard_map/all_to_all | solution.py:23
  123.3 12.7 %all-to-all-start.3 = ((bf16[32,8,128]{2,1,0:T(8,128)(2,1)}), bf16[32,8,128]{2,1,0:T(8,128)(2,1)S(1)}, u32[]{:S(2)}, u32[]{:S(2)}) async-start(bf16[32,8,128]{2,1,0:T(8,128)(2,1)} %shard_map.40), calls=%async_computation.3 | async-start | bytes 131072 | tf_op jit(solution)/shard_map/all_to_all | solution.py:23
  136.4 5.8 %collective-permute-start.5 = (bf16[2,256,128]{2,1,0:T(8,128)(2,1)S(1)}, bf16[2,256,128]{2,1,0:T(8,128)(2,1)S(1)}, u32[]{:S(2)}, u32[]{:S(2)}) collective-permute-start(bf16[2,256,128]{2,1,0:T(8,128)(2,1)S(1)} %slice_bitcast_fusion), channel_id=1, source_target_pairs={{0,8},{8,0},{1,9},{9,1},{2,10},{10,2},{3,11},{11,3},{4,12},{12,4},... | collective-permute-start | bytes 393224 | tf_op jit(solution)/shard_map/ppermute | solution.py:228
Sparse Core Ops, SparseCore 0:
  27.4 60.9 all-gather.1

commit v7 on v6

--- a/solution.py
+++ b/solution.py
@@ -65,15 +65,17 @@
     for k in range(NZ):
         columns = pl.ds((k % PER) * PIECE, PIECE)
         group = [pltpu.make_async_copy(other_hbm.at[k], other.at[k], sem.at[k, 0])]
+        first = 0
         for i, part in enumerate(weights_hbm):
             rows = part.shape[0]
             group.append(
                 pltpu.make_async_copy(
                     part.at[:, pl.ds(k * PIECE, PIECE)],
-                    weight.at[k // PER, pl.ds(i * rows, rows), columns],
+                    weight.at[k // PER, pl.ds(first, rows), columns],
                     sem.at[k, i + 1],
                 )
             )
+            first += rows
         for copy in group:
             copy.start()
         copies.append(group)
@@ -202,11 +204,14 @@
     q_mine = jnp.where(c == 0, q_first, q_second)
     q_theirs = lax.ppermute(jnp.where(c == 0, q_second, q_first), "c", swap)
     q_part = lax.all_gather(jnp.concatenate([q_mine, q_theirs]), "y", axis=0, tiled=True)
-    q_weights = [q_part] + [
-        lax.ppermute(q_part, "x", [(i, (i - k) % NX) for i in range(NX)]) for k in range(1, NX)
-    ]
-    own, q_weights = lax.optimization_barrier((own, q_weights))
+    up = [(i, (i + 1) % NX) for i in range(NX)]
+    down = [(i, (i - 1) % NX) for i in range(NX)]
+    q_after, q_before = lax.ppermute(q_part, "x", down), lax.ppermute(q_part, "x", up)
+    own, q_after, q_before = lax.optimization_barrier((own, q_after, q_before))
     other = lax.ppermute(own, "c", swap)
+    half = q_part.shape[0] // 2
+    q_far = [lax.ppermute(q_after[:half], "x", down), lax.ppermute(q_before[half:], "x", up)]
+    q_weights = [q_part, q_after, *q_far, q_before]
 
     query = project(
         query_kernel, own, other, q_weights, column_order(1, x, c), shape(2, 2, TOK, HD)

time: 151 us -> 149 us (0.987)
  waiting for transfers between devices: 40.1 us -> 21.3 us
  starting transfers between devices: 35 us -> 48.1 us
  local copies, waits for them, and re-layouts: 3.66 us -> 6.92 us
    ppermute x3 -> x4, waiting for transfers between devices: 22.1 us -> 9.31 us  [the longest x1 6.09 us: on_device(): lax.ppermute(q_part, 'x', down)]
    all_to_all x3, starting transfers between devices: 16.1 us -> 22.9 us  [exchange(): return lax.all_to_all(x, axes, 0, 0, tiled=True)]
    all_to_all x3, waiting for transfers between devices: 12.5 us -> 6.52 us  [exchange(): return lax.all_to_all(x, axes, 0, 0, tiled=True)]
    ppermute x3 -> x4, starting transfers between devices: 8.05 us -> 11.6 us  [the longest x1 4.39 us: on_device(): lax.ppermute(q_after[:half], 'x', down)]
    ppermute x1, starting transfers between devices: 2.86 us -> 5.64 us  [on_device(): other = lax.ppermute(own, 'c', swap)]
    slice x0 -> x2, local copies, waits for them, and re-layouts: none -> 2.64 us  [the longest x1 1.68 us: on_device(): q_before[half:]]
  transfers between devices with their start and end apart: 10 -> 11, of which waited for: 8 -> 7; matrix products, arithmetic and copies ran while one was open for 1% -> 3% of each run, Pallas kernels for 3% -> 4%
where the time goes in v7:
time: 149 us; the launch traced here: 148 us
  starting transfers between devices  48.1 us (32%)
  blocking collectives  44.3 us (30%)
  waiting for transfers between devices  21.3 us (14%)
  between operations  13.7 us (9%)
  Pallas kernels  11.9 us (8%)
  local copies, waits for them, and re-layouts  6.92 us (5%)
  other arithmetic  1.63 us (1%)
    all_gather x1, blocking collectives, on_device(): lax.all_gather(jnp.concatenate([q_mine, q_theirs]), 'y', axis=0, tiled=True)  25 us
    all_to_all x3, starting transfers between devices, exchange(): return lax.all_to_all(x, axes, 0, 0, tiled=True)  22.9 us
    all_to_all x1, blocking collectives, exchange(): return lax.all_to_all(x, axes, 0, 0, tiled=True)  19.3 us
    pallas_call x2, Pallas kernels, project(): pl.pallas_call(kernel, in_specs=[vmem, vmem] + [pl.BlockSpec(memory_space...  10.2 us
    all_to_all x3, waiting for transfers between devices, exchange(): return lax.all_to_all(x, axes, 0, 0, tiled=True)  6.52 us
    ppermute x1, waiting for transfers between devices, on_device(): lax.ppermute(q_part, 'x', down)  6.09 us
    ppermute x1, starting transfers between devices, on_device(): other = lax.ppermute(own, 'c', swap)  5.64 us
    ppermute x1, starting transfers between devices, on_device(): mine, theirs = (out[0], lax.ppermute(out[1], 'c', swap))  4.82 us
  transfers between devices with their start and end apart: 11, of which 7 were waited for; matrix products, arithmetic and copies ran while one was open for 3% of the time, Pallas kernels for 4%

profile of v7, /device:TPU:1, one launch (start us, length us, event | category | flops | bytes accessed | tf_op | source)
XLA Modules:
  0.0 147.9 jit_solution(9023352110802123751)
XLA Ops:
  6.5 1.1 fusion.2
  7.9 19.3 %all_to_all.20 = bf16[8,8,4096]{2,1,0:T(8,128)(2,1)} all-to-all(bf16[8,8,4096]{2,1,0:T(8,128)(2,1)S(1)} %bitcast.27), channel_id=1, replica_groups=mesh['x'=4,'y'=8,'c'=2,'z'=8] {'x','c'}, dimensions={0} | all-to-all | bytes 1048576 | tf_op jit(solution)/shard_map/all_to_all | solution.py:23
  27.3 1.5 %broadcast_in_dim.6 = bf16[8,256,512]{2,1,0:T(8,128)(2,1)} broadcast(bf16[256,512]{1,0:T(8,128)(2,1)S(1)} %copy-done.4), dimensions={1,2} | broadcast | bytes 2359296 | tf_op jit(solution)/shard_map/broadcast_in_dim | solution.py:19
  28.8 5.9 %all-to-all-start = ((bf16[8,256,512]{2,1,0:T(8,128)(2,1)}), bf16[8,256,512]{2,1,0:T(8,128)(2,1)S(1)}, u32[]{:S(2)}, u32[]{:S(2)}) async-start(bf16[8,256,512]{2,1,0:T(8,128)(2,1)} %broadcast_in_dim.6), calls=%async_computation | async-start | bytes 4194304 | tf_op jit(solution)/shard_map/all_to_all | solution.py:23
  34.9 3.2 %collective-permute-start = (bf16[4,4096]{1,0:T(4,128)(2,1)S(1)}, bf16[4,4096]{1,0:T(4,128)(2,1)S(1)}, u32[]{:S(2)}, u32[]{:S(2)}) collective-permute-start(bf16[4,4096]{1,0:T(4,128)(2,1)S(1)} %select_n.35), channel_id=1, source_target_pairs={{0,8},{8,0},{1,9},{9,1},{2,10},{10,2},{3,11},{11,3},{4,12},{12,4},... | collective-permute-start | bytes 98312 | tf_op jit(solution)/shard_map/ppermute | solution.py:205
  38.2 0.8 collective-permute-done
  39.0 25.0 %all_gather.6.refs_0_ = bf16[64,4096]{1,0:T(8,128)(2,1)S(1)} all-gather(bf16[8,4096]{1,0:T(8,128)(2,1)S(1)} %pad_maximum_fusion.2), channel_id=1, replica_groups=mesh['x'=4,'y'=8,'c'=2,'z'=8] {'y'}, dimensions={0}, use_global_device_ids=true | all-gather | bytes 589824 | tf_op jit(solution)/shard_map/all_gather | solution.py:206
  64.0 2.9 %collective-permute-start.1 = (bf16[64,4096]{1,0:T(8,128)(2,1)S(1)}, bf16[64,4096]{1,0:T(8,128)(2,1)S(1)}, u32[]{:S(2)}, u32[]{:S(2)}) collective-permute-start(bf16[64,4096]{1,0:T(8,128)(2,1)S(1)} %all_gather.6.refs_0_), channel_id=1, source_target_pairs={{0,384},{128,0},{256,128},{384,256},{1,385},{129,1},{257,129},{385... | collective-permute-start | bytes 1572872 | tf_op jit(solution)/shard_map/ppermute | solution.py:209
  66.9 2.4 %collective-permute-start.2 = (bf16[64,4096]{1,0:T(8,128)(2,1)S(1)}, bf16[64,4096]{1,0:T(8,128)(2,1)}, u32[]{:S(2)}, u32[]{:S(2)}) collective-permute-start(bf16[64,4096]{1,0:T(8,128)(2,1)S(1)} %all_gather.6.refs_0_), channel_id=1, source_target_pairs={{0,128},{128,256},{256,384},{384,0},{1,129},{129,257},{257,385},{3... | collective-permute-start | bytes 1572872 | tf_op jit(solution)/shard_map/ppermute | solution.py:209
  69.3 6.1 %collective-permute-done.1.refs_1_ = bf16[64,4096]{1,0:T(8,128)(2,1)S(1)} collective-permute-done((bf16[64,4096]{1,0:T(8,128)(2,1)S(1)}, bf16[64,4096]{1,0:T(8,128)(2,1)S(1)}, u32[]{:S(2)}, u32[]{:S(2)}) %collective-permute-start.1) | collective-permute-done | bytes 524320 | tf_op jit(solution)/shard_map/ppermute | solution.py:209
  75.4 0.8 copy-done.1
  76.2 3.2 %collective-permute-done.2.refs_4_ = bf16[64,4096]{1,0:T(8,128)(2,1)} collective-permute-done((bf16[64,4096]{1,0:T(8,128)(2,1)S(1)}, bf16[64,4096]{1,0:T(8,128)(2,1)}, u32[]{:S(2)}, u32[]{:S(2)}) %collective-permute-start.2) | collective-permute-done | bytes 524320 | tf_op jit(solution)/shard_map/ppermute | solution.py:209
  79.4 3.7 %all-to-all-done.own_ref = bf16[8,256,512]{2,1,0:T(8,128)(2,1)S(1)} async-done(((bf16[8,256,512]{2,1,0:T(8,128)(2,1)}), bf16[8,256,512]{2,1,0:T(8,128)(2,1)S(1)}, u32[]{:S(2)}, u32[]{:S(2)}) %all-to-all-start) | async-done | bytes 2097184 | tf_op jit(solution)/shard_map/all_to_all | solution.py:23
  83.1 5.6 %collective-permute-start.3 = (bf16[8,256,512]{2,1,0:T(8,128)(2,1)S(1)}, bf16[8,256,512]{2,1,0:T(8,128)(2,1)}, u32[]{:S(2)}, u32[]{:S(2)}) collective-permute-start(bf16[8,256,512]{2,1,0:T(8,128)(2,1)S(1)} %all-to-all-done.own_ref), channel_id=1, source_target_pairs={{0,8},{8,0},{1,9},{9,1},{2,10},{10,2},{3,11},{11,3},{4,12},{12,4},... | collective-permute-start | bytes 6291464 | tf_op jit(solution)/shard_map/ppermute | solution.py:211
  88.8 0.2 fusion.order_ref
  88.9 3.7 %collective-permute-done.3.other_hbm = bf16[8,256,512]{2,1,0:T(8,128)(2,1)} collective-permute-done((bf16[8,256,512]{2,1,0:T(8,128)(2,1)S(1)}, bf16[8,256,512]{2,1,0:T(8,128)(2,1)}, u32[]{:S(2)}, u32[]{:S(2)}) %collective-permute-start.3) | collective-permute-done | bytes 2097184 | tf_op jit(solution)/shard_map/ppermute | solution.py:211
  92.7 5.6 %shard_map.38 = (bf16[2,2,2,256,128]{4,3,2,1,0:T(8,128)(2,1)S(1)}, f32[2,2,128,128]{3,2,1,0:T(8,128)S(1)}, bf16[32,8,128]{2,1,0:T(8,128)(2,1)}) custom-call(bf16[8,256,512]{2,1,0:T(8,128)(2,1)S(1)} %all-to-all-done.own_ref, bf16[512,512]{1,0:T(8,128)(2,1)S(1)} %fusion.order_ref, bf16[8,256,512]{2,1,0:T(8,128)(2,1)} %collective-permute-done.3.other_hbm, ...), custom_call_target="tpu_custom_call" | custom-call | tf_op jit(solution)/shard_map/pallas_call | solution.py:126
  98.3 7.8 %all-to-all-start.2 = ((bf16[32,8,128]{2,1,0:T(8,128)(2,1)}), bf16[32,8,128]{2,1,0:T(8,128)(2,1)S(1)}, u32[]{:S(2)}, u32[]{:S(2)}) async-start(bf16[32,8,128]{2,1,0:T(8,128)(2,1)} %get-tuple-element.16), calls=%async_computation.2 | async-start | bytes 131072 | tf_op jit(solution)/shard_map/all_to_all | solution.py:23
  106.1 1.0 slice.28
  107.1 4.4 %collective-permute-start.4 = (bf16[32,4096]{1,0:T(8,128)(2,1)S(1)}, bf16[32,4096]{1,0:T(8,128)(2,1)S(1)}, u32[]{:S(2)}, u32[]{:S(2)}) collective-permute-start(bf16[32,4096]{1,0:T(8,128)(2,1)S(1)} %slice.28), channel_id=1, source_target_pairs={{0,384},{128,0},{256,128},{384,256},{1,385},{129,1},{257,129},{385... | collective-permute-start | bytes 786440 | tf_op jit(solution)/shard_map/ppermute | solution.py:213
  111.5 1.7 %slice.29 = bf16[32,4096]{1,0:T(8,128)(2,1)} slice(bf16[64,4096]{1,0:T(8,128)(2,1)} %collective-permute-done.2.refs_4_), slice={[32:64], [0:4096]} | slice | bytes 524288 | tf_op jit(solution)/shard_map/slice | solution.py:213
  113.2 1.9 %collective-permute-start.5 = (bf16[32,4096]{1,0:T(8,128)(2,1)}, bf16[32,4096]{1,0:T(8,128)(2,1)}, u32[]{:S(2)}, u32[]{:S(2)}) collective-permute-start(bf16[32,4096]{1,0:T(8,128)(2,1)} %slice.29), channel_id=1, source_target_pairs={{0,128},{128,256},{256,384},{384,0},{1,129},{129,257},{257,385},{3... | collective-permute-start | bytes 786440 | tf_op jit(solution)/shard_map/ppermute | solution.py:213
  115.1 0.7 shard_map.40
  115.8 9.2 %all-to-all-start.3 = ((bf16[32,8,128]{2,1,0:T(8,128)(2,1)}), bf16[32,8,128]{2,1,0:T(8,128)(2,1)S(1)}, u32[]{:S(2)}, u32[]{:S(2)}) async-start(bf16[32,8,128]{2,1,0:T(8,128)(2,1)} %shard_map.40), calls=%async_computation.3 | async-start | bytes 131072 | tf_op jit(solution)/shard_map/all_to_all | solution.py:23
  125.1 0.7 copy-done.5
  125.8 4.6 %shard_map.37.query_ref = bf16[2,2,256,128]{3,2,1,0:T(8,128)(2,1)S(1)} custom-call(bf16[8,256,512]{2,1,0:T(8,128)(2,1)S(1)} %all-to-all-done.own_ref, bf16[256,256]{1,0:T(8,128)(2,1)S(1)} %fusion.1.order_ref, bf16[8,256,512]{2,1,0:T(8,128)(2,1)} %collective-permute-done.3.other_hbm, bf16[64,4096]{1,0:T(8,128)(2,1)} %copy-done, bf16[64,4096]{1,0:T(8,128)(2,1)} %copy-done.1, ...), custom_call_target="tpu_custom_call" | custom-call | tf_op jit(solution)/shard_map/pallas_call | solution.py:126
  130.4 0.7 shard_map.39.inner_ref
  131.0 2.8 %all-to-all-done.3.prior_ref = bf16[32,8,128]{2,1,0:T(8,128)(2,1)S(1)} async-done(((bf16[32,8,128]{2,1,0:T(8,128)(2,1)}), bf16[32,8,128]{2,1,0:T(8,128)(2,1)S(1)}, u32[]{:S(2)}, u32[]{:S(2)}) %all-to-all-start.3) | async-done | bytes 65568 | tf_op jit(solution)/shard_map/all_to_all | solution.py:23
  133.8 0.4 shard_map.41
  134.2 4.8 %collective-permute-start.6 = (bf16[2,256,128]{2,1,0:T(8,128)(2,1)S(1)}, bf16[2,256,128]{2,1,0:T(8,128)(2,1)S(1)}, u32[]{:S(2)}, u32[]{:S(2)}) collective-permute-start(bf16[2,256,128]{2,1,0:T(8,128)(2,1)S(1)} %slice_bitcast_fusion), channel_id=1, source_target_pairs={{0,8},{8,0},{1,9},{9,1},{2,10},{10,2},{3,11},{11,3},{4,12},{12,4},... | collective-permute-start | bytes 393224 | tf_op jit(solution)/shard_map/ppermute | solution.py:233
  139.1 1.0 collective-permute-done.6
  140.1 1.0 copy.7
  (30 shorter events, 0.7 us)
Async XLA Ops:
  6.5 20.8 %copy-start.4 = (bf16[256,512]{1,0:T(8,128)(2,1)S(1)}, bf16[256,512]{1,0:T(8,128)(2,1)}, u32[]{:S(2)}) copy-start(bf16[256,512]{1,0:T(8,128)(2,1)} %param.3) | copy-start | bytes 786436
  6.5 86.1 %all-gather.2.cloned.1.call-start = ((), (), s32[]{:S(2)}) async-start(), calls=%async_computation.4 | async-start | bytes 4718592 | tf_op jit(solution)/shard_map/all_gather | solution.py:200
  28.8 5.9 %copy-start.2 = (bf16[3,4096,2,2]{1,3,2,0:T(2,128)(2,1)S(1)}, bf16[3,4096,2,2]{1,3,2,0:T(2,128)(2,1)}, u32[]{:S(2)}) copy-start(bf16[3,4096,2,2]{1,3,2,0:T(2,128)(2,1)} %param.5) | copy-start | bytes 294916
  28.8 5.9 %copy-start.3 = (bf16[3,4096,2,2]{1,3,2,0:T(2,128)(2,1)S(1)}, bf16[3,4096,2,2]{1,3,2,0:T(2,128)(2,1)}, u32[]{:S(2)}) copy-start(bf16[3,4096,2,2]{1,3,2,0:T(2,128)(2,1)} %param.4) | copy-start | bytes 294916
  28.8 54.3 %all-to-all-start = ((bf16[8,256,512]{2,1,0:T(8,128)(2,1)}), bf16[8,256,512]{2,1,0:T(8,128)(2,1)S(1)}, u32[]{:S(2)}, u32[]{:S(2)}) async-start(bf16[8,256,512]{2,1,0:T(8,128)(2,1)} %broadcast_in_dim.6), calls=%async_computation | async-start | bytes 4194304 | tf_op jit(solution)/shard_map/all_to_all | solution.py:23
  34.9 4.1 %collective-permute-start = (bf16[4,4096]{1,0:T(4,128)(2,1)S(1)}, bf16[4,4096]{1,0:T(4,128)(2,1)S(1)}, u32[]{:S(2)}, u32[]{:S(2)}) collective-permute-start(bf16[4,4096]{1,0:T(4,128)(2,1)S(1)} %select_n.35), channel_id=1, source_target_pairs={{0,8},{8,0},{1,9},{9,1},{2,10},{10,2},{3,11},{11,3},{4,12},{12,4},... | collective-permute-start | bytes 98312 | tf_op jit(solution)/shard_map/ppermute | solution.py:205
  64.0 11.4 %copy-start = (bf16[64,4096]{1,0:T(8,128)(2,1)}, bf16[64,4096]{1,0:T(8,128)(2,1)S(1)}, u32[]{:S(2)}) copy-start(bf16[64,4096]{1,0:T(8,128)(2,1)S(1)} %all_gather.6.refs_0_) | copy-start | bytes 1572868
  64.0 11.4 %collective-permute-start.1 = (bf16[64,4096]{1,0:T(8,128)(2,1)S(1)}, bf16[64,4096]{1,0:T(8,128)(2,1)S(1)}, u32[]{:S(2)}, u32[]{:S(2)}) collective-permute-start(bf16[64,4096]{1,0:T(8,128)(2,1)S(1)} %all_gather.6.refs_0_), channel_id=1, source_target_pairs={{0,384},{128,0},{256,128},{384,256},{1,385},{129,1},{257,129},{385... | collective-permute-start | bytes 1572872 | tf_op jit(solution)/shard_map/ppermute | solution.py:209
  66.9 12.5 %collective-permute-start.2 = (bf16[64,4096]{1,0:T(8,128)(2,1)S(1)}, bf16[64,4096]{1,0:T(8,128)(2,1)}, u32[]{:S(2)}, u32[]{:S(2)}) collective-permute-start(bf16[64,4096]{1,0:T(8,128)(2,1)S(1)} %all_gather.6.refs_0_), channel_id=1, source_target_pairs={{0,128},{128,256},{256,384},{384,0},{1,129},{129,257},{257,385},{3... | collective-permute-start | bytes 1572872 | tf_op jit(solution)/shard_map/ppermute | solution.py:209
  75.4 0.8 copy-start.1
  83.1 9.5 %collective-permute-start.3 = (bf16[8,256,512]{2,1,0:T(8,128)(2,1)S(1)}, bf16[8,256,512]{2,1,0:T(8,128)(2,1)}, u32[]{:S(2)}, u32[]{:S(2)}) collective-permute-start(bf16[8,256,512]{2,1,0:T(8,128)(2,1)S(1)} %all-to-all-done.own_ref), channel_id=1, source_target_pairs={{0,8},{8,0},{1,9},{9,1},{2,10},{10,2},{3,11},{11,3},{4,12},{12,4},... | collective-permute-start | bytes 6291464 | tf_op jit(solution)/shard_map/ppermute | solution.py:211
  98.3 16.8 %all-to-all-start.2 = ((bf16[32,8,128]{2,1,0:T(8,128)(2,1)}), bf16[32,8,128]{2,1,0:T(8,128)(2,1)S(1)}, u32[]{:S(2)}, u32[]{:S(2)}) async-start(bf16[32,8,128]{2,1,0:T(8,128)(2,1)} %get-tuple-element.16), calls=%async_computation.2 | async-start | bytes 131072 | tf_op jit(solution)/shard_map/all_to_all | solution.py:23
  107.1 18.0 %collective-permute-start.4 = (bf16[32,4096]{1,0:T(8,128)(2,1)S(1)}, bf16[32,4096]{1,0:T(8,128)(2,1)S(1)}, u32[]{:S(2)}, u32[]{:S(2)}) collective-permute-start(bf16[32,4096]{1,0:T(8,128)(2,1)S(1)} %slice.28), channel_id=1, source_target_pairs={{0,384},{128,0},{256,128},{384,256},{1,385},{129,1},{257,129},{385... | collective-permute-start | bytes 786440 | tf_op jit(solution)/shard_map/ppermute | solution.py:213
  113.2 11.9 %collective-permute-start.5 = (bf16[32,4096]{1,0:T(8,128)(2,1)}, bf16[32,4096]{1,0:T(8,128)(2,1)}, u32[]{:S(2)}, u32[]{:S(2)}) collective-permute-start(bf16[32,4096]{1,0:T(8,128)(2,1)} %slice.29), channel_id=1, source_target_pairs={{0,128},{128,256},{256,384},{384,0},{1,129},{129,257},{257,385},{3... | collective-permute-start | bytes 786440 | tf_op jit(solution)/shard_map/ppermute | solution.py:213
  115.8 18.0 %all-to-all-start.3 = ((bf16[32,8,128]{2,1,0:T(8,128)(2,1)}), bf16[32,8,128]{2,1,0:T(8,128)(2,1)S(1)}, u32[]{:S(2)}, u32[]{:S(2)}) async-start(bf16[32,8,128]{2,1,0:T(8,128)(2,1)} %shard_map.40), calls=%async_computation.3 | async-start | bytes 131072 | tf_op jit(solution)/shard_map/all_to_all | solution.py:23
  125.1 0.7 copy-start.5
  134.2 5.8 %collective-permute-start.6 = (bf16[2,256,128]{2,1,0:T(8,128)(2,1)S(1)}, bf16[2,256,128]{2,1,0:T(8,128)(2,1)S(1)}, u32[]{:S(2)}, u32[]{:S(2)}) collective-permute-start(bf16[2,256,128]{2,1,0:T(8,128)(2,1)S(1)} %slice_bitcast_fusion), channel_id=1, source_target_pairs={{0,8},{8,0},{1,9},{9,1},{2,10},{10,2},{3,11},{11,3},{4,12},{12,4},... | collective-permute-start | bytes 393224 | tf_op jit(solution)/shard_map/ppermute | solution.py:233
Sparse Core Ops, SparseCore 0:
  27.4 60.9 all-gather.1

commit v8 on v7

--- a/solution.py
+++ b/solution.py
@@ -209,9 +209,7 @@
     q_after, q_before = lax.ppermute(q_part, "x", down), lax.ppermute(q_part, "x", up)
     own, q_after, q_before = lax.optimization_barrier((own, q_after, q_before))
     other = lax.ppermute(own, "c", swap)
-    half = q_part.shape[0] // 2
-    q_far = [lax.ppermute(q_after[:half], "x", down), lax.ppermute(q_before[half:], "x", up)]
-    q_weights = [q_part, q_after, *q_far, q_before]
+    q_weights = [q_part, q_after, lax.ppermute(q_after, "x", down), q_before]
 
     query = project(
         query_kernel, own, other, q_weights, column_order(1, x, c), shape(2, 2, TOK, HD)
@@ -225,7 +223,8 @@
         (shape(2, 2, 2, TOK, HD), shape(2, 2, HD, HD, dtype=F32), shape(NX * NY, 8, HD)),
     )
 
-    slices = call(prefix_kernel, shape(NX * NY, 8, HD), exchange(total, ("x", "y")))
+    totals, query = lax.optimization_barrier((exchange(total, ("x", "y")), query))
+    slices = call(prefix_kernel, shape(NX * NY, 8, HD), totals)
     prior = exchange(slices, ("x", "y"))
 
     inner = call(inner_kernel, shape(2, 2, TOK, HD, dtype=F32), query, kv)

time: 149 us -> 144 us (0.966)
  starting transfers between devices: 48.1 us -> 39.9 us
  waiting for transfers between devices: 21.3 us -> 29.1 us
  local copies, waits for them, and re-layouts: 6.92 us -> 2.82 us
    all_to_all x3, waiting for transfers between devices: 6.52 us -> 16.1 us  [exchange(): return lax.all_to_all(x, axes, 0, 0, tiled=True)]
    all_to_all x3, starting transfers between devices: 22.9 us -> 18.6 us  [exchange(): return lax.all_to_all(x, axes, 0, 0, tiled=True)]
    ppermute x2 -> x1, starting transfers between devices: 6.3 us -> 2.79 us  [on_device(): q_weights = [q_part, q_after, lax.ppermute(q_after, 'x', down), q_before]]
    ppermute x1, waiting for transfers between devices: 3.72 us -> 0.9 us  [on_device(): other = lax.ppermute(own, 'c', swap)]
    slice x2 -> x0, local copies, waits for them, and re-layouts: 2.64 us -> none  [the longest x1 1.68 us: on_device(): q_before[half:]]
  transfers between devices with their start and end apart: 11 -> 10, of which waited for: 7 -> 8; matrix products, arithmetic and copies ran while one was open for 3% -> 1% of each run, Pallas kernels for 4% -> 8%
where the time goes in v8:
time: 144 us; the launch traced here: 143 us
  blocking collectives  44.3 us (31%)
  starting transfers between devices  39.9 us (28%)
  waiting for transfers between devices  29.1 us (20%)
  between operations  13.6 us (9%)
  Pallas kernels  11.8 us (8%)
  local copies, waits for them, and re-layouts  2.82 us (2%)
  other arithmetic  1.63 us (1%)
    all_gather x1, blocking collectives, on_device(): lax.all_gather(jnp.concatenate([q_mine, q_theirs]), 'y', axis=0, tiled=True)  24.9 us
    all_to_all x1, blocking collectives, exchange(): return lax.all_to_all(x, axes, 0, 0, tiled=True)  19.3 us
    all_to_all x3, starting transfers between devices, exchange(): return lax.all_to_all(x, axes, 0, 0, tiled=True)  18.6 us
    all_to_all x3, waiting for transfers between devices, exchange(): return lax.all_to_all(x, axes, 0, 0, tiled=True)  16.1 us
    pallas_call x2, Pallas kernels, project(): pl.pallas_call(kernel, in_specs=[vmem, vmem] + [pl.BlockSpec(memory_space...  10.1 us
    ppermute x1, waiting for transfers between devices, on_device(): lax.ppermute(q_part, 'x', down)  6.07 us
    ppermute x1, starting transfers between devices, on_device(): other = lax.ppermute(own, 'c', swap)  5.64 us
    ppermute x1, starting transfers between devices, on_device(): mine, theirs = (out[0], lax.ppermute(out[1], 'c', swap))  4.28 us
  transfers between devices with their start and end apart: 10, of which 8 were waited for; matrix products, arithmetic and copies ran while one was open for 1% of the time, Pallas kernels for 8%

profile of v8, /device:TPU:1, one launch (start us, length us, event | category | flops | bytes accessed | tf_op | source)
XLA Modules:
  0.0 143.1 jit_solution(2911414826153820442)
XLA Ops:
  6.5 1.1 fusion.2
  7.6 0.1 copy.5
  7.8 0.1 copy.6
  7.9 19.3 %all_to_all.20 = bf16[8,8,4096]{2,1,0:T(8,128)(2,1)} all-to-all(bf16[8,8,4096]{2,1,0:T(8,128)(2,1)S(1)} %bitcast.27), channel_id=1, replica_groups=mesh['x'=4,'y'=8,'c'=2,'z'=8] {'x','c'}, dimensions={0} | all-to-all | bytes 1048576 | tf_op jit(solution)/shard_map/all_to_all | solution.py:23
  27.3 1.5 %broadcast_in_dim.6 = bf16[8,256,512]{2,1,0:T(8,128)(2,1)} broadcast(bf16[256,512]{1,0:T(8,128)(2,1)S(1)} %copy-done.3), dimensions={1,2} | broadcast | bytes 2359296 | tf_op jit(solution)/shard_map/broadcast_in_dim | solution.py:19
  28.8 5.9 %all-to-all-start = ((bf16[8,256,512]{2,1,0:T(8,128)(2,1)}), bf16[8,256,512]{2,1,0:T(8,128)(2,1)S(1)}, u32[]{:S(2)}, u32[]{:S(2)}) async-start(bf16[8,256,512]{2,1,0:T(8,128)(2,1)} %broadcast_in_dim.6), calls=%async_computation | async-start | bytes 4194304 | tf_op jit(solution)/shard_map/all_to_all | solution.py:23
  34.7 0.1 broadcast_select_fusion.1
  34.9 3.2 %collective-permute-start = (bf16[4,4096]{1,0:T(4,128)(2,1)S(1)}, bf16[4,4096]{1,0:T(4,128)(2,1)S(1)}, u32[]{:S(2)}, u32[]{:S(2)}) collective-permute-start(bf16[4,4096]{1,0:T(4,128)(2,1)S(1)} %select_n.35), channel_id=1, source_target_pairs={{0,8},{8,0},{1,9},{9,1},{2,10},{10,2},{3,11},{11,3},{4,12},{12,4},... | collective-permute-start | bytes 98312 | tf_op jit(solution)/shard_map/ppermute | solution.py:205
  38.2 0.8 collective-permute-done
  39.0 24.9 %all_gather.6.refs_0_ = bf16[64,4096]{1,0:T(8,128)(2,1)S(1)} all-gather(bf16[8,4096]{1,0:T(8,128)(2,1)S(1)} %pad_maximum_fusion.2), channel_id=1, replica_groups=mesh['x'=4,'y'=8,'c'=2,'z'=8] {'y'}, dimensions={0}, use_global_device_ids=true | all-gather | bytes 589824 | tf_op jit(solution)/shard_map/all_gather | solution.py:206
  64.0 2.9 %collective-permute-start.1 = (bf16[64,4096]{1,0:T(8,128)(2,1)S(1)}, bf16[64,4096]{1,0:T(8,128)(2,1)}, u32[]{:S(2)}, u32[]{:S(2)}) collective-permute-start(bf16[64,4096]{1,0:T(8,128)(2,1)S(1)} %all_gather.6.refs_0_), channel_id=1, source_target_pairs={{0,384},{128,0},{256,128},{384,256},{1,385},{129,1},{257,129},{385... | collective-permute-start | bytes 1572872 | tf_op jit(solution)/shard_map/ppermute | solution.py:209
  66.9 2.3 %collective-permute-start.2 = (bf16[64,4096]{1,0:T(8,128)(2,1)S(1)}, bf16[64,4096]{1,0:T(8,128)(2,1)}, u32[]{:S(2)}, u32[]{:S(2)}) collective-permute-start(bf16[64,4096]{1,0:T(8,128)(2,1)S(1)} %all_gather.6.refs_0_), channel_id=1, source_target_pairs={{0,128},{128,256},{256,384},{384,0},{1,129},{129,257},{257,385},{3... | collective-permute-start | bytes 1572872 | tf_op jit(solution)/shard_map/ppermute | solution.py:209
  69.3 6.1 %collective-permute-done.1.refs_1_ = bf16[64,4096]{1,0:T(8,128)(2,1)} collective-permute-done((bf16[64,4096]{1,0:T(8,128)(2,1)S(1)}, bf16[64,4096]{1,0:T(8,128)(2,1)}, u32[]{:S(2)}, u32[]{:S(2)}) %collective-permute-start.1) | collective-permute-done | bytes 524320 | tf_op jit(solution)/shard_map/ppermute | solution.py:209
  75.4 4.2 %collective-permute-done.2.refs_3_ = bf16[64,4096]{1,0:T(8,128)(2,1)} collective-permute-done((bf16[64,4096]{1,0:T(8,128)(2,1)S(1)}, bf16[64,4096]{1,0:T(8,128)(2,1)}, u32[]{:S(2)}, u32[]{:S(2)}) %collective-permute-start.2) | collective-permute-done | bytes 524320 | tf_op jit(solution)/shard_map/ppermute | solution.py:209
  79.5 3.6 %all-to-all-done.own_ref = bf16[8,256,512]{2,1,0:T(8,128)(2,1)S(1)} async-done(((bf16[8,256,512]{2,1,0:T(8,128)(2,1)}), bf16[8,256,512]{2,1,0:T(8,128)(2,1)S(1)}, u32[]{:S(2)}, u32[]{:S(2)}) %all-to-all-start) | async-done | bytes 2097184 | tf_op jit(solution)/shard_map/all_to_all | solution.py:23
  83.1 5.6 %collective-permute-start.3 = (bf16[8,256,512]{2,1,0:T(8,128)(2,1)S(1)}, bf16[8,256,512]{2,1,0:T(8,128)(2,1)}, u32[]{:S(2)}, u32[]{:S(2)}) collective-permute-start(bf16[8,256,512]{2,1,0:T(8,128)(2,1)S(1)} %all-to-all-done.own_ref), channel_id=1, source_target_pairs={{0,8},{8,0},{1,9},{9,1},{2,10},{10,2},{3,11},{11,3},{4,12},{12,4},... | collective-permute-start | bytes 6291464 | tf_op jit(solution)/shard_map/ppermute | solution.py:211
  88.8 2.8 %collective-permute-start.4 = (bf16[64,4096]{1,0:T(8,128)(2,1)}, bf16[64,4096]{1,0:T(8,128)(2,1)}, u32[]{:S(2)}, u32[]{:S(2)}) collective-permute-start(bf16[64,4096]{1,0:T(8,128)(2,1)} %collective-permute-done.1.refs_1_), channel_id=1, source_target_pairs={{0,384},{128,0},{256,128},{384,256},{1,385},{129,1},{257,129},{385... | collective-permute-start | bytes 1572872 | tf_op jit(solution)/shard_map/ppermute | solution.py:212
  91.6 0.2 fusion.order_ref
  91.8 0.9 collective-permute-done.3.other_hbm
  92.7 5.6 %shard_map.37 = (bf16[2,2,2,256,128]{4,3,2,1,0:T(8,128)(2,1)S(1)}, f32[2,2,128,128]{3,2,1,0:T(8,128)S(1)}, bf16[32,8,128]{2,1,0:T(8,128)(2,1)}) custom-call(bf16[8,256,512]{2,1,0:T(8,128)(2,1)S(1)} %all-to-all-done.own_ref, bf16[512,512]{1,0:T(8,128)(2,1)S(1)} %fusion.order_ref, bf16[8,256,512]{2,1,0:T(8,128)(2,1)} %collective-permute-done.3.other_hbm, ...), custom_call_target="tpu_custom_call" | custom-call | tf_op jit(solution)/shard_map/pallas_call | solution.py:126
  98.3 7.8 %all-to-all-start.2 = ((bf16[32,8,128]{2,1,0:T(8,128)(2,1)}), bf16[32,8,128]{2,1,0:T(8,128)(2,1)S(1)}, u32[]{:S(2)}, u32[]{:S(2)}) async-start(bf16[32,8,128]{2,1,0:T(8,128)(2,1)} %get-tuple-element.14), calls=%async_computation.2 | async-start | bytes 131072 | tf_op jit(solution)/shard_map/all_to_all | solution.py:23
  106.1 0.1 fusion.1.order_ref
  106.3 4.5 %shard_map.38.query_ref = bf16[2,2,256,128]{3,2,1,0:T(8,128)(2,1)S(1)} custom-call(bf16[8,256,512]{2,1,0:T(8,128)(2,1)S(1)} %all-to-all-done.own_ref, bf16[256,256]{1,0:T(8,128)(2,1)S(1)} %fusion.1.order_ref, bf16[8,256,512]{2,1,0:T(8,128)(2,1)} %collective-permute-done.3.other_hbm, bf16[64,4096]{1,0:T(8,128)(2,1)} %copy-done, ...), custom_call_target="tpu_custom_call" | custom-call | tf_op jit(solution)/shard_map/pallas_call | solution.py:126
  110.8 4.3 %all-to-all-done.2.total_ref = bf16[32,8,128]{2,1,0:T(8,128)(2,1)S(1)} async-done(((bf16[32,8,128]{2,1,0:T(8,128)(2,1)}), bf16[32,8,128]{2,1,0:T(8,128)(2,1)S(1)}, u32[]{:S(2)}, u32[]{:S(2)}) %all-to-all-start.2) | async-done | bytes 65568 | tf_op jit(solution)/shard_map/all_to_all | solution.py:23
  115.1 0.7 shard_map.40
  115.8 4.9 %all-to-all-start.3 = ((bf16[32,8,128]{2,1,0:T(8,128)(2,1)}), bf16[32,8,128]{2,1,0:T(8,128)(2,1)S(1)}, u32[]{:S(2)}, u32[]{:S(2)}) async-start(bf16[32,8,128]{2,1,0:T(8,128)(2,1)} %shard_map.40), calls=%async_computation.3 | async-start | bytes 131072 | tf_op jit(solution)/shard_map/all_to_all | solution.py:23
  120.7 0.7 shard_map.39.inner_ref
  121.3 8.2 %all-to-all-done.3.prior_ref = bf16[32,8,128]{2,1,0:T(8,128)(2,1)S(1)} async-done(((bf16[32,8,128]{2,1,0:T(8,128)(2,1)}), bf16[32,8,128]{2,1,0:T(8,128)(2,1)S(1)}, u32[]{:S(2)}, u32[]{:S(2)}) %all-to-all-start.3) | async-done | bytes 65568 | tf_op jit(solution)/shard_map/all_to_all | solution.py:23
  129.5 0.4 shard_map.41
  129.9 4.3 %collective-permute-start.5 = (bf16[2,256,128]{2,1,0:T(8,128)(2,1)S(1)}, bf16[2,256,128]{2,1,0:T(8,128)(2,1)S(1)}, u32[]{:S(2)}, u32[]{:S(2)}) collective-permute-start(bf16[2,256,128]{2,1,0:T(8,128)(2,1)S(1)} %slice_bitcast_fusion), channel_id=1, source_target_pairs={{0,8},{8,0},{1,9},{9,1},{2,10},{10,2},{3,11},{11,3},{4,12},{12,4},... | collective-permute-start | bytes 393224 | tf_op jit(solution)/shard_map/ppermute | solution.py:232
  134.2 1.0 collective-permute-done.5
  135.3 1.0 copy.7
  (22 shorter events, 0.3 us)
Async XLA Ops:
  6.5 20.7 %copy-start.3 = (bf16[256,512]{1,0:T(8,128)(2,1)S(1)}, bf16[256,512]{1,0:T(8,128)(2,1)}, u32[]{:S(2)}) copy-start(bf16[256,512]{1,0:T(8,128)(2,1)} %param.3) | copy-start | bytes 786436
  6.5 86.1 %all-gather.2.cloned.1.call-start = ((), (), s32[]{:S(2)}) async-start(), calls=%async_computation.4 | async-start | bytes 4718592 | tf_op jit(solution)/shard_map/all_gather | solution.py:200
  28.8 5.9 %copy-start.1 = (bf16[3,4096,2,2]{1,3,2,0:T(2,128)(2,1)S(1)}, bf16[3,4096,2,2]{1,3,2,0:T(2,128)(2,1)}, u32[]{:S(2)}) copy-start(bf16[3,4096,2,2]{1,3,2,0:T(2,128)(2,1)} %param.5) | copy-start | bytes 294916
  28.8 5.9 %copy-start.2 = (bf16[3,4096,2,2]{1,3,2,0:T(2,128)(2,1)S(1)}, bf16[3,4096,2,2]{1,3,2,0:T(2,128)(2,1)}, u32[]{:S(2)}) copy-start(bf16[3,4096,2,2]{1,3,2,0:T(2,128)(2,1)} %param.4) | copy-start | bytes 294916
  28.8 54.3 %all-to-all-start = ((bf16[8,256,512]{2,1,0:T(8,128)(2,1)}), bf16[8,256,512]{2,1,0:T(8,128)(2,1)S(1)}, u32[]{:S(2)}, u32[]{:S(2)}) async-start(bf16[8,256,512]{2,1,0:T(8,128)(2,1)} %broadcast_in_dim.6), calls=%async_computation | async-start | bytes 4194304 | tf_op jit(solution)/shard_map/all_to_all | solution.py:23
  34.9 4.1 %collective-permute-start = (bf16[4,4096]{1,0:T(4,128)(2,1)S(1)}, bf16[4,4096]{1,0:T(4,128)(2,1)S(1)}, u32[]{:S(2)}, u32[]{:S(2)}) collective-permute-start(bf16[4,4096]{1,0:T(4,128)(2,1)S(1)} %select_n.35), channel_id=1, source_target_pairs={{0,8},{8,0},{1,9},{9,1},{2,10},{10,2},{3,11},{11,3},{4,12},{12,4},... | collective-permute-start | bytes 98312 | tf_op jit(solution)/shard_map/ppermute | solution.py:205
  64.0 11.4 %copy-start = (bf16[64,4096]{1,0:T(8,128)(2,1)}, bf16[64,4096]{1,0:T(8,128)(2,1)S(1)}, u32[]{:S(2)}) copy-start(bf16[64,4096]{1,0:T(8,128)(2,1)S(1)} %all_gather.6.refs_0_) | copy-start | bytes 1572868
  64.0 11.4 %collective-permute-start.1 = (bf16[64,4096]{1,0:T(8,128)(2,1)S(1)}, bf16[64,4096]{1,0:T(8,128)(2,1)}, u32[]{:S(2)}, u32[]{:S(2)}) collective-permute-start(bf16[64,4096]{1,0:T(8,128)(2,1)S(1)} %all_gather.6.refs_0_), channel_id=1, source_target_pairs={{0,384},{128,0},{256,128},{384,256},{1,385},{129,1},{257,129},{385... | collective-permute-start | bytes 1572872 | tf_op jit(solution)/shard_map/ppermute | solution.py:209
  66.9 12.6 %collective-permute-start.2 = (bf16[64,4096]{1,0:T(8,128)(2,1)S(1)}, bf16[64,4096]{1,0:T(8,128)(2,1)}, u32[]{:S(2)}, u32[]{:S(2)}) collective-permute-start(bf16[64,4096]{1,0:T(8,128)(2,1)S(1)} %all_gather.6.refs_0_), channel_id=1, source_target_pairs={{0,128},{128,256},{256,384},{384,0},{1,129},{129,257},{257,385},{3... | collective-permute-start | bytes 1572872 | tf_op jit(solution)/shard_map/ppermute | solution.py:209
  83.1 9.5 %collective-permute-start.3 = (bf16[8,256,512]{2,1,0:T(8,128)(2,1)S(1)}, bf16[8,256,512]{2,1,0:T(8,128)(2,1)}, u32[]{:S(2)}, u32[]{:S(2)}) collective-permute-start(bf16[8,256,512]{2,1,0:T(8,128)(2,1)S(1)} %all-to-all-done.own_ref), channel_id=1, source_target_pairs={{0,8},{8,0},{1,9},{9,1},{2,10},{10,2},{3,11},{11,3},{4,12},{12,4},... | collective-permute-start | bytes 6291464 | tf_op jit(solution)/shard_map/ppermute | solution.py:211
  88.8 17.5 %collective-permute-start.4 = (bf16[64,4096]{1,0:T(8,128)(2,1)}, bf16[64,4096]{1,0:T(8,128)(2,1)}, u32[]{:S(2)}, u32[]{:S(2)}) collective-permute-start(bf16[64,4096]{1,0:T(8,128)(2,1)} %collective-permute-done.1.refs_1_), channel_id=1, source_target_pairs={{0,384},{128,0},{256,128},{384,256},{1,385},{129,1},{257,129},{385... | collective-permute-start | bytes 1572872 | tf_op jit(solution)/shard_map/ppermute | solution.py:212
  98.3 16.8 %all-to-all-start.2 = ((bf16[32,8,128]{2,1,0:T(8,128)(2,1)}), bf16[32,8,128]{2,1,0:T(8,128)(2,1)S(1)}, u32[]{:S(2)}, u32[]{:S(2)}) async-start(bf16[32,8,128]{2,1,0:T(8,128)(2,1)} %get-tuple-element.14), calls=%async_computation.2 | async-start | bytes 131072 | tf_op jit(solution)/shard_map/all_to_all | solution.py:23
  115.8 13.8 %all-to-all-start.3 = ((bf16[32,8,128]{2,1,0:T(8,128)(2,1)}), bf16[32,8,128]{2,1,0:T(8,128)(2,1)S(1)}, u32[]{:S(2)}, u32[]{:S(2)}) async-start(bf16[32,8,128]{2,1,0:T(8,128)(2,1)} %shard_map.40), calls=%async_computation.3 | async-start | bytes 131072 | tf_op jit(solution)/shard_map/all_to_all | solution.py:23
  129.9 5.3 %collective-permute-start.5 = (bf16[2,256,128]{2,1,0:T(8,128)(2,1)S(1)}, bf16[2,256,128]{2,1,0:T(8,128)(2,1)S(1)}, u32[]{:S(2)}, u32[]{:S(2)}) collective-permute-start(bf16[2,256,128]{2,1,0:T(8,128)(2,1)S(1)} %slice_bitcast_fusion), channel_id=1, source_target_pairs={{0,8},{8,0},{1,9},{9,1},{2,10},{10,2},{3,11},{11,3},{4,12},{12,4},... | collective-permute-start | bytes 393224 | tf_op jit(solution)/shard_map/ppermute | solution.py:232
Sparse Core Ops, SparseCore 0:
  27.4 60.9 all-gather.1

commit v9 on v8

--- a/solution.py
+++ b/solution.py
@@ -139,7 +139,23 @@
     )(own, order, *far)
 
 
-def prefix_kernel(total_ref, out_ref):
+def arrived_kernel(block_hbm, out_ref, sem):
+    copy = pltpu.make_async_copy(block_hbm.at[pl.ds(0, 8), pl.ds(0, HD)], out_ref, sem)
+    copy.start()
+    copy.wait()
+
+
+def arrived(block):
+    return pl.pallas_call(
+        arrived_kernel,
+        in_specs=[pl.BlockSpec(memory_space=pltpu.HBM)],
+        out_specs=pl.BlockSpec(memory_space=pltpu.VMEM),
+        out_shape=shape(8, HD),
+        scratch_shapes=[pltpu.SemaphoreType.DMA],
+    )(pltpu.with_memory_space_constraint(block, pltpu.HBM))
+
+
+def prefix_kernel(total_ref, arrived_ref, out_ref):
     run = jnp.zeros(total_ref.shape[1:], F32)
     for chip in range(NX * NY):
         out_ref[chip] = run.astype(BF16)
@@ -172,11 +188,12 @@
             out_ref[block, s] = (combined * scale).astype(BF16)
 
 
-def call(kernel, out_shape, *args):
+def call(kernel, out_shape, *args, unread=0):
+    spaces = [pltpu.VMEM] * (len(args) - unread) + [pl.ANY] * unread
     return pl.pallas_call(
         kernel,
         out_shape=out_shape,
-        in_specs=[pl.BlockSpec(memory_space=pltpu.VMEM)] * len(args),
+        in_specs=[pl.BlockSpec(memory_space=space) for space in spaces],
         out_specs=pl.BlockSpec(memory_space=pltpu.VMEM),
         compiler_params=pltpu.CompilerParams(vmem_limit_bytes=12 << 20),
     )(*args)
@@ -209,7 +226,8 @@
     q_after, q_before = lax.ppermute(q_part, "x", down), lax.ppermute(q_part, "x", up)
     own, q_after, q_before = lax.optimization_barrier((own, q_after, q_before))
     other = lax.ppermute(own, "c", swap)
-    q_weights = [q_part, q_after, lax.ppermute(q_after, "x", down), q_before]
+    q_far = lax.ppermute(q_after, "x", down)
+    q_weights = [q_part, q_after, q_far, q_before]
 
     query = project(
         query_kernel, own, other, q_weights, column_order(1, x, c), shape(2, 2, TOK, HD)
@@ -223,8 +241,9 @@
         (shape(2, 2, 2, TOK, HD), shape(2, 2, HD, HD, dtype=F32), shape(NX * NY, 8, HD)),
     )
 
-    totals, query = lax.optimization_barrier((exchange(total, ("x", "y")), query))
-    slices = call(prefix_kernel, shape(NX * NY, 8, HD), totals)
+    slices = call(
+        prefix_kernel, shape(NX * NY, 8, HD), exchange(total, ("x", "y")), arrived(q_far), unread=1
+    )
     prior = exchange(slices, ("x", "y"))
 
     inner = call(inner_kernel, shape(2, 2, TOK, HD, dtype=F32), query, kv)

time: 144 us -> 144 us (level)
  no operation moved by 1% of the time
where the time goes in v9:
time: 144 us; the launch traced here: 143 us
  blocking collectives  44.3 us (31%)
  starting transfers between devices  39.3 us (27%)
  waiting for transfers between devices  27.8 us (19%)
  between operations  13.6 us (9%)
  Pallas kernels  13.1 us (9%)
  local copies, waits for them, and re-layouts  3.48 us (2%)
  other arithmetic  1.62 us (1%)
    all_gather x1, blocking collectives, on_device(): lax.all_gather(jnp.concatenate([q_mine, q_theirs]), 'y', axis=0, tiled=True)  24.9 us
    all_to_all x1, blocking collectives, exchange(): return lax.all_to_all(x, axes, 0, 0, tiled=True)  19.3 us
    all_to_all x3, starting transfers between devices, exchange(): return lax.all_to_all(x, axes, 0, 0, tiled=True)  17.6 us
    all_to_all x3, waiting for transfers between devices, exchange(): return lax.all_to_all(x, axes, 0, 0, tiled=True)  15 us
    pallas_call x2, Pallas kernels, project(): pl.pallas_call(kernel, in_specs=[vmem, vmem] + [pl.BlockSpec(memory_space...  10.1 us
    ppermute x1, waiting for transfers between devices, on_device(): lax.ppermute(q_part, 'x', down)  6.15 us
    ppermute x1, starting transfers between devices, on_device(): other = lax.ppermute(own, 'c', swap)  5.64 us
    ppermute x1, starting transfers between devices, on_device(): mine, theirs = (out[0], lax.ppermute(out[1], 'c', swap))  4.82 us
  transfers between devices with their start and end apart: 10, of which 8 were waited for; matrix products, arithmetic and copies ran while one was open for 1% of the time, Pallas kernels for 8%

profile of v9, /device:TPU:1, one launch (start us, length us, event | category | flops | bytes accessed | tf_op | source)
XLA Modules:
  0.0 143.2 jit_solution(18227386125433591051)
XLA Ops:
  6.5 1.1 fusion.2
  7.6 0.1 copy.5
  7.9 19.3 %all_to_all.20 = bf16[8,8,4096]{2,1,0:T(8,128)(2,1)} all-to-all(bf16[8,8,4096]{2,1,0:T(8,128)(2,1)S(1)} %bitcast.27), channel_id=1, replica_groups=mesh['x'=4,'y'=8,'c'=2,'z'=8] {'x','c'}, dimensions={0} | all-to-all | bytes 1048576 | tf_op jit(solution)/shard_map/all_to_all | solution.py:23
  27.3 1.5 %broadcast_in_dim.6 = bf16[8,256,512]{2,1,0:T(8,128)(2,1)} broadcast(bf16[256,512]{1,0:T(8,128)(2,1)S(1)} %copy-done.4), dimensions={1,2} | broadcast | bytes 2359296 | tf_op jit(solution)/shard_map/broadcast_in_dim | solution.py:19
  28.8 5.9 %all-to-all-start = ((bf16[8,256,512]{2,1,0:T(8,128)(2,1)}), bf16[8,256,512]{2,1,0:T(8,128)(2,1)S(1)}, u32[]{:S(2)}, u32[]{:S(2)}) async-start(bf16[8,256,512]{2,1,0:T(8,128)(2,1)} %broadcast_in_dim.6), calls=%async_computation | async-start | bytes 4194304 | tf_op jit(solution)/shard_map/all_to_all | solution.py:23
  34.7 0.1 broadcast_select_fusion.1
  34.9 3.2 %collective-permute-start = (bf16[4,4096]{1,0:T(4,128)(2,1)S(1)}, bf16[4,4096]{1,0:T(4,128)(2,1)S(1)}, u32[]{:S(2)}, u32[]{:S(2)}) collective-permute-start(bf16[4,4096]{1,0:T(4,128)(2,1)S(1)} %select_n.35), channel_id=1, source_target_pairs={{0,8},{8,0},{1,9},{9,1},{2,10},{10,2},{3,11},{11,3},{4,12},{12,4},... | collective-permute-start | bytes 98312 | tf_op jit(solution)/shard_map/ppermute | solution.py:222
  38.2 0.8 collective-permute-done
  39.0 24.9 %all_gather.6.refs_0_ = bf16[64,4096]{1,0:T(8,128)(2,1)S(1)} all-gather(bf16[8,4096]{1,0:T(8,128)(2,1)S(1)} %pad_maximum_fusion.2), channel_id=1, replica_groups=mesh['x'=4,'y'=8,'c'=2,'z'=8] {'y'}, dimensions={0}, use_global_device_ids=true | all-gather | bytes 589824 | tf_op jit(solution)/shard_map/all_gather | solution.py:223
  64.0 2.9 %collective-permute-start.1 = (bf16[64,4096]{1,0:T(8,128)(2,1)S(1)}, bf16[64,4096]{1,0:T(8,128)(2,1)}, u32[]{:S(2)}, u32[]{:S(2)}) collective-permute-start(bf16[64,4096]{1,0:T(8,128)(2,1)S(1)} %all_gather.6.refs_0_), channel_id=1, source_target_pairs={{0,384},{128,0},{256,128},{384,256},{1,385},{129,1},{257,129},{385... | collective-permute-start | bytes 1572872 | tf_op jit(solution)/shard_map/ppermute | solution.py:226
  66.9 2.4 %collective-permute-start.2 = (bf16[64,4096]{1,0:T(8,128)(2,1)S(1)}, bf16[64,4096]{1,0:T(8,128)(2,1)}, u32[]{:S(2)}, u32[]{:S(2)}) collective-permute-start(bf16[64,4096]{1,0:T(8,128)(2,1)S(1)} %all_gather.6.refs_0_), channel_id=1, source_target_pairs={{0,128},{128,256},{256,384},{384,0},{1,129},{129,257},{257,385},{3... | collective-permute-start | bytes 1572872 | tf_op jit(solution)/shard_map/ppermute | solution.py:226
  69.3 6.1 %collective-permute-done.1.refs_1_ = bf16[64,4096]{1,0:T(8,128)(2,1)} collective-permute-done((bf16[64,4096]{1,0:T(8,128)(2,1)S(1)}, bf16[64,4096]{1,0:T(8,128)(2,1)}, u32[]{:S(2)}, u32[]{:S(2)}) %collective-permute-start.1) | collective-permute-done | bytes 524320 | tf_op jit(solution)/shard_map/ppermute | solution.py:226
  75.4 4.0 %collective-permute-done.2.refs_3_ = bf16[64,4096]{1,0:T(8,128)(2,1)} collective-permute-done((bf16[64,4096]{1,0:T(8,128)(2,1)S(1)}, bf16[64,4096]{1,0:T(8,128)(2,1)}, u32[]{:S(2)}, u32[]{:S(2)}) %collective-permute-start.2) | collective-permute-done | bytes 524320 | tf_op jit(solution)/shard_map/ppermute | solution.py:226
  79.4 3.7 %all-to-all-done.own_ref = bf16[8,256,512]{2,1,0:T(8,128)(2,1)S(1)} async-done(((bf16[8,256,512]{2,1,0:T(8,128)(2,1)}), bf16[8,256,512]{2,1,0:T(8,128)(2,1)S(1)}, u32[]{:S(2)}, u32[]{:S(2)}) %all-to-all-start) | async-done | bytes 2097184 | tf_op jit(solution)/shard_map/all_to_all | solution.py:23
  83.1 5.6 %collective-permute-start.3 = (bf16[8,256,512]{2,1,0:T(8,128)(2,1)S(1)}, bf16[8,256,512]{2,1,0:T(8,128)(2,1)}, u32[]{:S(2)}, u32[]{:S(2)}) collective-permute-start(bf16[8,256,512]{2,1,0:T(8,128)(2,1)S(1)} %all-to-all-done.own_ref), channel_id=1, source_target_pairs={{0,8},{8,0},{1,9},{9,1},{2,10},{10,2},{3,11},{11,3},{4,12},{12,4},... | collective-permute-start | bytes 6291464 | tf_op jit(solution)/shard_map/ppermute | solution.py:228
  88.8 2.8 %collective-permute-start.4 = (bf16[64,4096]{1,0:T(8,128)(2,1)}, bf16[64,4096]{1,0:T(8,128)(2,1)}, u32[]{:S(2)}, u32[]{:S(2)}) collective-permute-start(bf16[64,4096]{1,0:T(8,128)(2,1)} %collective-permute-done.1.refs_1_), channel_id=1, source_target_pairs={{0,384},{128,0},{256,128},{384,256},{1,385},{129,1},{257,129},{385... | collective-permute-start | bytes 1572872 | tf_op jit(solution)/shard_map/ppermute | solution.py:229
  91.6 0.2 fusion.order_ref
  91.7 0.9 collective-permute-done.3.other_hbm
  92.7 5.6 %shard_map.38 = (bf16[2,2,2,256,128]{4,3,2,1,0:T(8,128)(2,1)S(1)}, f32[2,2,128,128]{3,2,1,0:T(8,128)S(1)}, bf16[32,8,128]{2,1,0:T(8,128)(2,1)}) custom-call(bf16[8,256,512]{2,1,0:T(8,128)(2,1)S(1)} %all-to-all-done.own_ref, bf16[512,512]{1,0:T(8,128)(2,1)S(1)} %fusion.order_ref, bf16[8,256,512]{2,1,0:T(8,128)(2,1)} %collective-permute-done.3.other_hbm, ...), custom_call_target="tpu_custom_call" | custom-call | tf_op jit(solution)/shard_map/pallas_call | solution.py:126
  98.3 7.8 %all-to-all-start.2 = ((bf16[32,8,128]{2,1,0:T(8,128)(2,1)}), bf16[32,8,128]{2,1,0:T(8,128)(2,1)S(1)}, u32[]{:S(2)}, u32[]{:S(2)}) async-start(bf16[32,8,128]{2,1,0:T(8,128)(2,1)} %get-tuple-element.16), calls=%async_computation.2 | async-start | bytes 131072 | tf_op jit(solution)/shard_map/all_to_all | solution.py:23
  106.2 1.3 shard_map.40.arrived_ref
  107.4 7.7 %all-to-all-done.2.total_ref = bf16[32,8,128]{2,1,0:T(8,128)(2,1)S(1)} async-done(((bf16[32,8,128]{2,1,0:T(8,128)(2,1)}), bf16[32,8,128]{2,1,0:T(8,128)(2,1)S(1)}, u32[]{:S(2)}, u32[]{:S(2)}) %all-to-all-start.2) | async-done | bytes 65568 | tf_op jit(solution)/shard_map/all_to_all | solution.py:23
  115.1 0.7 copy-done
  115.7 0.7 shard_map.41
  116.4 3.9 %all-to-all-start.3 = ((bf16[32,8,128]{2,1,0:T(8,128)(2,1)}), bf16[32,8,128]{2,1,0:T(8,128)(2,1)S(1)}, u32[]{:S(2)}, u32[]{:S(2)}) async-start(bf16[32,8,128]{2,1,0:T(8,128)(2,1)} %shard_map.41), calls=%async_computation.3 | async-start | bytes 131072 | tf_op jit(solution)/shard_map/all_to_all | solution.py:23
  120.4 4.5 %shard_map.37.query_ref = bf16[2,2,256,128]{3,2,1,0:T(8,128)(2,1)S(1)} custom-call(bf16[8,256,512]{2,1,0:T(8,128)(2,1)S(1)} %all-to-all-done.own_ref, bf16[256,256]{1,0:T(8,128)(2,1)S(1)} %fusion.1.order_ref, bf16[8,256,512]{2,1,0:T(8,128)(2,1)} %collective-permute-done.3.other_hbm, bf16[64,4096]{1,0:T(8,128)(2,1)} %copy-done.1, ...), custom_call_target="tpu_custom_call" | custom-call | tf_op jit(solution)/shard_map/pallas_call | solution.py:126
  124.9 0.7 shard_map.39.inner_ref
  125.6 3.6 %all-to-all-done.3.prior_ref = bf16[32,8,128]{2,1,0:T(8,128)(2,1)S(1)} async-done(((bf16[32,8,128]{2,1,0:T(8,128)(2,1)}), bf16[32,8,128]{2,1,0:T(8,128)(2,1)S(1)}, u32[]{:S(2)}, u32[]{:S(2)}) %all-to-all-start.3) | async-done | bytes 65568 | tf_op jit(solution)/shard_map/all_to_all | solution.py:23
  129.1 0.4 shard_map.42
  129.5 4.8 %collective-permute-start.5 = (bf16[2,256,128]{2,1,0:T(8,128)(2,1)S(1)}, bf16[2,256,128]{2,1,0:T(8,128)(2,1)S(1)}, u32[]{:S(2)}, u32[]{:S(2)}) collective-permute-start(bf16[2,256,128]{2,1,0:T(8,128)(2,1)S(1)} %slice_bitcast_fusion), channel_id=1, source_target_pairs={{0,8},{8,0},{1,9},{9,1},{2,10},{10,2},{3,11},{11,3},{4,12},{12,4},... | collective-permute-start | bytes 393224 | tf_op jit(solution)/shard_map/ppermute | solution.py:251
  134.4 1.0 collective-permute-done.5
  135.4 1.0 copy.7
  (25 shorter events, 0.5 us)
Async XLA Ops:
  6.5 20.7 %copy-start.4 = (bf16[256,512]{1,0:T(8,128)(2,1)S(1)}, bf16[256,512]{1,0:T(8,128)(2,1)}, u32[]{:S(2)}) copy-start(bf16[256,512]{1,0:T(8,128)(2,1)} %param.3) | copy-start | bytes 786436
  6.5 86.1 %all-gather.2.cloned.1.call-start = ((), (), s32[]{:S(2)}) async-start(), calls=%async_computation.4 | async-start | bytes 4718592 | tf_op jit(solution)/shard_map/all_gather | solution.py:217
  28.8 5.9 %copy-start.2 = (bf16[3,4096,2,2]{1,3,2,0:T(2,128)(2,1)S(1)}, bf16[3,4096,2,2]{1,3,2,0:T(2,128)(2,1)}, u32[]{:S(2)}) copy-start(bf16[3,4096,2,2]{1,3,2,0:T(2,128)(2,1)} %param.5) | copy-start | bytes 294916
  28.8 5.9 %copy-start.3 = (bf16[3,4096,2,2]{1,3,2,0:T(2,128)(2,1)S(1)}, bf16[3,4096,2,2]{1,3,2,0:T(2,128)(2,1)}, u32[]{:S(2)}) copy-start(bf16[3,4096,2,2]{1,3,2,0:T(2,128)(2,1)} %param.4) | copy-start | bytes 294916
  28.8 54.3 %all-to-all-start = ((bf16[8,256,512]{2,1,0:T(8,128)(2,1)}), bf16[8,256,512]{2,1,0:T(8,128)(2,1)S(1)}, u32[]{:S(2)}, u32[]{:S(2)}) async-start(bf16[8,256,512]{2,1,0:T(8,128)(2,1)} %broadcast_in_dim.6), calls=%async_computation | async-start | bytes 4194304 | tf_op jit(solution)/shard_map/all_to_all | solution.py:23
  34.9 4.1 %collective-permute-start = (bf16[4,4096]{1,0:T(4,128)(2,1)S(1)}, bf16[4,4096]{1,0:T(4,128)(2,1)S(1)}, u32[]{:S(2)}, u32[]{:S(2)}) collective-permute-start(bf16[4,4096]{1,0:T(4,128)(2,1)S(1)} %select_n.35), channel_id=1, source_target_pairs={{0,8},{8,0},{1,9},{9,1},{2,10},{10,2},{3,11},{11,3},{4,12},{12,4},... | collective-permute-start | bytes 98312 | tf_op jit(solution)/shard_map/ppermute | solution.py:222
  64.0 11.4 %copy-start.1 = (bf16[64,4096]{1,0:T(8,128)(2,1)}, bf16[64,4096]{1,0:T(8,128)(2,1)S(1)}, u32[]{:S(2)}) copy-start(bf16[64,4096]{1,0:T(8,128)(2,1)S(1)} %all_gather.6.refs_0_) | copy-start | bytes 1572868
  64.0 11.4 %collective-permute-start.1 = (bf16[64,4096]{1,0:T(8,128)(2,1)S(1)}, bf16[64,4096]{1,0:T(8,128)(2,1)}, u32[]{:S(2)}, u32[]{:S(2)}) collective-permute-start(bf16[64,4096]{1,0:T(8,128)(2,1)S(1)} %all_gather.6.refs_0_), channel_id=1, source_target_pairs={{0,384},{128,0},{256,128},{384,256},{1,385},{129,1},{257,129},{385... | collective-permute-start | bytes 1572872 | tf_op jit(solution)/shard_map/ppermute | solution.py:226
  66.9 12.5 %collective-permute-start.2 = (bf16[64,4096]{1,0:T(8,128)(2,1)S(1)}, bf16[64,4096]{1,0:T(8,128)(2,1)}, u32[]{:S(2)}, u32[]{:S(2)}) collective-permute-start(bf16[64,4096]{1,0:T(8,128)(2,1)S(1)} %all_gather.6.refs_0_), channel_id=1, source_target_pairs={{0,128},{128,256},{256,384},{384,0},{1,129},{129,257},{257,385},{3... | collective-permute-start | bytes 1572872 | tf_op jit(solution)/shard_map/ppermute | solution.py:226
  83.1 9.5 %collective-permute-start.3 = (bf16[8,256,512]{2,1,0:T(8,128)(2,1)S(1)}, bf16[8,256,512]{2,1,0:T(8,128)(2,1)}, u32[]{:S(2)}, u32[]{:S(2)}) collective-permute-start(bf16[8,256,512]{2,1,0:T(8,128)(2,1)S(1)} %all-to-all-done.own_ref), channel_id=1, source_target_pairs={{0,8},{8,0},{1,9},{9,1},{2,10},{10,2},{3,11},{11,3},{4,12},{12,4},... | collective-permute-start | bytes 6291464 | tf_op jit(solution)/shard_map/ppermute | solution.py:228
  88.8 17.4 %collective-permute-start.4 = (bf16[64,4096]{1,0:T(8,128)(2,1)}, bf16[64,4096]{1,0:T(8,128)(2,1)}, u32[]{:S(2)}, u32[]{:S(2)}) collective-permute-start(bf16[64,4096]{1,0:T(8,128)(2,1)} %collective-permute-done.1.refs_1_), channel_id=1, source_target_pairs={{0,384},{128,0},{256,128},{384,256},{1,385},{129,1},{257,129},{385... | collective-permute-start | bytes 1572872 | tf_op jit(solution)/shard_map/ppermute | solution.py:229
  98.3 16.8 %all-to-all-start.2 = ((bf16[32,8,128]{2,1,0:T(8,128)(2,1)}), bf16[32,8,128]{2,1,0:T(8,128)(2,1)S(1)}, u32[]{:S(2)}, u32[]{:S(2)}) async-start(bf16[32,8,128]{2,1,0:T(8,128)(2,1)} %get-tuple-element.16), calls=%async_computation.2 | async-start | bytes 131072 | tf_op jit(solution)/shard_map/all_to_all | solution.py:23
  115.1 0.7 copy-start
  116.4 12.7 %all-to-all-start.3 = ((bf16[32,8,128]{2,1,0:T(8,128)(2,1)}), bf16[32,8,128]{2,1,0:T(8,128)(2,1)S(1)}, u32[]{:S(2)}, u32[]{:S(2)}) async-start(bf16[32,8,128]{2,1,0:T(8,128)(2,1)} %shard_map.41), calls=%async_computation.3 | async-start | bytes 131072 | tf_op jit(solution)/shard_map/all_to_all | solution.py:23
  129.5 5.8 %collective-permute-start.5 = (bf16[2,256,128]{2,1,0:T(8,128)(2,1)S(1)}, bf16[2,256,128]{2,1,0:T(8,128)(2,1)S(1)}, u32[]{:S(2)}, u32[]{:S(2)}) collective-permute-start(bf16[2,256,128]{2,1,0:T(8,128)(2,1)S(1)} %slice_bitcast_fusion), channel_id=1, source_target_pairs={{0,8},{8,0},{1,9},{9,1},{2,10},{10,2},{3,11},{11,3},{4,12},{12,4},... | collective-permute-start | bytes 393224 | tf_op jit(solution)/shard_map/ppermute | solution.py:251
Sparse Core Ops, SparseCore 0:
  27.4 60.9 all-gather.1

commit v10 on v9

--- a/solution.py
+++ b/solution.py
@@ -189,7 +189,11 @@
 
 
 def call(kernel, out_shape, *args, unread=0):
-    spaces = [pltpu.VMEM] * (len(args) - unread) + [pl.ANY] * unread
+    spaces = [pltpu.VMEM] * (len(args) - unread) + [pltpu.HBM] * unread
+    args = [
+        pltpu.with_memory_space_constraint(arg, space) if space is pltpu.HBM else arg
+        for arg, space in zip(args, spaces)
+    ]
     return pl.pallas_call(
         kernel,
         out_shape=out_shape,

time: 144 us -> 143 us (level)
  no operation moved by 1% of the time
where the time goes in v10:
time: 143 us
  blocking collectives  44.3 us (31%)
  starting transfers between devices  39.3 us (27%)
  waiting for transfers between devices  27.8 us (19%)
  between operations  13.6 us (10%)
  Pallas kernels  13.1 us (9%)
  local copies, waits for them, and re-layouts  2.82 us (2%)
  other arithmetic  1.62 us (1%)
    all_gather x1, blocking collectives, on_device(): lax.all_gather(jnp.concatenate([q_mine, q_theirs]), 'y', axis=0, tiled=True)  24.9 us
    all_to_all x1, blocking collectives, exchange(): return lax.all_to_all(x, axes, 0, 0, tiled=True)  19.3 us
    all_to_all x3, starting transfers between devices, exchange(): return lax.all_to_all(x, axes, 0, 0, tiled=True)  17.6 us
    all_to_all x3, waiting for transfers between devices, exchange(): return lax.all_to_all(x, axes, 0, 0, tiled=True)  14.9 us
    pallas_call x2, Pallas kernels, project(): pl.pallas_call(kernel, in_specs=[vmem, vmem] + [pl.BlockSpec(memory_space...  10.1 us
    ppermute x1, waiting for transfers between devices, on_device(): lax.ppermute(q_part, 'x', down)  6.07 us
    ppermute x1, starting transfers between devices, on_device(): other = lax.ppermute(own, 'c', swap)  5.64 us
    ppermute x1, starting transfers between devices, on_device(): mine, theirs = (out[0], lax.ppermute(out[1], 'c', swap))  4.81 us
  transfers between devices with their start and end apart: 10, of which 8 were waited for; matrix products, arithmetic and copies ran while one was open for 1% of the time, Pallas kernels for 8%

profile of v10, /device:TPU:1, one launch (start us, length us, event | category | flops | bytes accessed | tf_op | source)
XLA Modules:
  0.0 142.6 jit_solution(8979548004970557890)
XLA Ops:
  6.5 1.1 fusion.2
  7.6 0.1 copy.5
  7.9 19.3 %all_to_all.20 = bf16[8,8,4096]{2,1,0:T(8,128)(2,1)} all-to-all(bf16[8,8,4096]{2,1,0:T(8,128)(2,1)S(1)} %bitcast.27), channel_id=1, replica_groups=mesh['x'=4,'y'=8,'c'=2,'z'=8] {'x','c'}, dimensions={0} | all-to-all | bytes 1048576 | tf_op jit(solution)/shard_map/all_to_all | solution.py:23
  27.3 1.5 %broadcast_in_dim.6 = bf16[8,256,512]{2,1,0:T(8,128)(2,1)} broadcast(bf16[256,512]{1,0:T(8,128)(2,1)S(1)} %copy-done.3), dimensions={1,2} | broadcast | bytes 2359296 | tf_op jit(solution)/shard_map/broadcast_in_dim | solution.py:19
  28.8 5.9 %all-to-all-start = ((bf16[8,256,512]{2,1,0:T(8,128)(2,1)}), bf16[8,256,512]{2,1,0:T(8,128)(2,1)S(1)}, u32[]{:S(2)}, u32[]{:S(2)}) async-start(bf16[8,256,512]{2,1,0:T(8,128)(2,1)} %broadcast_in_dim.6), calls=%async_computation | async-start | bytes 4194304 | tf_op jit(solution)/shard_map/all_to_all | solution.py:23
  34.7 0.1 broadcast_select_fusion.1
  34.9 3.2 %collective-permute-start = (bf16[4,4096]{1,0:T(4,128)(2,1)S(1)}, bf16[4,4096]{1,0:T(4,128)(2,1)S(1)}, u32[]{:S(2)}, u32[]{:S(2)}) collective-permute-start(bf16[4,4096]{1,0:T(4,128)(2,1)S(1)} %select_n.35), channel_id=1, source_target_pairs={{0,8},{8,0},{1,9},{9,1},{2,10},{10,2},{3,11},{11,3},{4,12},{12,4},... | collective-permute-start | bytes 98312 | tf_op jit(solution)/shard_map/ppermute | solution.py:226
  38.2 0.8 collective-permute-done
  39.0 24.9 %all_gather.6.refs_0_ = bf16[64,4096]{1,0:T(8,128)(2,1)S(1)} all-gather(bf16[8,4096]{1,0:T(8,128)(2,1)S(1)} %pad_maximum_fusion.2), channel_id=1, replica_groups=mesh['x'=4,'y'=8,'c'=2,'z'=8] {'y'}, dimensions={0}, use_global_device_ids=true | all-gather | bytes 589824 | tf_op jit(solution)/shard_map/all_gather | solution.py:227
  64.0 2.9 %collective-permute-start.1 = (bf16[64,4096]{1,0:T(8,128)(2,1)S(1)}, bf16[64,4096]{1,0:T(8,128)(2,1)}, u32[]{:S(2)}, u32[]{:S(2)}) collective-permute-start(bf16[64,4096]{1,0:T(8,128)(2,1)S(1)} %all_gather.6.refs_0_), channel_id=1, source_target_pairs={{0,384},{128,0},{256,128},{384,256},{1,385},{129,1},{257,129},{385... | collective-permute-start | bytes 1572872 | tf_op jit(solution)/shard_map/ppermute | solution.py:230
  66.9 2.3 %collective-permute-start.2 = (bf16[64,4096]{1,0:T(8,128)(2,1)S(1)}, bf16[64,4096]{1,0:T(8,128)(2,1)}, u32[]{:S(2)}, u32[]{:S(2)}) collective-permute-start(bf16[64,4096]{1,0:T(8,128)(2,1)S(1)} %all_gather.6.refs_0_), channel_id=1, source_target_pairs={{0,128},{128,256},{256,384},{384,0},{1,129},{129,257},{257,385},{3... | collective-permute-start | bytes 1572872 | tf_op jit(solution)/shard_map/ppermute | solution.py:230
  69.3 6.1 %collective-permute-done.1.refs_1_ = bf16[64,4096]{1,0:T(8,128)(2,1)} collective-permute-done((bf16[64,4096]{1,0:T(8,128)(2,1)S(1)}, bf16[64,4096]{1,0:T(8,128)(2,1)}, u32[]{:S(2)}, u32[]{:S(2)}) %collective-permute-start.1) | collective-permute-done | bytes 524320 | tf_op jit(solution)/shard_map/ppermute | solution.py:230
  75.4 4.2 %collective-permute-done.2.refs_3_ = bf16[64,4096]{1,0:T(8,128)(2,1)} collective-permute-done((bf16[64,4096]{1,0:T(8,128)(2,1)S(1)}, bf16[64,4096]{1,0:T(8,128)(2,1)}, u32[]{:S(2)}, u32[]{:S(2)}) %collective-permute-start.2) | collective-permute-done | bytes 524320 | tf_op jit(solution)/shard_map/ppermute | solution.py:230
  79.5 3.6 %all-to-all-done.own_ref = bf16[8,256,512]{2,1,0:T(8,128)(2,1)S(1)} async-done(((bf16[8,256,512]{2,1,0:T(8,128)(2,1)}), bf16[8,256,512]{2,1,0:T(8,128)(2,1)S(1)}, u32[]{:S(2)}, u32[]{:S(2)}) %all-to-all-start) | async-done | bytes 2097184 | tf_op jit(solution)/shard_map/all_to_all | solution.py:23
  83.1 5.6 %collective-permute-start.3 = (bf16[8,256,512]{2,1,0:T(8,128)(2,1)S(1)}, bf16[8,256,512]{2,1,0:T(8,128)(2,1)}, u32[]{:S(2)}, u32[]{:S(2)}) collective-permute-start(bf16[8,256,512]{2,1,0:T(8,128)(2,1)S(1)} %all-to-all-done.own_ref), channel_id=1, source_target_pairs={{0,8},{8,0},{1,9},{9,1},{2,10},{10,2},{3,11},{11,3},{4,12},{12,4},... | collective-permute-start | bytes 6291464 | tf_op jit(solution)/shard_map/ppermute | solution.py:232
  88.8 2.8 %collective-permute-start.4 = (bf16[64,4096]{1,0:T(8,128)(2,1)}, bf16[64,4096]{1,0:T(8,128)(2,1)}, u32[]{:S(2)}, u32[]{:S(2)}) collective-permute-start(bf16[64,4096]{1,0:T(8,128)(2,1)} %collective-permute-done.1.refs_1_), channel_id=1, source_target_pairs={{0,384},{128,0},{256,128},{384,256},{1,385},{129,1},{257,129},{385... | collective-permute-start | bytes 1572872 | tf_op jit(solution)/shard_map/ppermute | solution.py:233
  91.6 0.2 fusion.order_ref
  91.7 0.9 collective-permute-done.3.other_hbm
  92.7 5.6 %shard_map.38 = (bf16[2,2,2,256,128]{4,3,2,1,0:T(8,128)(2,1)S(1)}, f32[2,2,128,128]{3,2,1,0:T(8,128)S(1)}, bf16[32,8,128]{2,1,0:T(8,128)(2,1)}) custom-call(bf16[8,256,512]{2,1,0:T(8,128)(2,1)S(1)} %all-to-all-done.own_ref, bf16[512,512]{1,0:T(8,128)(2,1)S(1)} %fusion.order_ref, bf16[8,256,512]{2,1,0:T(8,128)(2,1)} %collective-permute-done.3.other_hbm, ...), custom_call_target="tpu_custom_call" | custom-call | tf_op jit(solution)/shard_map/pallas_call | solution.py:126
  98.3 7.8 %all-to-all-start.2 = ((bf16[32,8,128]{2,1,0:T(8,128)(2,1)}), bf16[32,8,128]{2,1,0:T(8,128)(2,1)S(1)}, u32[]{:S(2)}, u32[]{:S(2)}) async-start(bf16[32,8,128]{2,1,0:T(8,128)(2,1)} %get-tuple-element.16), calls=%async_computation.2 | async-start | bytes 131072 | tf_op jit(solution)/shard_map/all_to_all | solution.py:23
  106.2 1.3 shard_map.40.arrived_ref
  107.4 7.7 %all-to-all-done.2.total_ref = bf16[32,8,128]{2,1,0:T(8,128)(2,1)S(1)} async-done(((bf16[32,8,128]{2,1,0:T(8,128)(2,1)}), bf16[32,8,128]{2,1,0:T(8,128)(2,1)S(1)}, u32[]{:S(2)}, u32[]{:S(2)}) %all-to-all-start.2) | async-done | bytes 65568 | tf_op jit(solution)/shard_map/all_to_all | solution.py:23
  115.1 0.7 shard_map.41
  115.8 3.9 %all-to-all-start.3 = ((bf16[32,8,128]{2,1,0:T(8,128)(2,1)}), bf16[32,8,128]{2,1,0:T(8,128)(2,1)S(1)}, u32[]{:S(2)}, u32[]{:S(2)}) async-start(bf16[32,8,128]{2,1,0:T(8,128)(2,1)} %shard_map.41), calls=%async_computation.3 | async-start | bytes 131072 | tf_op jit(solution)/shard_map/all_to_all | solution.py:23
  119.6 0.1 fusion.1.order_ref
  119.7 4.5 %shard_map.37.query_ref = bf16[2,2,256,128]{3,2,1,0:T(8,128)(2,1)S(1)} custom-call(bf16[8,256,512]{2,1,0:T(8,128)(2,1)S(1)} %all-to-all-done.own_ref, bf16[256,256]{1,0:T(8,128)(2,1)S(1)} %fusion.1.order_ref, bf16[8,256,512]{2,1,0:T(8,128)(2,1)} %collective-permute-done.3.other_hbm, bf16[64,4096]{1,0:T(8,128)(2,1)} %copy-done, ...), custom_call_target="tpu_custom_call" | custom-call | tf_op jit(solution)/shard_map/pallas_call | solution.py:126
  124.2 0.7 shard_map.39.inner_ref
  124.9 3.6 %all-to-all-done.3.prior_ref = bf16[32,8,128]{2,1,0:T(8,128)(2,1)S(1)} async-done(((bf16[32,8,128]{2,1,0:T(8,128)(2,1)}), bf16[32,8,128]{2,1,0:T(8,128)(2,1)S(1)}, u32[]{:S(2)}, u32[]{:S(2)}) %all-to-all-start.3) | async-done | bytes 65568 | tf_op jit(solution)/shard_map/all_to_all | solution.py:23
  128.5 0.4 shard_map.42
  128.9 4.8 %collective-permute-start.5 = (bf16[2,256,128]{2,1,0:T(8,128)(2,1)S(1)}, bf16[2,256,128]{2,1,0:T(8,128)(2,1)S(1)}, u32[]{:S(2)}, u32[]{:S(2)}) collective-permute-start(bf16[2,256,128]{2,1,0:T(8,128)(2,1)S(1)} %slice_bitcast_fusion), channel_id=1, source_target_pairs={{0,8},{8,0},{1,9},{9,1},{2,10},{10,2},{3,11},{11,3},{4,12},{12,4},... | collective-permute-start | bytes 393224 | tf_op jit(solution)/shard_map/ppermute | solution.py:255
  133.7 1.0 collective-permute-done.5
  134.7 1.0 copy.7
  (23 shorter events, 0.4 us)
Async XLA Ops:
  6.5 20.7 %copy-start.3 = (bf16[256,512]{1,0:T(8,128)(2,1)S(1)}, bf16[256,512]{1,0:T(8,128)(2,1)}, u32[]{:S(2)}) copy-start(bf16[256,512]{1,0:T(8,128)(2,1)} %param.3) | copy-start | bytes 786436
  6.5 86.1 %all-gather.2.cloned.1.call-start = ((), (), s32[]{:S(2)}) async-start(), calls=%async_computation.4 | async-start | bytes 4718592 | tf_op jit(solution)/shard_map/all_gather | solution.py:221
  28.8 5.9 %copy-start.1 = (bf16[3,4096,2,2]{1,3,2,0:T(2,128)(2,1)S(1)}, bf16[3,4096,2,2]{1,3,2,0:T(2,128)(2,1)}, u32[]{:S(2)}) copy-start(bf16[3,4096,2,2]{1,3,2,0:T(2,128)(2,1)} %param.5) | copy-start | bytes 294916
  28.8 5.9 %copy-start.2 = (bf16[3,4096,2,2]{1,3,2,0:T(2,128)(2,1)S(1)}, bf16[3,4096,2,2]{1,3,2,0:T(2,128)(2,1)}, u32[]{:S(2)}) copy-start(bf16[3,4096,2,2]{1,3,2,0:T(2,128)(2,1)} %param.4) | copy-start | bytes 294916
  28.8 54.3 %all-to-all-start = ((bf16[8,256,512]{2,1,0:T(8,128)(2,1)}), bf16[8,256,512]{2,1,0:T(8,128)(2,1)S(1)}, u32[]{:S(2)}, u32[]{:S(2)}) async-start(bf16[8,256,512]{2,1,0:T(8,128)(2,1)} %broadcast_in_dim.6), calls=%async_computation | async-start | bytes 4194304 | tf_op jit(solution)/shard_map/all_to_all | solution.py:23
  34.9 4.1 %collective-permute-start = (bf16[4,4096]{1,0:T(4,128)(2,1)S(1)}, bf16[4,4096]{1,0:T(4,128)(2,1)S(1)}, u32[]{:S(2)}, u32[]{:S(2)}) collective-permute-start(bf16[4,4096]{1,0:T(4,128)(2,1)S(1)} %select_n.35), channel_id=1, source_target_pairs={{0,8},{8,0},{1,9},{9,1},{2,10},{10,2},{3,11},{11,3},{4,12},{12,4},... | collective-permute-start | bytes 98312 | tf_op jit(solution)/shard_map/ppermute | solution.py:226
  64.0 11.4 %copy-start = (bf16[64,4096]{1,0:T(8,128)(2,1)}, bf16[64,4096]{1,0:T(8,128)(2,1)S(1)}, u32[]{:S(2)}) copy-start(bf16[64,4096]{1,0:T(8,128)(2,1)S(1)} %all_gather.6.refs_0_) | copy-start | bytes 1572868
  64.0 11.4 %collective-permute-start.1 = (bf16[64,4096]{1,0:T(8,128)(2,1)S(1)}, bf16[64,4096]{1,0:T(8,128)(2,1)}, u32[]{:S(2)}, u32[]{:S(2)}) collective-permute-start(bf16[64,4096]{1,0:T(8,128)(2,1)S(1)} %all_gather.6.refs_0_), channel_id=1, source_target_pairs={{0,384},{128,0},{256,128},{384,256},{1,385},{129,1},{257,129},{385... | collective-permute-start | bytes 1572872 | tf_op jit(solution)/shard_map/ppermute | solution.py:230
  66.9 12.6 %collective-permute-start.2 = (bf16[64,4096]{1,0:T(8,128)(2,1)S(1)}, bf16[64,4096]{1,0:T(8,128)(2,1)}, u32[]{:S(2)}, u32[]{:S(2)}) collective-permute-start(bf16[64,4096]{1,0:T(8,128)(2,1)S(1)} %all_gather.6.refs_0_), channel_id=1, source_target_pairs={{0,128},{128,256},{256,384},{384,0},{1,129},{129,257},{257,385},{3... | collective-permute-start | bytes 1572872 | tf_op jit(solution)/shard_map/ppermute | solution.py:230
  83.1 9.5 %collective-permute-start.3 = (bf16[8,256,512]{2,1,0:T(8,128)(2,1)S(1)}, bf16[8,256,512]{2,1,0:T(8,128)(2,1)}, u32[]{:S(2)}, u32[]{:S(2)}) collective-permute-start(bf16[8,256,512]{2,1,0:T(8,128)(2,1)S(1)} %all-to-all-done.own_ref), channel_id=1, source_target_pairs={{0,8},{8,0},{1,9},{9,1},{2,10},{10,2},{3,11},{11,3},{4,12},{12,4},... | collective-permute-start | bytes 6291464 | tf_op jit(solution)/shard_map/ppermute | solution.py:232
  88.8 17.4 %collective-permute-start.4 = (bf16[64,4096]{1,0:T(8,128)(2,1)}, bf16[64,4096]{1,0:T(8,128)(2,1)}, u32[]{:S(2)}, u32[]{:S(2)}) collective-permute-start(bf16[64,4096]{1,0:T(8,128)(2,1)} %collective-permute-done.1.refs_1_), channel_id=1, source_target_pairs={{0,384},{128,0},{256,128},{384,256},{1,385},{129,1},{257,129},{385... | collective-permute-start | bytes 1572872 | tf_op jit(solution)/shard_map/ppermute | solution.py:233
  98.3 16.8 %all-to-all-start.2 = ((bf16[32,8,128]{2,1,0:T(8,128)(2,1)}), bf16[32,8,128]{2,1,0:T(8,128)(2,1)S(1)}, u32[]{:S(2)}, u32[]{:S(2)}) async-start(bf16[32,8,128]{2,1,0:T(8,128)(2,1)} %get-tuple-element.16), calls=%async_computation.2 | async-start | bytes 131072 | tf_op jit(solution)/shard_map/all_to_all | solution.py:23
  115.8 12.7 %all-to-all-start.3 = ((bf16[32,8,128]{2,1,0:T(8,128)(2,1)}), bf16[32,8,128]{2,1,0:T(8,128)(2,1)S(1)}, u32[]{:S(2)}, u32[]{:S(2)}) async-start(bf16[32,8,128]{2,1,0:T(8,128)(2,1)} %shard_map.41), calls=%async_computation.3 | async-start | bytes 131072 | tf_op jit(solution)/shard_map/all_to_all | solution.py:23
  128.9 5.8 %collective-permute-start.5 = (bf16[2,256,128]{2,1,0:T(8,128)(2,1)S(1)}, bf16[2,256,128]{2,1,0:T(8,128)(2,1)S(1)}, u32[]{:S(2)}, u32[]{:S(2)}) collective-permute-start(bf16[2,256,128]{2,1,0:T(8,128)(2,1)S(1)} %slice_bitcast_fusion), channel_id=1, source_target_pairs={{0,8},{8,0},{1,9},{9,1},{2,10},{10,2},{3,11},{11,3},{4,12},{12,4},... | collective-permute-start | bytes 393224 | tf_op jit(solution)/shard_map/ppermute | solution.py:255
Sparse Core Ops, SparseCore 0:
  27.4 60.9 all-gather.1

commit v11 on v10

--- a/solution.py
+++ b/solution.py
@@ -84,14 +84,18 @@
         for i in pieces:
             for copy in copies[i]:
                 copy.wait()
-        tokens = jnp.concatenate(
-            [jnp.concatenate([ref[i] for i in pieces], 1) for ref in (own_ref, other)], 0
-        )
-        part = lax.dot_general(tokens, weight[k], NT, preferred_element_type=F32)
-        if k == 0:
-            acc[...] = part
-        else:
-            acc[...] += part
+        for block, ref in enumerate((own_ref, other)):
+            part = None
+            for i in pieces:
+                one = lax.dot_general(
+                    ref[i], weight[k, :, (i % PER) * PIECE : (i % PER + 1) * PIECE], NT,
+                    preferred_element_type=F32,
+                )
+                part = one if part is None else part + one
+            if k == 0:
+                acc[block * TOK : (block + 1) * TOK] = part
+            else:
+                acc[block * TOK : (block + 1) * TOK] += part
 
 
 def query_kernel(own_ref, order_ref, other_hbm, *refs):
@@ -174,10 +178,10 @@
             out_ref[block, s] = jnp.dot(weights, kv_ref[1, block, s], preferred_element_type=F32)
 
 
-def cross_kernel(query_ref, inner_ref, state_ref, prior_ref, out_ref):
+def cross_kernel(query_ref, inner_ref, state_ref, prior_ref, mine_ref, theirs_ref):
     core = lax.axis_index("c")
     prior = prior_ref[...].astype(F32).reshape(2, HD, HD)
-    for block in range(2):
+    for block, out_ref in enumerate((mine_ref, theirs_ref)):
         later = jnp.where(core == (1 - block), jnp.float32(1.0), jnp.float32(0.0))
         for s in range(2):
             carried = (prior[s] + later * state_ref[1 - block, s]).astype(BF16)
@@ -185,7 +189,7 @@
                 query_ref[block, s], carried, preferred_element_type=F32
             )
             scale = lax.rsqrt(jnp.mean(combined * combined, axis=-1, keepdims=True) + 1e-05)
-            out_ref[block, s] = (combined * scale).astype(BF16)
+            out_ref[s] = (combined * scale).astype(BF16)
 
 
 def call(kernel, out_shape, *args, unread=0):
@@ -198,7 +202,7 @@
         kernel,
         out_shape=out_shape,
         in_specs=[pl.BlockSpec(memory_space=space) for space in spaces],
-        out_specs=pl.BlockSpec(memory_space=pltpu.VMEM),
+        out_specs=jax.tree.map(lambda s: pl.BlockSpec(memory_space=pltpu.VMEM), out_shape),
         compiler_params=pltpu.CompilerParams(vmem_limit_bytes=12 << 20),
     )(*args)
 
@@ -251,8 +255,9 @@
     prior = exchange(slices, ("x", "y"))
 
     inner = call(inner_kernel, shape(2, 2, TOK, HD, dtype=F32), query, kv)
-    out = call(cross_kernel, shape(2, 2, TOK, HD), query, inner, state, prior)
-    mine, theirs = out[0], lax.ppermute(out[1], "c", swap)
+    block = shape(2, TOK, HD)
+    mine, sent = call(cross_kernel, (block, block), query, inner, state, prior)
+    theirs = lax.ppermute(sent, "c", swap)
     first = jnp.where(c == 0, mine, theirs)
     second = jnp.where(c == 0, theirs, mine)
     return jnp.stack([first, second], axis=2)

time: 143 us -> 143 us (level)
  no operation moved by 1% of the time
where the time goes in v11:
time: 143 us; the launch traced here: 142 us
  blocking collectives  44.3 us (31%)
  starting transfers between devices  39.3 us (27%)
  waiting for transfers between devices  28.7 us (20%)
  between operations  13.6 us (10%)
  Pallas kernels  12 us (8%)
  local copies, waits for them, and re-layouts  2.8 us (2%)
  other arithmetic  1.62 us (1%)
    all_gather x1, blocking collectives, on_device(): lax.all_gather(jnp.concatenate([q_mine, q_theirs]), 'y', axis=0, tiled=True)  24.9 us
    all_to_all x1, blocking collectives, exchange(): return lax.all_to_all(x, axes, 0, 0, tiled=True)  19.3 us
    all_to_all x3, starting transfers between devices, exchange(): return lax.all_to_all(x, axes, 0, 0, tiled=True)  17.6 us
    all_to_all x3, waiting for transfers between devices, exchange(): return lax.all_to_all(x, axes, 0, 0, tiled=True)  15.9 us
    pallas_call x2, Pallas kernels, project(): pl.pallas_call(kernel, in_specs=[vmem, vmem] + [pl.BlockSpec(memory_space...  9.08 us
    ppermute x1, waiting for transfers between devices, on_device(): lax.ppermute(q_part, 'x', down)  6.15 us
    ppermute x1, starting transfers between devices, on_device(): other = lax.ppermute(own, 'c', swap)  5.64 us
    ppermute x1, starting transfers between devices, on_device(): theirs = lax.ppermute(sent, 'c', swap)  4.82 us
  transfers between devices with their start and end apart: 10, of which 8 were waited for; matrix products, arithmetic and copies ran while one was open for 1% of the time, Pallas kernels for 8%

profile of v11, /device:TPU:1, one launch (start us, length us, event | category | flops | bytes accessed | tf_op | source)
XLA Modules:
  0.0 142.4 jit_solution(17589049538311218254)
XLA Ops:
  6.5 1.1 fusion.2
  7.6 0.1 copy.5
  7.9 19.3 %all_to_all.20 = bf16[8,8,4096]{2,1,0:T(8,128)(2,1)} all-to-all(bf16[8,8,4096]{2,1,0:T(8,128)(2,1)S(1)} %bitcast.19), channel_id=1, replica_groups=mesh['x'=4,'y'=8,'c'=2,'z'=8] {'x','c'}, dimensions={0} | all-to-all | bytes 1048576 | tf_op jit(solution)/shard_map/all_to_all | solution.py:23
  27.3 1.5 %broadcast_in_dim.6 = bf16[8,256,512]{2,1,0:T(8,128)(2,1)} broadcast(bf16[256,512]{1,0:T(8,128)(2,1)S(1)} %copy-done.3), dimensions={1,2} | broadcast | bytes 2359296 | tf_op jit(solution)/shard_map/broadcast_in_dim | solution.py:19
  28.8 5.9 %all-to-all-start = ((bf16[8,256,512]{2,1,0:T(8,128)(2,1)}), bf16[8,256,512]{2,1,0:T(8,128)(2,1)S(1)}, u32[]{:S(2)}, u32[]{:S(2)}) async-start(bf16[8,256,512]{2,1,0:T(8,128)(2,1)} %broadcast_in_dim.6), calls=%async_computation | async-start | bytes 4194304 | tf_op jit(solution)/shard_map/all_to_all | solution.py:23
  34.7 0.1 broadcast_select_fusion.1
  34.9 3.2 %collective-permute-start = (bf16[4,4096]{1,0:T(4,128)(2,1)S(1)}, bf16[4,4096]{1,0:T(4,128)(2,1)S(1)}, u32[]{:S(2)}, u32[]{:S(2)}) collective-permute-start(bf16[4,4096]{1,0:T(4,128)(2,1)S(1)} %select_n.35), channel_id=1, source_target_pairs={{0,8},{8,0},{1,9},{9,1},{2,10},{10,2},{3,11},{11,3},{4,12},{12,4},... | collective-permute-start | bytes 98312 | tf_op jit(solution)/shard_map/ppermute | solution.py:230
  38.2 0.8 collective-permute-done
  39.0 24.9 %all_gather.6.refs_0_ = bf16[64,4096]{1,0:T(8,128)(2,1)S(1)} all-gather(bf16[8,4096]{1,0:T(8,128)(2,1)S(1)} %pad_maximum_fusion.2), channel_id=1, replica_groups=mesh['x'=4,'y'=8,'c'=2,'z'=8] {'y'}, dimensions={0}, use_global_device_ids=true | all-gather | bytes 589824 | tf_op jit(solution)/shard_map/all_gather | solution.py:231
  64.0 2.9 %collective-permute-start.1 = (bf16[64,4096]{1,0:T(8,128)(2,1)S(1)}, bf16[64,4096]{1,0:T(8,128)(2,1)}, u32[]{:S(2)}, u32[]{:S(2)}) collective-permute-start(bf16[64,4096]{1,0:T(8,128)(2,1)S(1)} %all_gather.6.refs_0_), channel_id=1, source_target_pairs={{0,384},{128,0},{256,128},{384,256},{1,385},{129,1},{257,129},{385... | collective-permute-start | bytes 1572872 | tf_op jit(solution)/shard_map/ppermute | solution.py:234
  66.9 2.4 %collective-permute-start.2 = (bf16[64,4096]{1,0:T(8,128)(2,1)S(1)}, bf16[64,4096]{1,0:T(8,128)(2,1)}, u32[]{:S(2)}, u32[]{:S(2)}) collective-permute-start(bf16[64,4096]{1,0:T(8,128)(2,1)S(1)} %all_gather.6.refs_0_), channel_id=1, source_target_pairs={{0,128},{128,256},{256,384},{384,0},{1,129},{129,257},{257,385},{3... | collective-permute-start | bytes 1572872 | tf_op jit(solution)/shard_map/ppermute | solution.py:234
  69.3 6.1 %collective-permute-done.1.refs_1_ = bf16[64,4096]{1,0:T(8,128)(2,1)} collective-permute-done((bf16[64,4096]{1,0:T(8,128)(2,1)S(1)}, bf16[64,4096]{1,0:T(8,128)(2,1)}, u32[]{:S(2)}, u32[]{:S(2)}) %collective-permute-start.1) | collective-permute-done | bytes 524320 | tf_op jit(solution)/shard_map/ppermute | solution.py:234
  75.4 4.0 %collective-permute-done.2.refs_3_ = bf16[64,4096]{1,0:T(8,128)(2,1)} collective-permute-done((bf16[64,4096]{1,0:T(8,128)(2,1)S(1)}, bf16[64,4096]{1,0:T(8,128)(2,1)}, u32[]{:S(2)}, u32[]{:S(2)}) %collective-permute-start.2) | collective-permute-done | bytes 524320 | tf_op jit(solution)/shard_map/ppermute | solution.py:234
  79.4 3.7 %all-to-all-done.own_ref = bf16[8,256,512]{2,1,0:T(8,128)(2,1)S(1)} async-done(((bf16[8,256,512]{2,1,0:T(8,128)(2,1)}), bf16[8,256,512]{2,1,0:T(8,128)(2,1)S(1)}, u32[]{:S(2)}, u32[]{:S(2)}) %all-to-all-start) | async-done | bytes 2097184 | tf_op jit(solution)/shard_map/all_to_all | solution.py:23
  83.1 5.6 %collective-permute-start.3 = (bf16[8,256,512]{2,1,0:T(8,128)(2,1)S(1)}, bf16[8,256,512]{2,1,0:T(8,128)(2,1)}, u32[]{:S(2)}, u32[]{:S(2)}) collective-permute-start(bf16[8,256,512]{2,1,0:T(8,128)(2,1)S(1)} %all-to-all-done.own_ref), channel_id=1, source_target_pairs={{0,8},{8,0},{1,9},{9,1},{2,10},{10,2},{3,11},{11,3},{4,12},{12,4},... | collective-permute-start | bytes 6291464 | tf_op jit(solution)/shard_map/ppermute | solution.py:236
  88.8 2.8 %collective-permute-start.4 = (bf16[64,4096]{1,0:T(8,128)(2,1)}, bf16[64,4096]{1,0:T(8,128)(2,1)}, u32[]{:S(2)}, u32[]{:S(2)}) collective-permute-start(bf16[64,4096]{1,0:T(8,128)(2,1)} %collective-permute-done.1.refs_1_), channel_id=1, source_target_pairs={{0,384},{128,0},{256,128},{384,256},{1,385},{129,1},{257,129},{385... | collective-permute-start | bytes 1572872 | tf_op jit(solution)/shard_map/ppermute | solution.py:237
  91.6 0.2 fusion.order_ref
  91.7 0.9 collective-permute-done.3.other_hbm
  92.7 5.5 %shard_map.38 = (bf16[2,2,2,256,128]{4,3,2,1,0:T(8,128)(2,1)S(1)}, f32[2,2,128,128]{3,2,1,0:T(8,128)S(1)}, bf16[32,8,128]{2,1,0:T(8,128)(2,1)}) custom-call(bf16[8,256,512]{2,1,0:T(8,128)(2,1)S(1)} %all-to-all-done.own_ref, bf16[512,512]{1,0:T(8,128)(2,1)S(1)} %fusion.order_ref, bf16[8,256,512]{2,1,0:T(8,128)(2,1)} %collective-permute-done.3.other_hbm, ...), custom_call_target="tpu_custom_call" | custom-call | tf_op jit(solution)/shard_map/pallas_call | solution.py:130
  98.2 7.8 %all-to-all-start.2 = ((bf16[32,8,128]{2,1,0:T(8,128)(2,1)}), bf16[32,8,128]{2,1,0:T(8,128)(2,1)S(1)}, u32[]{:S(2)}, u32[]{:S(2)}) async-start(bf16[32,8,128]{2,1,0:T(8,128)(2,1)} %get-tuple-element.18), calls=%async_computation.2 | async-start | bytes 131072 | tf_op jit(solution)/shard_map/all_to_all | solution.py:23
  106.0 1.3 shard_map.40.arrived_ref
  107.3 7.7 %all-to-all-done.2.total_ref = bf16[32,8,128]{2,1,0:T(8,128)(2,1)S(1)} async-done(((bf16[32,8,128]{2,1,0:T(8,128)(2,1)}), bf16[32,8,128]{2,1,0:T(8,128)(2,1)S(1)}, u32[]{:S(2)}, u32[]{:S(2)}) %all-to-all-start.2) | async-done | bytes 65568 | tf_op jit(solution)/shard_map/all_to_all | solution.py:23
  115.0 0.7 shard_map.41
  115.6 3.9 %all-to-all-start.3 = ((bf16[32,8,128]{2,1,0:T(8,128)(2,1)}), bf16[32,8,128]{2,1,0:T(8,128)(2,1)S(1)}, u32[]{:S(2)}, u32[]{:S(2)}) async-start(bf16[32,8,128]{2,1,0:T(8,128)(2,1)} %shard_map.41), calls=%async_computation.3 | async-start | bytes 131072 | tf_op jit(solution)/shard_map/all_to_all | solution.py:23
  119.5 0.1 fusion.1.order_ref
  119.6 3.6 %shard_map.37.query_ref = bf16[2,2,256,128]{3,2,1,0:T(8,128)(2,1)S(1)} custom-call(bf16[8,256,512]{2,1,0:T(8,128)(2,1)S(1)} %all-to-all-done.own_ref, bf16[256,256]{1,0:T(8,128)(2,1)S(1)} %fusion.1.order_ref, bf16[8,256,512]{2,1,0:T(8,128)(2,1)} %collective-permute-done.3.other_hbm, bf16[64,4096]{1,0:T(8,128)(2,1)} %copy-done, ...), custom_call_target="tpu_custom_call" | custom-call | tf_op jit(solution)/shard_map/pallas_call | solution.py:130
  123.2 0.7 shard_map.39.inner_ref
  123.8 4.5 %all-to-all-done.3.prior_ref = bf16[32,8,128]{2,1,0:T(8,128)(2,1)S(1)} async-done(((bf16[32,8,128]{2,1,0:T(8,128)(2,1)}), bf16[32,8,128]{2,1,0:T(8,128)(2,1)S(1)}, u32[]{:S(2)}, u32[]{:S(2)}) %all-to-all-start.3) | async-done | bytes 65568 | tf_op jit(solution)/shard_map/all_to_all | solution.py:23
  128.4 0.4 shard_map.42
  128.7 4.8 %collective-permute-start.5 = (bf16[2,256,128]{2,1,0:T(8,128)(2,1)S(1)}, bf16[2,256,128]{2,1,0:T(8,128)(2,1)S(1)}, u32[]{:S(2)}, u32[]{:S(2)}) collective-permute-start(bf16[2,256,128]{2,1,0:T(8,128)(2,1)S(1)} %get-tuple-element.20), channel_id=1, source_target_pairs={{0,8},{8,0},{1,9},{9,1},{2,10},{10,2},{3,11},{11,3},{4,12},{12,4},... | collective-permute-start | bytes 393224 | tf_op jit(solution)/shard_map/ppermute | solution.py:260
  133.6 1.0 collective-permute-done.5
  134.6 1.0 copy.7
  (22 shorter events, 0.3 us)
Async XLA Ops:
  6.5 20.7 %copy-start.3 = (bf16[256,512]{1,0:T(8,128)(2,1)S(1)}, bf16[256,512]{1,0:T(8,128)(2,1)}, u32[]{:S(2)}) copy-start(bf16[256,512]{1,0:T(8,128)(2,1)} %param.3) | copy-start | bytes 786436
  6.5 86.1 %all-gather.2.cloned.1.call-start = ((), (), s32[]{:S(2)}) async-start(), calls=%async_computation.4 | async-start | bytes 4718592 | tf_op jit(solution)/shard_map/all_gather | solution.py:225
  28.8 5.9 %copy-start.1 = (bf16[3,4096,2,2]{1,3,2,0:T(2,128)(2,1)S(1)}, bf16[3,4096,2,2]{1,3,2,0:T(2,128)(2,1)}, u32[]{:S(2)}) copy-start(bf16[3,4096,2,2]{1,3,2,0:T(2,128)(2,1)} %param.5) | copy-start | bytes 294916
  28.8 5.9 %copy-start.2 = (bf16[3,4096,2,2]{1,3,2,0:T(2,128)(2,1)S(1)}, bf16[3,4096,2,2]{1,3,2,0:T(2,128)(2,1)}, u32[]{:S(2)}) copy-start(bf16[3,4096,2,2]{1,3,2,0:T(2,128)(2,1)} %param.4) | copy-start | bytes 294916
  28.8 54.3 %all-to-all-start = ((bf16[8,256,512]{2,1,0:T(8,128)(2,1)}), bf16[8,256,512]{2,1,0:T(8,128)(2,1)S(1)}, u32[]{:S(2)}, u32[]{:S(2)}) async-start(bf16[8,256,512]{2,1,0:T(8,128)(2,1)} %broadcast_in_dim.6), calls=%async_computation | async-start | bytes 4194304 | tf_op jit(solution)/shard_map/all_to_all | solution.py:23
  34.9 4.1 %collective-permute-start = (bf16[4,4096]{1,0:T(4,128)(2,1)S(1)}, bf16[4,4096]{1,0:T(4,128)(2,1)S(1)}, u32[]{:S(2)}, u32[]{:S(2)}) collective-permute-start(bf16[4,4096]{1,0:T(4,128)(2,1)S(1)} %select_n.35), channel_id=1, source_target_pairs={{0,8},{8,0},{1,9},{9,1},{2,10},{10,2},{3,11},{11,3},{4,12},{12,4},... | collective-permute-start | bytes 98312 | tf_op jit(solution)/shard_map/ppermute | solution.py:230
  64.0 11.4 %copy-start = (bf16[64,4096]{1,0:T(8,128)(2,1)}, bf16[64,4096]{1,0:T(8,128)(2,1)S(1)}, u32[]{:S(2)}) copy-start(bf16[64,4096]{1,0:T(8,128)(2,1)S(1)} %all_gather.6.refs_0_) | copy-start | bytes 1572868
  64.0 11.4 %collective-permute-start.1 = (bf16[64,4096]{1,0:T(8,128)(2,1)S(1)}, bf16[64,4096]{1,0:T(8,128)(2,1)}, u32[]{:S(2)}, u32[]{:S(2)}) collective-permute-start(bf16[64,4096]{1,0:T(8,128)(2,1)S(1)} %all_gather.6.refs_0_), channel_id=1, source_target_pairs={{0,384},{128,0},{256,128},{384,256},{1,385},{129,1},{257,129},{385... | collective-permute-start | bytes 1572872 | tf_op jit(solution)/shard_map/ppermute | solution.py:234
  66.9 12.5 %collective-permute-start.2 = (bf16[64,4096]{1,0:T(8,128)(2,1)S(1)}, bf16[64,4096]{1,0:T(8,128)(2,1)}, u32[]{:S(2)}, u32[]{:S(2)}) collective-permute-start(bf16[64,4096]{1,0:T(8,128)(2,1)S(1)} %all_gather.6.refs_0_), channel_id=1, source_target_pairs={{0,128},{128,256},{256,384},{384,0},{1,129},{129,257},{257,385},{3... | collective-permute-start | bytes 1572872 | tf_op jit(solution)/shard_map/ppermute | solution.py:234
  83.1 9.5 %collective-permute-start.3 = (bf16[8,256,512]{2,1,0:T(8,128)(2,1)S(1)}, bf16[8,256,512]{2,1,0:T(8,128)(2,1)}, u32[]{:S(2)}, u32[]{:S(2)}) collective-permute-start(bf16[8,256,512]{2,1,0:T(8,128)(2,1)S(1)} %all-to-all-done.own_ref), channel_id=1, source_target_pairs={{0,8},{8,0},{1,9},{9,1},{2,10},{10,2},{3,11},{11,3},{4,12},{12,4},... | collective-permute-start | bytes 6291464 | tf_op jit(solution)/shard_map/ppermute | solution.py:236
  88.8 17.3 %collective-permute-start.4 = (bf16[64,4096]{1,0:T(8,128)(2,1)}, bf16[64,4096]{1,0:T(8,128)(2,1)}, u32[]{:S(2)}, u32[]{:S(2)}) collective-permute-start(bf16[64,4096]{1,0:T(8,128)(2,1)} %collective-permute-done.1.refs_1_), channel_id=1, source_target_pairs={{0,384},{128,0},{256,128},{384,256},{1,385},{129,1},{257,129},{385... | collective-permute-start | bytes 1572872 | tf_op jit(solution)/shard_map/ppermute | solution.py:237
  98.2 16.8 %all-to-all-start.2 = ((bf16[32,8,128]{2,1,0:T(8,128)(2,1)}), bf16[32,8,128]{2,1,0:T(8,128)(2,1)S(1)}, u32[]{:S(2)}, u32[]{:S(2)}) async-start(bf16[32,8,128]{2,1,0:T(8,128)(2,1)} %get-tuple-element.18), calls=%async_computation.2 | async-start | bytes 131072 | tf_op jit(solution)/shard_map/all_to_all | solution.py:23
  115.6 12.7 %all-to-all-start.3 = ((bf16[32,8,128]{2,1,0:T(8,128)(2,1)}), bf16[32,8,128]{2,1,0:T(8,128)(2,1)S(1)}, u32[]{:S(2)}, u32[]{:S(2)}) async-start(bf16[32,8,128]{2,1,0:T(8,128)(2,1)} %shard_map.41), calls=%async_computation.3 | async-start | bytes 131072 | tf_op jit(solution)/shard_map/all_to_all | solution.py:23
  128.7 5.8 %collective-permute-start.5 = (bf16[2,256,128]{2,1,0:T(8,128)(2,1)S(1)}, bf16[2,256,128]{2,1,0:T(8,128)(2,1)S(1)}, u32[]{:S(2)}, u32[]{:S(2)}) collective-permute-start(bf16[2,256,128]{2,1,0:T(8,128)(2,1)S(1)} %get-tuple-element.20), channel_id=1, source_target_pairs={{0,8},{8,0},{1,9},{9,1},{2,10},{10,2},{3,11},{11,3},{4,12},{12,4},... | collective-permute-start | bytes 393224 | tf_op jit(solution)/shard_map/ppermute | solution.py:260
Sparse Core Ops, SparseCore 0:
  27.4 60.9 all-gather.1

commit v12 on v11

--- a/solution.py
+++ b/solution.py
@@ -143,23 +143,7 @@
     )(own, order, *far)
 
 
-def arrived_kernel(block_hbm, out_ref, sem):
-    copy = pltpu.make_async_copy(block_hbm.at[pl.ds(0, 8), pl.ds(0, HD)], out_ref, sem)
-    copy.start()
-    copy.wait()
-
-
-def arrived(block):
-    return pl.pallas_call(
-        arrived_kernel,
-        in_specs=[pl.BlockSpec(memory_space=pltpu.HBM)],
-        out_specs=pl.BlockSpec(memory_space=pltpu.VMEM),
-        out_shape=shape(8, HD),
-        scratch_shapes=[pltpu.SemaphoreType.DMA],
-    )(pltpu.with_memory_space_constraint(block, pltpu.HBM))
-
-
-def prefix_kernel(total_ref, arrived_ref, out_ref):
+def prefix_kernel(total_ref, out_ref):
     run = jnp.zeros(total_ref.shape[1:], F32)
     for chip in range(NX * NY):
         out_ref[chip] = run.astype(BF16)
@@ -249,9 +233,8 @@
         (shape(2, 2, 2, TOK, HD), shape(2, 2, HD, HD, dtype=F32), shape(NX * NY, 8, HD)),
     )
 
-    slices = call(
-        prefix_kernel, shape(NX * NY, 8, HD), exchange(total, ("x", "y")), arrived(q_far), unread=1
-    )
+    totals, query = lax.optimization_barrier((exchange(total, ("x", "y")), query))
+    slices = call(prefix_kernel, shape(NX * NY, 8, HD), totals)
     prior = exchange(slices, ("x", "y"))
 
     inner = call(inner_kernel, shape(2, 2, TOK, HD, dtype=F32), query, kv)

time: 143 us -> 143 us (level)
  transfers between devices with their start and end apart: 10 -> 10, of which waited for: 8 -> 8; matrix products, arithmetic and copies ran while one was open for 1% -> 1% of each run, Pallas kernels for 8% -> 7%
where the time goes in v12:
time: 143 us; the launch traced here: 142 us
  blocking collectives  44.3 us (31%)
  starting transfers between devices  39.4 us (28%)
  waiting for transfers between devices  30 us (21%)
  between operations  13.6 us (10%)
  Pallas kernels  10.8 us (8%)
  local copies, waits for them, and re-layouts  2.8 us (2%)
  other arithmetic  1.63 us (1%)
    all_gather x1, blocking collectives, on_device(): lax.all_gather(jnp.concatenate([q_mine, q_theirs]), 'y', axis=0, tiled=True)  24.9 us
    all_to_all x1, blocking collectives, exchange(): return lax.all_to_all(x, axes, 0, 0, tiled=True)  19.3 us
    all_to_all x3, starting transfers between devices, exchange(): return lax.all_to_all(x, axes, 0, 0, tiled=True)  17.7 us
    all_to_all x3, waiting for transfers between devices, exchange(): return lax.all_to_all(x, axes, 0, 0, tiled=True)  17.1 us
    pallas_call x2, Pallas kernels, project(): pl.pallas_call(kernel, in_specs=[vmem, vmem] + [pl.BlockSpec(memory_space...  9.07 us
    ppermute x1, waiting for transfers between devices, on_device(): lax.ppermute(q_part, 'x', down)  6.15 us
    ppermute x1, starting transfers between devices, on_device(): other = lax.ppermute(own, 'c', swap)  5.64 us
    ppermute x1, starting transfers between devices, on_device(): theirs = lax.ppermute(sent, 'c', swap)  4.72 us
  transfers between devices with their start and end apart: 10, of which 8 were waited for; matrix products, arithmetic and copies ran while one was open for 1% of the time, Pallas kernels for 7%

profile of v12, /device:TPU:1, one launch (start us, length us, event | category | flops | bytes accessed | tf_op | source)
XLA Modules:
  0.0 142.4 jit_solution(11665540207539533662)
XLA Ops:
  6.5 1.1 fusion.2
  7.6 0.1 copy.5
  7.8 0.1 copy.6
  7.9 19.3 %all_to_all.20 = bf16[8,8,4096]{2,1,0:T(8,128)(2,1)} all-to-all(bf16[8,8,4096]{2,1,0:T(8,128)(2,1)S(1)} %bitcast.19), channel_id=1, replica_groups=mesh['x'=4,'y'=8,'c'=2,'z'=8] {'x','c'}, dimensions={0} | all-to-all | bytes 1048576 | tf_op jit(solution)/shard_map/all_to_all | solution.py:23
  27.3 1.5 %broadcast_in_dim.6 = bf16[8,256,512]{2,1,0:T(8,128)(2,1)} broadcast(bf16[256,512]{1,0:T(8,128)(2,1)S(1)} %copy-done.3), dimensions={1,2} | broadcast | bytes 2359296 | tf_op jit(solution)/shard_map/broadcast_in_dim | solution.py:19
  28.8 5.9 %all-to-all-start = ((bf16[8,256,512]{2,1,0:T(8,128)(2,1)}), bf16[8,256,512]{2,1,0:T(8,128)(2,1)S(1)}, u32[]{:S(2)}, u32[]{:S(2)}) async-start(bf16[8,256,512]{2,1,0:T(8,128)(2,1)} %broadcast_in_dim.6), calls=%async_computation | async-start | bytes 4194304 | tf_op jit(solution)/shard_map/all_to_all | solution.py:23
  34.7 0.1 broadcast_select_fusion.1
  34.9 3.2 %collective-permute-start = (bf16[4,4096]{1,0:T(4,128)(2,1)S(1)}, bf16[4,4096]{1,0:T(4,128)(2,1)S(1)}, u32[]{:S(2)}, u32[]{:S(2)}) collective-permute-start(bf16[4,4096]{1,0:T(4,128)(2,1)S(1)} %select_n.35), channel_id=1, source_target_pairs={{0,8},{8,0},{1,9},{9,1},{2,10},{10,2},{3,11},{11,3},{4,12},{12,4},... | collective-permute-start | bytes 98312 | tf_op jit(solution)/shard_map/ppermute | solution.py:214
  38.2 0.8 collective-permute-done
  39.0 24.9 %all_gather.6.refs_0_ = bf16[64,4096]{1,0:T(8,128)(2,1)S(1)} all-gather(bf16[8,4096]{1,0:T(8,128)(2,1)S(1)} %pad_maximum_fusion.2), channel_id=1, replica_groups=mesh['x'=4,'y'=8,'c'=2,'z'=8] {'y'}, dimensions={0}, use_global_device_ids=true | all-gather | bytes 589824 | tf_op jit(solution)/shard_map/all_gather | solution.py:215
  64.0 2.9 %collective-permute-start.1 = (bf16[64,4096]{1,0:T(8,128)(2,1)S(1)}, bf16[64,4096]{1,0:T(8,128)(2,1)}, u32[]{:S(2)}, u32[]{:S(2)}) collective-permute-start(bf16[64,4096]{1,0:T(8,128)(2,1)S(1)} %all_gather.6.refs_0_), channel_id=1, source_target_pairs={{0,384},{128,0},{256,128},{384,256},{1,385},{129,1},{257,129},{385... | collective-permute-start | bytes 1572872 | tf_op jit(solution)/shard_map/ppermute | solution.py:218
  66.9 2.3 %collective-permute-start.2 = (bf16[64,4096]{1,0:T(8,128)(2,1)S(1)}, bf16[64,4096]{1,0:T(8,128)(2,1)}, u32[]{:S(2)}, u32[]{:S(2)}) collective-permute-start(bf16[64,4096]{1,0:T(8,128)(2,1)S(1)} %all_gather.6.refs_0_), channel_id=1, source_target_pairs={{0,128},{128,256},{256,384},{384,0},{1,129},{129,257},{257,385},{3... | collective-permute-start | bytes 1572872 | tf_op jit(solution)/shard_map/ppermute | solution.py:218
  69.3 6.1 %collective-permute-done.1.refs_1_ = bf16[64,4096]{1,0:T(8,128)(2,1)} collective-permute-done((bf16[64,4096]{1,0:T(8,128)(2,1)S(1)}, bf16[64,4096]{1,0:T(8,128)(2,1)}, u32[]{:S(2)}, u32[]{:S(2)}) %collective-permute-start.1) | collective-permute-done | bytes 524320 | tf_op jit(solution)/shard_map/ppermute | solution.py:218
  75.4 4.1 %collective-permute-done.2.refs_3_ = bf16[64,4096]{1,0:T(8,128)(2,1)} collective-permute-done((bf16[64,4096]{1,0:T(8,128)(2,1)S(1)}, bf16[64,4096]{1,0:T(8,128)(2,1)}, u32[]{:S(2)}, u32[]{:S(2)}) %collective-permute-start.2) | collective-permute-done | bytes 524320 | tf_op jit(solution)/shard_map/ppermute | solution.py:218
  79.5 3.6 %all-to-all-done.own_ref = bf16[8,256,512]{2,1,0:T(8,128)(2,1)S(1)} async-done(((bf16[8,256,512]{2,1,0:T(8,128)(2,1)}), bf16[8,256,512]{2,1,0:T(8,128)(2,1)S(1)}, u32[]{:S(2)}, u32[]{:S(2)}) %all-to-all-start) | async-done | bytes 2097184 | tf_op jit(solution)/shard_map/all_to_all | solution.py:23
  83.1 5.6 %collective-permute-start.3 = (bf16[8,256,512]{2,1,0:T(8,128)(2,1)S(1)}, bf16[8,256,512]{2,1,0:T(8,128)(2,1)}, u32[]{:S(2)}, u32[]{:S(2)}) collective-permute-start(bf16[8,256,512]{2,1,0:T(8,128)(2,1)S(1)} %all-to-all-done.own_ref), channel_id=1, source_target_pairs={{0,8},{8,0},{1,9},{9,1},{2,10},{10,2},{3,11},{11,3},{4,12},{12,4},... | collective-permute-start | bytes 6291464 | tf_op jit(solution)/shard_map/ppermute | solution.py:220
  88.8 2.8 %collective-permute-start.4 = (bf16[64,4096]{1,0:T(8,128)(2,1)}, bf16[64,4096]{1,0:T(8,128)(2,1)}, u32[]{:S(2)}, u32[]{:S(2)}) collective-permute-start(bf16[64,4096]{1,0:T(8,128)(2,1)} %collective-permute-done.1.refs_1_), channel_id=1, source_target_pairs={{0,384},{128,0},{256,128},{384,256},{1,385},{129,1},{257,129},{385... | collective-permute-start | bytes 1572872 | tf_op jit(solution)/shard_map/ppermute | solution.py:221
  91.6 0.2 fusion.order_ref
  91.8 0.9 collective-permute-done.3.other_hbm
  92.7 5.5 %shard_map.37 = (bf16[2,2,2,256,128]{4,3,2,1,0:T(8,128)(2,1)S(1)}, f32[2,2,128,128]{3,2,1,0:T(8,128)S(1)}, bf16[32,8,128]{2,1,0:T(8,128)(2,1)}) custom-call(bf16[8,256,512]{2,1,0:T(8,128)(2,1)S(1)} %all-to-all-done.own_ref, bf16[512,512]{1,0:T(8,128)(2,1)S(1)} %fusion.order_ref, bf16[8,256,512]{2,1,0:T(8,128)(2,1)} %collective-permute-done.3.other_hbm, ...), custom_call_target="tpu_custom_call" | custom-call | tf_op jit(solution)/shard_map/pallas_call | solution.py:130
  98.2 7.8 %all-to-all-start.2 = ((bf16[32,8,128]{2,1,0:T(8,128)(2,1)}), bf16[32,8,128]{2,1,0:T(8,128)(2,1)S(1)}, u32[]{:S(2)}, u32[]{:S(2)}) async-start(bf16[32,8,128]{2,1,0:T(8,128)(2,1)} %get-tuple-element.16), calls=%async_computation.2 | async-start | bytes 131072 | tf_op jit(solution)/shard_map/all_to_all | solution.py:23
  106.0 0.1 fusion.1.order_ref
  106.1 3.6 %shard_map.38.query_ref = bf16[2,2,256,128]{3,2,1,0:T(8,128)(2,1)S(1)} custom-call(bf16[8,256,512]{2,1,0:T(8,128)(2,1)S(1)} %all-to-all-done.own_ref, bf16[256,256]{1,0:T(8,128)(2,1)S(1)} %fusion.1.order_ref, bf16[8,256,512]{2,1,0:T(8,128)(2,1)} %collective-permute-done.3.other_hbm, bf16[64,4096]{1,0:T(8,128)(2,1)} %copy-done, ...), custom_call_target="tpu_custom_call" | custom-call | tf_op jit(solution)/shard_map/pallas_call | solution.py:130
  109.7 5.3 %all-to-all-done.2.total_ref = bf16[32,8,128]{2,1,0:T(8,128)(2,1)S(1)} async-done(((bf16[32,8,128]{2,1,0:T(8,128)(2,1)}), bf16[32,8,128]{2,1,0:T(8,128)(2,1)S(1)}, u32[]{:S(2)}, u32[]{:S(2)}) %all-to-all-start.2) | async-done | bytes 65568 | tf_op jit(solution)/shard_map/all_to_all | solution.py:23
  115.0 0.7 shard_map.40
  115.6 4.0 %all-to-all-start.3 = ((bf16[32,8,128]{2,1,0:T(8,128)(2,1)}), bf16[32,8,128]{2,1,0:T(8,128)(2,1)S(1)}, u32[]{:S(2)}, u32[]{:S(2)}) async-start(bf16[32,8,128]{2,1,0:T(8,128)(2,1)} %shard_map.40), calls=%async_computation.3 | async-start | bytes 131072 | tf_op jit(solution)/shard_map/all_to_all | solution.py:23
  119.6 0.7 shard_map.39.inner_ref
  120.3 8.2 %all-to-all-done.3.prior_ref = bf16[32,8,128]{2,1,0:T(8,128)(2,1)S(1)} async-done(((bf16[32,8,128]{2,1,0:T(8,128)(2,1)}), bf16[32,8,128]{2,1,0:T(8,128)(2,1)S(1)}, u32[]{:S(2)}, u32[]{:S(2)}) %all-to-all-start.3) | async-done | bytes 65568 | tf_op jit(solution)/shard_map/all_to_all | solution.py:23
  128.5 0.4 shard_map.41
  128.8 4.7 %collective-permute-start.5 = (bf16[2,256,128]{2,1,0:T(8,128)(2,1)S(1)}, bf16[2,256,128]{2,1,0:T(8,128)(2,1)S(1)}, u32[]{:S(2)}, u32[]{:S(2)}) collective-permute-start(bf16[2,256,128]{2,1,0:T(8,128)(2,1)S(1)} %get-tuple-element.24), channel_id=1, source_target_pairs={{0,8},{8,0},{1,9},{9,1},{2,10},{10,2},{3,11},{11,3},{4,12},{12,4},... | collective-permute-start | bytes 393224 | tf_op jit(solution)/shard_map/ppermute | solution.py:243
  133.6 1.0 collective-permute-done.5
  134.6 1.0 copy.7
  (21 shorter events, 0.3 us)
Async XLA Ops:
  6.5 20.7 %copy-start.3 = (bf16[256,512]{1,0:T(8,128)(2,1)S(1)}, bf16[256,512]{1,0:T(8,128)(2,1)}, u32[]{:S(2)}) copy-start(bf16[256,512]{1,0:T(8,128)(2,1)} %param.3) | copy-start | bytes 786436
  6.5 86.1 %all-gather.2.cloned.1.call-start = ((), (), s32[]{:S(2)}) async-start(), calls=%async_computation.4 | async-start | bytes 4718592 | tf_op jit(solution)/shard_map/all_gather | solution.py:209
  28.8 5.9 %copy-start.1 = (bf16[3,4096,2,2]{1,3,2,0:T(2,128)(2,1)S(1)}, bf16[3,4096,2,2]{1,3,2,0:T(2,128)(2,1)}, u32[]{:S(2)}) copy-start(bf16[3,4096,2,2]{1,3,2,0:T(2,128)(2,1)} %param.5) | copy-start | bytes 294916
  28.8 5.9 %copy-start.2 = (bf16[3,4096,2,2]{1,3,2,0:T(2,128)(2,1)S(1)}, bf16[3,4096,2,2]{1,3,2,0:T(2,128)(2,1)}, u32[]{:S(2)}) copy-start(bf16[3,4096,2,2]{1,3,2,0:T(2,128)(2,1)} %param.4) | copy-start | bytes 294916
  28.8 54.3 %all-to-all-start = ((bf16[8,256,512]{2,1,0:T(8,128)(2,1)}), bf16[8,256,512]{2,1,0:T(8,128)(2,1)S(1)}, u32[]{:S(2)}, u32[]{:S(2)}) async-start(bf16[8,256,512]{2,1,0:T(8,128)(2,1)} %broadcast_in_dim.6), calls=%async_computation | async-start | bytes 4194304 | tf_op jit(solution)/shard_map/all_to_all | solution.py:23
  34.9 4.1 %collective-permute-start = (bf16[4,4096]{1,0:T(4,128)(2,1)S(1)}, bf16[4,4096]{1,0:T(4,128)(2,1)S(1)}, u32[]{:S(2)}, u32[]{:S(2)}) collective-permute-start(bf16[4,4096]{1,0:T(4,128)(2,1)S(1)} %select_n.35), channel_id=1, source_target_pairs={{0,8},{8,0},{1,9},{9,1},{2,10},{10,2},{3,11},{11,3},{4,12},{12,4},... | collective-permute-start | bytes 98312 | tf_op jit(solution)/shard_map/ppermute | solution.py:214
  64.0 11.4 %copy-start = (bf16[64,4096]{1,0:T(8,128)(2,1)}, bf16[64,4096]{1,0:T(8,128)(2,1)S(1)}, u32[]{:S(2)}) copy-start(bf16[64,4096]{1,0:T(8,128)(2,1)S(1)} %all_gather.6.refs_0_) | copy-start | bytes 1572868
  64.0 11.4 %collective-permute-start.1 = (bf16[64,4096]{1,0:T(8,128)(2,1)S(1)}, bf16[64,4096]{1,0:T(8,128)(2,1)}, u32[]{:S(2)}, u32[]{:S(2)}) collective-permute-start(bf16[64,4096]{1,0:T(8,128)(2,1)S(1)} %all_gather.6.refs_0_), channel_id=1, source_target_pairs={{0,384},{128,0},{256,128},{384,256},{1,385},{129,1},{257,129},{385... | collective-permute-start | bytes 1572872 | tf_op jit(solution)/shard_map/ppermute | solution.py:218
  66.9 12.6 %collective-permute-start.2 = (bf16[64,4096]{1,0:T(8,128)(2,1)S(1)}, bf16[64,4096]{1,0:T(8,128)(2,1)}, u32[]{:S(2)}, u32[]{:S(2)}) collective-permute-start(bf16[64,4096]{1,0:T(8,128)(2,1)S(1)} %all_gather.6.refs_0_), channel_id=1, source_target_pairs={{0,128},{128,256},{256,384},{384,0},{1,129},{129,257},{257,385},{3... | collective-permute-start | bytes 1572872 | tf_op jit(solution)/shard_map/ppermute | solution.py:218
  83.1 9.5 %collective-permute-start.3 = (bf16[8,256,512]{2,1,0:T(8,128)(2,1)S(1)}, bf16[8,256,512]{2,1,0:T(8,128)(2,1)}, u32[]{:S(2)}, u32[]{:S(2)}) collective-permute-start(bf16[8,256,512]{2,1,0:T(8,128)(2,1)S(1)} %all-to-all-done.own_ref), channel_id=1, source_target_pairs={{0,8},{8,0},{1,9},{9,1},{2,10},{10,2},{3,11},{11,3},{4,12},{12,4},... | collective-permute-start | bytes 6291464 | tf_op jit(solution)/shard_map/ppermute | solution.py:220
  88.8 17.3 %collective-permute-start.4 = (bf16[64,4096]{1,0:T(8,128)(2,1)}, bf16[64,4096]{1,0:T(8,128)(2,1)}, u32[]{:S(2)}, u32[]{:S(2)}) collective-permute-start(bf16[64,4096]{1,0:T(8,128)(2,1)} %collective-permute-done.1.refs_1_), channel_id=1, source_target_pairs={{0,384},{128,0},{256,128},{384,256},{1,385},{129,1},{257,129},{385... | collective-permute-start | bytes 1572872 | tf_op jit(solution)/shard_map/ppermute | solution.py:221
  98.2 16.8 %all-to-all-start.2 = ((bf16[32,8,128]{2,1,0:T(8,128)(2,1)}), bf16[32,8,128]{2,1,0:T(8,128)(2,1)S(1)}, u32[]{:S(2)}, u32[]{:S(2)}) async-start(bf16[32,8,128]{2,1,0:T(8,128)(2,1)} %get-tuple-element.16), calls=%async_computation.2 | async-start | bytes 131072 | tf_op jit(solution)/shard_map/all_to_all | solution.py:23
  115.6 12.8 %all-to-all-start.3 = ((bf16[32,8,128]{2,1,0:T(8,128)(2,1)}), bf16[32,8,128]{2,1,0:T(8,128)(2,1)S(1)}, u32[]{:S(2)}, u32[]{:S(2)}) async-start(bf16[32,8,128]{2,1,0:T(8,128)(2,1)} %shard_map.40), calls=%async_computation.3 | async-start | bytes 131072 | tf_op jit(solution)/shard_map/all_to_all | solution.py:23
  128.8 5.7 %collective-permute-start.5 = (bf16[2,256,128]{2,1,0:T(8,128)(2,1)S(1)}, bf16[2,256,128]{2,1,0:T(8,128)(2,1)S(1)}, u32[]{:S(2)}, u32[]{:S(2)}) collective-permute-start(bf16[2,256,128]{2,1,0:T(8,128)(2,1)S(1)} %get-tuple-element.24), channel_id=1, source_target_pairs={{0,8},{8,0},{1,9},{9,1},{2,10},{10,2},{3,11},{11,3},{4,12},{12,4},... | collective-permute-start | bytes 393224 | tf_op jit(solution)/shard_map/ppermute | solution.py:243
Sparse Core Ops, SparseCore 0:
  27.4 60.9 all-gather.1
